TPU v7x, 128 devices: a whole 4x4x4 slice. The times are simulated.
128 devices in a mesh: gx: 8 (over x, core), gy: 16 (over y, z).
Axes of the slice: x: 4, y: 4, z: 4, core: 2. Of those that a mesh axis runs over, the one named last changes fastest.
Arguments:
- state: float32 [1024, 2, 128, 128], P(('gx', 'gy')), may hold values from -6 to 6
- hamiltonian: float32 [2, 128, 128], replicated, may hold values from -0.5 to 0.5
- couplings: float32 [16, 128, 128], replicated, may hold values from -0.125 to 0.125
- bath_coef: float32 [2, 16], replicated, may hold values from 0.2 to 1
- bath_rate: float32 [16], replicated, may hold values from 0.02 to 0.2
- occupation: int32 [1024, 16], P(('gx', 'gy')), may hold values from 0 to 5
- send_list: int32 [128, 128, 1], P(('gx', 'gy')), may hold values from -1 to 7
- up_index: int32 [1024, 16], P(('gx', 'gy')), may hold values from -1 to 135
- down_index: int32 [1024, 16], P(('gx', 'gy')), may hold values from -1 to 135
- step: float32 [1], replicated, may hold values from 0.5 to 1.5
Outputs:
- derivative: float32 [1024, 2, 128, 128], P(('gx', 'gy'))
- advanced: float32 [1024, 2, 128, 128], P(('gx', 'gy'))
All inputs are finite; a program needn't handle non-finite values.
Results may differ from a plain program's by a relative error of at most 0.0003.
Values sent between devices are 32-bit elements; how exact they have to be, the bound alone decides.
No kernel may reach another device: no remote copies, remote signals or barrier semaphores. Data moves between devices by JAX's collectives and lax.ppermute only.
A program may use at most 256 MiB of HBM per device.

v0:
```python
import jax
import jax.numpy as jnp
from jax import lax
from jax.sharding import Mesh
from jax.sharding import PartitionSpec as P

GX_GY = ("gx_0", "gx_1", "gy_0", "gy_1")


def cut_along(value, dim, count):
    dims = value.shape
    pieces = value.reshape(*dims[:dim], count, dims[dim] // count, *dims[dim + 1 :])
    return jnp.moveaxis(pieces, dim, 0)


def piece_ends(length, count):
    turn = length // count
    if turn >= 8:
        turn -= turn % 8
    return [turn * k for k in range(1, count)]


def joined_along(pieces, dim):
    pieces = jnp.moveaxis(pieces, 0, dim)
    dims = pieces.shape
    return pieces.reshape(*dims[:dim], dims[dim] * dims[dim + 1], *dims[dim + 2 :])


def several_exchanges(value, axis, pieces, split_dim, concat_dim):
    blocks = cut_along(value, split_dim, lax.axis_size(axis))
    widest = max(range(1, max(2, blocks.ndim - 1)), key=lambda d: blocks.shape[d])
    finished = []
    for slab in jnp.split(blocks, piece_ends(blocks.shape[widest], pieces), axis=widest):
        if slab.size:
            finished.append(lax.all_to_all(slab, axis, split_axis=0, concat_axis=0, tiled=True))
    return joined_along(jnp.concatenate(finished, axis=widest), concat_dim)


def over_axes(value, axes):
    for axis in axes:
        value = lax.psum(value, axis)
    return value


def left_product(matrix, rows):
    return jnp.einsum("ij,mcjl->mcil", matrix, rows, precision=lax.Precision.HIGHEST)


def right_product(rows, matrix):
    return jnp.einsum("mcij,jl->mcil", rows, matrix, precision=lax.Precision.HIGHEST)


def derive(
    local, buffer, occupation, up_index, down_index, hamiltonian, couplings, bath_coef, bath_rate
):
    counts = occupation.astype(local.dtype)
    modes = couplings.shape[0]
    rows = local.shape[0]
    joined = jnp.concatenate([up_index, down_index], axis=1).T.reshape(-1)
    picked = jnp.take(buffer, jnp.clip(joined, 0, buffer.shape[0] - 1), axis=0)
    picked = picked * (joined >= 0).astype(buffer.dtype)[:, None, None, None]
    picked = picked.reshape((2 * modes, rows) + local.shape[1:])
    stacked = jnp.concatenate([couplings, couplings], axis=0)
    lefts = jnp.einsum("kij,kmcjl->kmcil", stacked, picked, precision=lax.Precision.HIGHEST)
    rights = jnp.einsum("kmcij,kjl->kmcil", picked, stacked, precision=lax.Precision.HIGHEST)
    comm = jnp.sum(lefts[:modes] - rights[:modes], axis=0)
    left_low, right_low = (lefts[modes:], rights[modes:])
    coef_real = bath_coef[0][:, None, None, None]
    coef_imag = bath_coef[1][:, None, None, None]
    part_x = coef_real * (left_low[:, :, 0] - right_low[:, :, 0]) - coef_imag * (
        left_low[:, :, 1] + right_low[:, :, 1]
    )
    part_y = coef_real * (left_low[:, :, 1] - right_low[:, :, 1]) + coef_imag * (
        left_low[:, :, 0] + right_low[:, :, 0]
    )
    weight = counts.T[:, :, None, None]
    sum_x = jnp.sum(weight * part_x, axis=0)
    sum_y = jnp.sum(weight * part_y, axis=0)
    total = jnp.stack([comm[:, 1] + sum_y, -comm[:, 0] - sum_x], axis=1)
    ham_real, ham_imag = (hamiltonian[0], hamiltonian[1])
    real_part, imag_part = (local[:, 0:1], local[:, 1:2])
    left_real = left_product(ham_real, real_part) - left_product(ham_imag, imag_part)
    left_imag = left_product(ham_real, imag_part) + left_product(ham_imag, real_part)
    right_real = right_product(real_part, ham_real) - right_product(imag_part, ham_imag)
    right_imag = right_product(real_part, ham_imag) + right_product(imag_part, ham_real)
    comm_real = left_real - right_real
    comm_imag = left_imag - right_imag
    total = total + jnp.concatenate([comm_imag, -comm_real], axis=1)
    damping = jnp.sum(counts * bath_rate[None, :], axis=1)
    return total - damping[:, None, None, None] * local


def body(
    state,
    hamiltonian,
    couplings,
    bath_coef,
    bath_rate,
    occupation,
    send_list,
    up_index,
    down_index,
    step,
):
    peers = send_list.shape[1]
    chosen = send_list[0]
    outgoing = jnp.take(state, jnp.clip(chosen, 0, state.shape[0] - 1), axis=0)
    outgoing = outgoing * (chosen >= 0).astype(state.dtype)[:, :, None, None, None]
    arrived = several_exchanges(outgoing, GX_GY, 2, 0, 0)
    buffer = jnp.concatenate([state, arrived.reshape((-1,) + state.shape[1:])], axis=0)
    derivative = derive(
        state,
        buffer,
        occupation,
        up_index,
        down_index,
        hamiltonian,
        couplings,
        bath_coef,
        bath_rate,
    )
    square_sum = over_axes(jnp.sum(derivative * derivative), GX_GY)
    count = state.shape[0] * peers * 2 * state.shape[2] * state.shape[3]
    rms = jnp.sqrt(square_sum / count + 1e-06)
    advanced = state + step[0] / rms * derivative
    return (derivative, advanced)


def solution(mesh):
    torus = Mesh(mesh.devices.reshape(4, 2, 4, 4), ("gx_0", "gx_1", "gy_0", "gy_1"))
    in_specs = (
        P(GX_GY, None, None, None),
        P(),
        P(),
        P(),
        P(),
        P(GX_GY, None),
        P(GX_GY, None, None),
        P(GX_GY, None),
        P(GX_GY, None),
        P(),
    )
    out_specs = (P(GX_GY, None, None, None), P(GX_GY, None, None, None))
    return jax.shard_map(body, mesh=torus, in_specs=in_specs, out_specs=out_specs, check_vma=False)
```

profile of v0, /device:TPU:1, one launch (start us, length us, event | category | flops | bytes accessed | tf_op | source)
XLA Modules:
  0.0 504.2 jit_solution(4382770320333523669)
XLA Ops:
  2.6 11.0 %gather_fusion = f32[128,2,128,128]{3,2,1,0:T(8,128)} fusion(f32[8,2,128,128]{3,2,1,0:T(8,128)} %param.10, s32[1024]{0:T(1024)S(1)} %pad_clamp_fusion.1), kind=kCustom, calls=%fused_computation | custom fusion | bytes 33554944 | tf_op jit(solution)/shard_map/jit(_take)/gather | solution.py:107
  13.6 7.5 %fusion.3 = f32[128,1,1,2,128,128]{5,4,3,2,1,0:T(8,128)S(1)} fusion(f32[128,2,128,128]{3,2,1,0:T(8,128)} %gather_fusion, f32[128]{0:T(128)S(1)} %fusion.48, pred[128]{0:T(512)(128)(4,1)S(1)} %compare_and_fusion.1), kind=kLoop, calls=%fused_computation.10 | loop fusion | flops 8388608 | bytes 33555072 | tf_op jit(solution)/shard_map/mul | solution.py:108
  21.1 6.7 %fusion.56 = (f32[128,1,1,2,64,128]{5,4,3,2,1,0:T(8,128)}, f32[128,1,1,2,64,128]{5,4,3,2,1,0:T(8,128)}) fusion(f32[128,1,1,2,128,128]{5,4,3,2,1,0:T(8,128)S(1)} %fusion.3), kind=kLoop, calls=%fused_computation.97 | loop fusion | bytes 33554432 | tf_op jit(solution)/shard_map/split | solution.py:33
  27.8 109.9 %all_to_all.10 = f32[128,1,1,2,64,128]{5,4,3,2,1,0:T(8,128)} all-to-all(f32[128,1,1,2,64,128]{5,4,3,2,1,0:T(8,128)} %get-tuple-element.16), channel_id=1, replica_groups=mesh['gx_0'=4,'gx_1'=2,'gy_0'=4,'gy_1'=4] {'gx_0','gx_1','gy_0','gy_1'}, dimensions={0} | all-to-all | bytes 16777216 | tf_op jit(solution)/shard_map/all_to_all | solution.py:35
  137.7 7.2 %all-to-all-start.1 = ((f32[128,1,1,2,64,128]{5,4,3,2,1,0:T(8,128)}), f32[128,1,1,2,64,128]{5,4,3,2,1,0:T(8,128)}, u32[]{:S(2)}, u32[]{:S(2)}) async-start(f32[128,1,1,2,64,128]{5,4,3,2,1,0:T(8,128)} %get-tuple-element.17), calls=%async_computation.1 | async-start | bytes 16777216 | tf_op jit(solution)/shard_map/all_to_all | solution.py:35
  149.7 1.4 fusion.23
  151.1 1.4 fusion.21
  152.5 97.6 %all-to-all-done.1 = f32[128,1,1,2,64,128]{5,4,3,2,1,0:T(8,128)} async-done(((f32[128,1,1,2,64,128]{5,4,3,2,1,0:T(8,128)}), f32[128,1,1,2,64,128]{5,4,3,2,1,0:T(8,128)}, u32[]{:S(2)}, u32[]{:S(2)}) %all-to-all-start.1) | async-done | bytes 8388640 | tf_op jit(solution)/shard_map/all_to_all | solution.py:35
  250.1 6.9 %maximum_bitcast_fusion = f32[128,2,128,128]{3,2,1,0:T(8,128)S(1)} fusion(f32[128,1,1,2,64,128]{5,4,3,2,1,0:T(8,128)} %all-to-all-done.1, f32[128,1,1,2,64,128]{5,4,3,2,1,0:T(8,128)} %all_to_all.10), kind=kLoop, calls=%fused_computation.8 | loop fusion | flops 4194304 | bytes 33554432 | tf_op jit(solution)/shard_map/reshape;reshape | solution.py:110
  257.0 6.6 %pad_maximum_fusion = f32[136,2,128,128]{3,2,1,0:T(8,128)} fusion(f32[128,2,128,128]{3,2,1,0:T(8,128)S(1)} %maximum_bitcast_fusion, f32[8,2,128,128]{3,2,1,0:T(8,128)S(1)} %copy-done), kind=kLoop, calls=%fused_computation.5 | loop fusion | flops 4456448 | bytes 35651584 | tf_op jit(solution)/shard_map/concatenate | solution.py:110
  263.6 20.9 %gather_fusion.1 = f32[256,2,128,128]{3,2,1,0:T(8,128)} fusion(f32[136,2,128,128]{3,2,1,0:T(8,128)} %pad_maximum_fusion, s32[1024]{0:T(1024)S(1)} %pad_clamp_fusion), kind=kCustom, calls=%fused_computation.1 | custom fusion | bytes 67109888 | tf_op jit(solution)/shard_map/jit(_take)/gather | solution.py:60
  284.5 37.3 %fusion = f32[32,8,2,128,128]{4,3,2,1,0:T(8,128)} fusion(f32[32,8,2,128,128]{4,3,2,1,0:T(8,128)} %bitcast.147, f32[32,8]{1,0:T(8,128)S(1)} %copy.63, pred[32,8]{1,0:T(8,128)(4,1)S(1)} %copy.61, f32[16,128,128]{2,1,0:T(8,128)} %param.12), kind=kOutput, calls=%fused_computation.3 | convolution fusion | flops 12902203392 | bytes 68158720 | tf_op jit(solution)/shard_map/kmcij,kjl->kmcil/dot_general | solution.py:65
  321.9 57.4 %fusion.10 = f32[32,8,2,128,128]{3,4,2,1,0:T(8,128)} fusion(f32[32,8,2,128,128]{4,3,2,1,0:T(8,128)S(1)} %bitcast.148, f32[32,8]{1,0:T(8,128)S(1)} %copy.63, pred[32,8]{1,0:T(8,128)(4,1)S(1)} %copy.61, f32[16,128,128]{2,1,0:T(8,128)} %param.12), kind=kOutput, calls=%fused_computation.17 | convolution fusion | flops 12902203392 | bytes 68158720 | tf_op jit(solution)/shard_map/kij,kmcjl->kmcil/dot_general | solution.py:64
  379.2 11.7 %slice.71 = f32[16,8,2,128,128]{4,3,2,1,0:T(8,128)} slice(f32[32,8,2,128,128]{4,3,2,1,0:T(8,128)} %fusion), slice={[0:16], [0:8], [0:2], [0:128], [0:128]} | slice | bytes 33554432 | tf_op jit(solution)/shard_map/slice | solution.py:66
  390.9 10.8 %fusion.55 = (f32[16,8,1,128,128]{4,3,2,1,0:T(8,128)}, f32[16,8,1,128,128]{4,3,2,1,0:T(8,128)}) fusion(f32[32,8,2,128,128]{4,3,2,1,0:T(8,128)} %fusion), kind=kLoop, calls=%fused_computation.96 | loop fusion | bytes 33554432 | tf_op jit(solution)/shard_map/slice | solution.py:73
  401.8 9.2 %copy.101 = f32[16,8,1,128,128]{3,4,1,0,2:T(8,128)} copy(f32[16,8,1,128,128]{4,3,2,1,0:T(8,128)} %get-tuple-element.14) | data formatting | bytes 16777216
  411.0 17.6 %copy.98 = f32[16,8,2,128,128]{3,4,2,1,0:T(8,128)} copy(f32[16,8,2,128,128]{4,3,2,1,0:T(8,128)} %slice.71) | data formatting | bytes 33554432
  428.6 9.2 %copy.102 = f32[16,8,1,128,128]{3,4,1,0,2:T(8,128)} copy(f32[16,8,1,128,128]{4,3,2,1,0:T(8,128)} %get-tuple-element.15) | data formatting | bytes 16777216
  437.8 11.7 %fusion.2 = f32[8,2,128,128]{2,3,1,0:T(8,128)S(1)} fusion(f32[16,8,2,128,128]{3,4,2,1,0:T(8,128)} %copy.98, f32[32,8,2,128,128]{3,4,2,1,0:T(8,128)} %fusion.10), kind=kLoop, calls=%fused_computation.7 | loop fusion | flops 8126464 | bytes 34603008 | tf_op jit(solution)/shard_map/reduce_sum | solution.py:66
  450.8 11.0 %fusion.16 = (f32[8,128,128]{1,2,0:T(8,128)S(1)}, f32[8,128,128]{1,2,0:T(8,128)S(1)}) fusion(f32[16,8,1,128,128]{3,4,1,0,2:T(8,128)S(1)} %copy-done.4, f32[16,8,1,128,128]{3,4,1,0,2:T(8,128)} %copy.101, f32[32,8,2,128,128]{3,4,2,1,0:T(8,128)} %fusion.10, f32[16]{0:T(128)S(1)} %get-tuple-element.21, f32[16]{0:T(128)S(1)} %get-tuple-element.20, ...), kind=kLoop, calls=%fused_computation.28 | loop fusion | flops 29097984 | bytes 34603648 | tf_op jit(solution)/shard_map/reduce_sum | solution.py:78
  463.1 8.6 %psum.28 = f32[]{:T(128)} all-reduce(f32[]{:T(128)} %get-tuple-element.10), channel_id=1, replica_groups=mesh['gx_0'=4,'gx_1'=2,'gy_0'=4,'gy_1'=4] {'gx_0'}, use_global_device_ids=true, to_apply=%region_5.6 | all-reduce | flops 1 | bytes 8 | tf_op jit(solution)/shard_map/psum | solution.py:41
  471.6 6.3 %psum.29 = f32[]{:T(128)} all-reduce(f32[]{:T(128)} %psum.28), channel_id=1, replica_groups=mesh['gx_0'=4,'gx_1'=2,'gy_0'=4,'gy_1'=4] {'gx_1'}, use_global_device_ids=true, to_apply=%region_6.7 | all-reduce | flops 1 | bytes 8 | tf_op jit(solution)/shard_map/psum | solution.py:41
  477.9 11.5 %psum.30 = f32[]{:T(128)} all-reduce(f32[]{:T(128)} %psum.29), channel_id=1, replica_groups=mesh['gx_0'=4,'gx_1'=2,'gy_0'=4,'gy_1'=4] {'gy_0'}, use_global_device_ids=true, to_apply=%region_7.8 | all-reduce | flops 1 | bytes 8 | tf_op jit(solution)/shard_map/psum | solution.py:41
  490.1 10.6 %psum.31 = f32[]{:T(128)} all-reduce(f32[]{:T(128)} %psum.30), channel_id=1, replica_groups=mesh['gx_0'=4,'gx_1'=2,'gy_0'=4,'gy_1'=4] {'gy_1'}, use_global_device_ids=true, to_apply=%region_8.9 | all-reduce | flops 1 | bytes 8 | tf_op jit(solution)/shard_map/psum | solution.py:41
  (54 shorter events, 12.0 us)
Async XLA Ops:
  27.8 117.1 %copy-start = (f32[8,2,128,128]{3,2,1,0:T(8,128)S(1)}, f32[8,2,128,128]{3,2,1,0:T(8,128)}, u32[]{:S(2)}) copy-start(f32[8,2,128,128]{3,2,1,0:T(8,128)} %param.10) | copy-start | bytes 3145732
  27.8 117.5 %copy-start.10 = (s32[8,16]{1,0:T(8,128)S(1)}, s32[8,16]{1,0:T(8,128)}, u32[]{:S(2)}) copy-start(s32[8,16]{1,0:T(8,128)} %param.15) | copy-start | bytes 1540
  27.8 117.6 %copy-start.8 = (s32[8,16]{1,0:T(8,128)S(1)}, s32[8,16]{1,0:T(8,128)}, u32[]{:S(2)}) copy-start(s32[8,16]{1,0:T(8,128)} %param.18) | copy-start | bytes 1540
  27.8 117.6 %copy-start.9 = (s32[8,16]{1,0:T(8,128)S(1)}, s32[8,16]{1,0:T(8,128)}, u32[]{:S(2)}) copy-start(s32[8,16]{1,0:T(8,128)} %param.17) | copy-start | bytes 1540
  27.8 118.1 %copy-start.12 = (f32[16]{0:T(128)S(1)}, f32[16]{0:T(128)}, u32[]{:S(2)}) copy-start(f32[16]{0:T(128)} %param.14) | copy-start | bytes 196
  27.8 118.2 %copy-start.5 = (f32[2,128,128]{2,1,0:T(8,128)S(1)}, f32[2,128,128]{2,1,0:T(8,128)}, u32[]{:S(2)}) copy-start(f32[2,128,128]{2,1,0:T(8,128)} %param.11) | copy-start | bytes 393220
  27.8 120.7 %copy-start.11 = (f32[2,16]{1,0:T(2,128)S(1)}, f32[2,16]{1,0:T(2,128)}, u32[]{:S(2)}) copy-start(f32[2,16]{1,0:T(2,128)} %param.13) | copy-start | bytes 388
  137.7 112.4 %all-to-all-start.1 = ((f32[128,1,1,2,64,128]{5,4,3,2,1,0:T(8,128)}), f32[128,1,1,2,64,128]{5,4,3,2,1,0:T(8,128)}, u32[]{:S(2)}, u32[]{:S(2)}) async-start(f32[128,1,1,2,64,128]{5,4,3,2,1,0:T(8,128)} %get-tuple-element.17), calls=%async_computation.1 | async-start | bytes 16777216 | tf_op jit(solution)/shard_map/all_to_all | solution.py:35
  145.3 111.7 %copy-start.2 = (f32[8,2,128,128]{2,3,0,1:T(8,128)}, f32[8,2,128,128]{2,3,0,1:T(8,128)S(1)}, u32[]{:S(2)}) copy-start(f32[8,2,128,128]{2,3,0,1:T(8,128)S(1)} %copy.74) | copy-start | bytes 3145732
  284.5 37.3 %copy-start.1 = (f32[256,2,128,128]{3,2,1,0:T(8,128)S(1)}, f32[256,2,128,128]{3,2,1,0:T(8,128)}, u32[]{:S(2)}) copy-start(f32[256,2,128,128]{3,2,1,0:T(8,128)} %gather_fusion.1) | copy-start | bytes 100663296
  437.8 13.0 %copy-start.4 = (f32[16,8,1,128,128]{3,4,1,0,2:T(8,128)S(1)}, f32[16,8,1,128,128]{3,4,1,0,2:T(8,128)}, u32[]{:S(2)}) copy-start(f32[16,8,1,128,128]{3,4,1,0,2:T(8,128)} %copy.102) | copy-start | bytes 25165828
  450.8 11.1 %copy-start.3 = (f32[8,2,128,128]{2,3,0,1:T(8,128)S(1)}, f32[8,2,128,128]{2,3,0,1:T(8,128)}, u32[]{:S(2)}) copy-start(f32[8,2,128,128]{2,3,0,1:T(8,128)} %copy-done.2) | copy-start | bytes 3145732
  450.8 11.1 %copy-start.6 = (f32[8,1,128,128]{2,3,0,1:T(8,128)S(1)}, f32[8,1,128,128]{2,3,0,1:T(8,128)}, u32[]{:S(2)}) copy-start(f32[8,1,128,128]{2,3,0,1:T(8,128)} %fusion.23) | copy-start | bytes 1572868
  450.8 11.1 %copy-start.7 = (f32[8,1,128,128]{2,3,0,1:T(8,128)S(1)}, f32[8,1,128,128]{2,3,0,1:T(8,128)}, u32[]{:S(2)}) copy-start(f32[8,1,128,128]{2,3,0,1:T(8,128)} %fusion.21) | copy-start | bytes 1572868
where the time goes:
time: 508 us; the launch traced here: 504 us
  blocking collectives  147 us (29%)
  local copies, waits for them, and re-layouts  102 us (20%)
  matrix products  101 us (20%)
  waiting for transfers between devices  97.6 us (19%)
  other arithmetic  47.2 us (9%)
  starting transfers between devices  7.22 us (1%)
    all_to_all x1, blocking collectives, several_exchanges(): lax.all_to_all(slab, axis, split_axis=0, concat_axis=0, tiled=True)  110 us
    all_to_all x1, waiting for transfers between devices, several_exchanges(): lax.all_to_all(slab, axis, split_axis=0, concat_axis=0, tiled=True)  97.6 us
    dot_general x1, matrix products, derive(): jnp.einsum('kij,kmcjl->kmcil', stacked, picked, precision=lax.Precision.H...  57.4 us
    unnamed x32, local copies, waits for them, and re-layouts  40.4 us
    dot_general x1, matrix products, derive(): jnp.einsum('kmcij,kjl->kmcil', picked, stacked, precision=lax.Precision.H...  37.3 us
    psum x4, blocking collectives, over_axes(): value = lax.psum(value, axis)  37 us
    gather x1, local copies, waits for them, and re-layouts, derive(): picked = jnp.take(buffer, jnp.clip(joined, 0, buffer.shape[0] - 1), axis=0)  20.9 us
    slice x1, local copies, waits for them, and re-layouts, derive(): comm = jnp.sum(lefts[:modes] - rights[:modes], axis=0)  11.7 us
  transfers between devices with their start and end apart: 1, of which 1 were waited for; matrix products, arithmetic and copies ran while one was open for 1% of the time, Pallas kernels for 0%

commit v1 on v0

v1 whole, which is shorter than its diff:
```python
import functools

import jax
import jax.numpy as jnp
from jax import lax
from jax.experimental import pallas as pl
from jax.experimental.pallas import tpu as pltpu
from jax.sharding import Mesh
from jax.sharding import PartitionSpec as P

PLANE = ("gy_0", "gy_1")
LINE = ("gx_0", "gx_1")
ALL = LINE + PLANE
UNROLL = 4
F32 = jnp.float32
BF16 = jnp.bfloat16


def dot(a, b):
    return jnp.dot(a, b, preferred_element_type=F32)


def split(value):
    high = value.astype(BF16)
    return high, (value - high.astype(F32)).astype(BF16)


def load_mode(q_ref, k, rows_ref, cols_ref):
    high, low = split(q_ref[k])
    n = high.shape[0]
    rows_ref[k, :n] = high
    rows_ref[k, n:] = low
    cols_ref[k, :, :n] = high
    cols_ref[k, :, n:] = low


def products(q_rows, q_cols, u):
    n = u.shape[-1]
    high, low = split(u)
    q_high = q_rows[:n]
    wide_high = jnp.concatenate([high[0], high[1]], axis=1)
    wide_low = jnp.concatenate([low[0], low[1]], axis=1)
    z = dot(q_rows, wide_high)
    left = z[:n] + z[n:] + dot(q_high, wide_low)
    tall_high = high.reshape(2 * n, n)
    tall_low = low.reshape(2 * n, n)
    w = dot(tall_high, q_cols)
    right = w[:, :n] + w[:, n:] + dot(tall_low, q_high)
    return left[:, :n], left[:, n:], right[:n], right[n:]


def compact_kernel(table_ref, list_ref, count_ref):
    slots = table_ref.shape[0]

    def visit(i, count):
        source = table_ref[i]
        list_ref[count] = i * 128 + source
        return count + (source >= 0).astype(jnp.int32)

    count = lax.fori_loop(0, slots, visit, jnp.int32(0), unroll=8)
    for i in range(UNROLL):
        list_ref[count + i] = 0
    count_ref[0] = count


def compact(table):
    slots = table.shape[0]
    smem = pl.BlockSpec(memory_space=pltpu.SMEM)
    return pl.pallas_call(
        compact_kernel,
        out_shape=(
            jax.ShapeDtypeStruct((slots + UNROLL,), jnp.int32),
            jax.ShapeDtypeStruct((1,), jnp.int32),
        ),
        in_specs=[smem],
        out_specs=(smem, smem),
    )(table)


def add_terms(list_ref, count_ref, occ_ref, coef_ref, source_ref, rows_ref, cols_ref, out_ref):
    modes = rows_ref.shape[0]
    count = count_ref[0]

    def step(i, carry):
        for j in range(UNROLL):
            t = i * UNROLL + j
            code = list_ref[t]
            slot = code >> 7
            m = slot // (2 * modes)
            down = (slot // modes) % 2
            k = slot % modes
            weight = occ_ref[m * modes + k].astype(F32)
            live = t < count
            alpha = jnp.where(down == 1, weight * coef_ref[k], 1.0)
            beta = jnp.where(down == 1, weight * coef_ref[modes + k], 0.0)
            alpha = jnp.where(live, alpha, 0.0)
            beta = jnp.where(live, beta, 0.0)
            a_re, a_im, b_re, b_im = products(rows_ref[k], cols_ref[k], source_ref[code & 127])
            out_ref[m, 0] += alpha * (a_im - b_im) + beta * (a_re + b_re)
            out_ref[m, 1] += beta * (a_im + b_im) - alpha * (a_re - b_re)
        return carry

    lax.fori_loop(0, (count + UNROLL - 1) // UNROLL, step, 0)


def own_kernel(
    list_ref, count_ref, occ_ref, coef_ref, damp_ref, source_ref, q_ref, h_ref, out_ref, rows_ref, cols_ref,
    hrows_ref, hcols_ref
):
    for k in range(q_ref.shape[0]):
        load_mode(q_ref, k, rows_ref, cols_ref)
    for k in range(2):
        load_mode(h_ref, k, hrows_ref, hcols_ref)

    def one(m, carry):
        u = source_ref[m]
        ra, ia, rb, ib = products(hrows_ref[0], hcols_ref[0], u)
        rc, ic, rd, idd = products(hrows_ref[1], hcols_ref[1], u)
        comm_re = (ra - ic) - (rb - idd)
        comm_im = (ia + rc) - (ib + rd)
        out_ref[m, 0] = comm_im - damp_ref[m] * u[0]
        out_ref[m, 1] = -comm_re - damp_ref[m] * u[1]
        return carry

    lax.fori_loop(0, source_ref.shape[0], one, 0)
    add_terms(list_ref, count_ref, occ_ref, coef_ref, source_ref, rows_ref, cols_ref, out_ref)


def far_kernel(list_ref, count_ref, occ_ref, coef_ref, source_ref, q_ref, out_ref, rows_ref, cols_ref):
    for k in range(q_ref.shape[0]):
        load_mode(q_ref, k, rows_ref, cols_ref)

    def clear(m, carry):
        out_ref[m] = jnp.zeros(out_ref.shape[1:], F32)
        return carry

    lax.fori_loop(0, out_ref.shape[0], clear, 0)
    add_terms(list_ref, count_ref, occ_ref, coef_ref, source_ref, rows_ref, cols_ref, out_ref)


def call(kernel, scalars, arrays, dests, scratch):
    smem = pl.BlockSpec(memory_space=pltpu.SMEM)
    vmem = pl.BlockSpec(memory_space=pltpu.VMEM)
    n = arrays[0].shape[-1]
    return pl.pallas_call(
        kernel,
        out_shape=jax.ShapeDtypeStruct((dests, 2, n, n), F32),
        in_specs=[smem] * len(scalars) + [vmem] * len(arrays),
        out_specs=vmem,
        scratch_shapes=scratch,
        compiler_params=pltpu.CompilerParams(vmem_limit_bytes=48 << 20),
    )(*scalars, *arrays)


def body(
    state,
    hamiltonian,
    couplings,
    bath_coef,
    bath_rate,
    occupation,
    send_list,
    up_index,
    down_index,
    step,
):
    local, _, n, _ = state.shape
    modes = couplings.shape[0]
    nx, nc = lax.axis_size("gx_0"), lax.axis_size("gx_1")
    line, plane = nx * nc, lax.axis_size("gy_0") * lax.axis_size("gy_1")
    x, c = lax.axis_index("gx_0"), lax.axis_index("gx_1")
    me = x * nc + c
    q = lax.axis_index("gy_0") * lax.axis_size("gy_1") + lax.axis_index("gy_1")

    gathered = lax.all_gather(state, PLANE, axis=0, tiled=True)

    mine = jnp.stack([up_index, down_index, occupation])
    tables = lax.all_to_all(
        jnp.broadcast_to(mine, (line,) + mine.shape), LINE, split_axis=0, concat_axis=0, tiled=True
    )
    listed = send_list.reshape(line, plane).T
    listed = lax.all_to_all(listed, PLANE, split_axis=0, concat_axis=0, tiled=True)

    offset = jnp.arange(line, dtype=jnp.int32)
    dest = (x + offset % nx) % nx * nc + (c + offset // nx) % nc
    pick = (dest[:, None] == jnp.arange(line, dtype=jnp.int32)[None, :]).astype(jnp.int32)
    tables = jnp.sum(pick[:, :, None, None, None] * tables[None], axis=1)
    listed = jnp.sum(pick[None, :, :] * listed[:, None, :], axis=2)
    entry = jnp.transpose(tables[:, :2], (0, 2, 1, 3)).reshape(line, local * 2 * modes)
    occ = tables[:, 2].reshape(line, local * modes)
    far = entry - local
    far_plane = far % plane
    hit = far_plane[:, :, None] == jnp.arange(plane, dtype=jnp.int32)
    slot = jnp.sum(hit * listed.T[:, None, :], axis=2)
    good = (far >= 0) & (far // plane == me) & (slot >= 0)
    table = jnp.where(good, far_plane * local + slot, -1).reshape(2, -1)
    occ = occ.reshape(2, -1)

    coef = bath_coef.reshape(-1)
    damp = jnp.sum(occupation.astype(F32) * bath_rate[None, :], axis=1)
    near = jnp.stack([up_index, down_index], axis=1).reshape(-1)
    near = jnp.where(near < local, near, -1)
    near_list, near_count = compact(near)

    mode_scratch = [pltpu.VMEM((modes, 2 * n, n), BF16), pltpu.VMEM((modes, n, 2 * n), BF16)]
    ham_scratch = [pltpu.VMEM((2, 2 * n, n), BF16), pltpu.VMEM((2, n, 2 * n), BF16)]
    own = call(
        own_kernel,
        [near_list, near_count, occupation.reshape(-1), coef, damp],
        [state, couplings, hamiltonian],
        local,
        mode_scratch + ham_scratch,
    )
    other_list, other_count = compact(table[1])
    same_list, same_count = compact(table[0])

    swap = call(
        far_kernel, [other_list, other_count, occ[1], coef], [gathered, couplings], nx * local, mode_scratch
    )
    swapped = lax.ppermute(swap, "gx_1", [(i, (i + 1) % nc) for i in range(nc)])
    same = call(
        far_kernel, [same_list, same_count, occ[0], coef], [gathered, couplings], nx * local, mode_scratch
    )
    pieces = [
        same[d * local : (d + 1) * local] + swapped[d * local : (d + 1) * local] for d in range(nx)
    ]
    derivative = own + pieces[0]
    for d in (2, 1, 3):
        derivative = derivative + lax.ppermute(pieces[d], "gx_0", [(i, (i + d) % nx) for i in range(nx)])

    total = jnp.sum(derivative * derivative)
    for axis in ALL:
        size = lax.axis_size(axis)
        parts = [
            lax.ppermute(total, axis, [(i, (i + d) % size) for i in range(size)]) for d in range(1, size)
        ]
        total = functools.reduce(jnp.add, parts, total)
    count = local * line * plane * 2 * n * n
    rms = jnp.sqrt(total / count + 1e-06)
    return derivative, state + step[0] / rms * derivative


def solution(mesh):
    torus = Mesh(mesh.devices.reshape(4, 2, 4, 4), ("gx_0", "gx_1", "gy_0", "gy_1"))
    whole = P(ALL, None, None, None)
    index = P(ALL, None)
    in_specs = (whole, P(), P(), P(), P(), index, P(ALL, None, None), index, index, P())
    return jax.shard_map(body, mesh=torus, in_specs=in_specs, out_specs=(whole, whole), check_vma=False)
```

time: 508 us -> 262 us (0.52)
  blocking collectives: 147 us -> 0 us
  matrix products: 101 us -> 0 us
  local copies, waits for them, and re-layouts: 102 us -> 8.42 us
  Pallas kernels: 0 us -> 55.8 us
  starting transfers between devices: 7.22 us -> 44.3 us
  other arithmetic: 47.2 us -> 13.9 us
  between operations: 2.24 us -> 21.7 us
  waiting for transfers between devices: 97.6 us -> 113 us
    all_to_all x1 -> x0, blocking collectives: 110 us -> none  [several_exchanges(): lax.all_to_all(slab, axis, split_axis=0, concat_axis=0, tiled=True)]
    dot_general x10 -> x0, matrix products: 101 us -> none  [the longest x1 57.4 us: derive(): jnp.einsum('kij,kmcjl->kmcil', stacked, picked, precision=lax.Precision.H...]
    all_to_all x1 -> x2, waiting for transfers between devices: 97.6 us -> 8.59 us  [the longest x1 4.55 us: body(): lax.all_to_all(jnp.broadcast_to(mine, (line,) + mine.shape), LINE, split_...]
    all_gather x0 -> x1, waiting for transfers between devices: none -> 81.3 us  [body(): gathered = lax.all_gather(state, PLANE, axis=0, tiled=True)]
    pallas_call x0 -> x6, Pallas kernels: none -> 55.8 us  [the longest x3 44.8 us: call(): pl.pallas_call(kernel, out_shape=jax.ShapeDtypeStruct((dests, 2, n, n), F...]
    psum x4 -> x0, blocking collectives: 37 us -> none  [over_axes(): value = lax.psum(value, axis)]
    unnamed x32, local copies, waits for them, and re-layouts: 40.4 us -> 5.82 us
    gather x2 -> x0, local copies, waits for them, and re-layouts: 31.9 us -> none  [the longest x1 20.9 us: derive(): picked = jnp.take(buffer, jnp.clip(joined, 0, buffer.shape[0] - 1), axis=0)]
  transfers between devices with their start and end apart: 1 -> 17, of which waited for: 1 -> 4; matrix products, arithmetic and copies ran while one was open for 1% -> 3% of each run, Pallas kernels for 0% -> 16%
where the time goes in v1:
time: 262 us; the launch traced here: 257 us
  waiting for transfers between devices  113 us (43%)
  Pallas kernels  55.8 us (21%)
  starting transfers between devices  44.3 us (17%)
  between operations  21.7 us (8%)
  other arithmetic  13.9 us (5%)
  local copies, waits for them, and re-layouts  8.42 us (3%)
    all_gather x1, waiting for transfers between devices, body(): gathered = lax.all_gather(state, PLANE, axis=0, tiled=True)  81.3 us
    pallas_call x3, Pallas kernels, call(): pl.pallas_call(kernel, out_shape=jax.ShapeDtypeStruct((dests, 2, n, n), F...  44.8 us
    ppermute x3, waiting for transfers between devices, body(): lax.ppermute(pieces[d], 'gx_0', [(i, (i + d) % nx) for i in range(nx)])  22.3 us
    ppermute x10, starting transfers between devices, body(): lax.ppermute(total, axis, [(i, (i + d) % size) for i in range(size)])  20.3 us
    pallas_call x3, Pallas kernels, compact(): pl.pallas_call(compact_kernel, out_shape=(jax.ShapeDtypeStruct((slots + U...  11 us
    all_to_all x1, starting transfers between devices, body(): lax.all_to_all(listed, PLANE, split_axis=0, concat_axis=0, tiled=True)  8.6 us
    ppermute x3, starting transfers between devices, body(): lax.ppermute(pieces[d], 'gx_0', [(i, (i + d) % nx) for i in range(nx)])  7.12 us
    all_to_all x1, starting transfers between devices, body(): lax.all_to_all(jnp.broadcast_to(mine, (line,) + mine.shape), LINE, split_...  6.4 us
  transfers between devices with their start and end apart: 17, of which 4 were waited for; matrix products, arithmetic and copies ran while one was open for 3% of the time, Pallas kernels for 16%

profile of v1, /device:TPU:1, one launch (start us, length us, event | category | flops | bytes accessed | tf_op | source)
XLA Modules:
  0.0 257.1 jit_solution(15417722812068678941)
XLA Ops:
  10.5 8.6 %all-to-all-start.1 = ((s32[16,1,8]{2,1,0:T(1,128)}), s32[16,1,8]{2,1,0:T(1,128)S(1)}, u32[]{:S(2)}, u32[]{:S(2)}) async-start(s32[16,1,8]{2,1,0:T(1,128)} %copy.21), calls=%async_computation.1 | async-start | bytes 16384 | tf_op jit(solution)/shard_map/all_to_all | solution.py:182
  21.4 4.0 %all-to-all-done.1 = s32[16,1,8]{2,1,0:T(1,128)S(1)} async-done(((s32[16,1,8]{2,1,0:T(1,128)}), s32[16,1,8]{2,1,0:T(1,128)S(1)}, u32[]{:S(2)}, u32[]{:S(2)}) %all-to-all-start.1) | async-done | bytes 544 | tf_op jit(solution)/shard_map/all_to_all | solution.py:182
  25.4 6.4 %all-to-all-start = ((s32[8,1,384]{2,1,0:T(1,128)}), s32[8,1,384]{2,1,0:T(1,128)S(1)}, u32[]{:S(2)}, u32[]{:S(2)}) async-start(s32[8,1,384]{2,1,0:T(1,128)} %reshape.151), calls=%async_computation | async-start | bytes 24576 | tf_op jit(solution)/shard_map/all_to_all | solution.py:178
  32.0 4.6 %all-to-all-done = s32[8,1,384]{2,1,0:T(1,128)S(1)} async-done(((s32[8,1,384]{2,1,0:T(1,128)}), s32[8,1,384]{2,1,0:T(1,128)S(1)}, u32[]{:S(2)}, u32[]{:S(2)}) %all-to-all-start) | async-done | bytes 12320 | tf_op jit(solution)/shard_map/all_to_all | solution.py:178
  38.9 4.5 %shard_map.117 = (s32[1028]{0:T(1024)}, s32[1]{0:T(128)}) custom-call(s32[1024]{0:T(1024)} %bitcast.29), custom_call_target="tpu_custom_call" | custom-call | tf_op jit(solution)/shard_map/pallas_call | solution.py:69
  43.5 81.3 %all-gather.2.cloned.1.call-done.source_ref = f32[128,2,128,128]{3,2,1,0:T(8,128)} async-done(((f32[8,2,128,128]{3,2,1,0:T(8,128)}), f32[128,2,128,128]{3,2,1,0:T(8,128)}) %all-gather.2.cloned.1.call-update) | async-done | bytes 16777232 | tf_op jit(solution)/shard_map/all_gather | solution.py:175
  126.8 14.9 %shard_map.118 = f32[32,2,128,128]{3,2,1,0:T(8,128)} custom-call(s32[1028]{0:T(1024)S(1)} %copy-done.5, s32[1]{0:T(128)} %get-tuple-element.13.count_ref, s32[512]{0:T(512)S(1)} %squeeze.18.occ_ref, f32[32]{0:T(128)S(1)} %reshape.140.coef_ref, f32[128,2,128,128]{3,2,1,0:T(8,128)} %all-gather.2.cloned.1.call-done.source_ref, f32[16,128,128]{2,1,0:T(8,128)S(1)} %copy-done.2), custom_call_target="tpu_custom_call" | custom-call | tf_op jit(solution)/shard_map/pallas_call | solution.py:145
  141.7 1.9 collective-permute-start
  144.1 4.5 %shard_map.115 = (s32[1028]{0:T(1024)}, s32[1]{0:T(128)}) custom-call(s32[1024]{0:T(1024)} %bitcast.30), custom_call_target="tpu_custom_call" | custom-call | tf_op jit(solution)/shard_map/pallas_call | solution.py:69
  149.4 12.8 %shard_map.116 = f32[32,2,128,128]{3,2,1,0:T(8,128)S(1)} custom-call(s32[1028]{0:T(1024)S(1)} %copy-done.6, s32[1]{0:T(128)} %get-tuple-element.11.count_ref, s32[512]{0:T(512)S(1)} %squeeze.16.occ_ref, f32[32]{0:T(128)S(1)} %reshape.140.coef_ref, f32[128,2,128,128]{3,2,1,0:T(8,128)} %all-gather.2.cloned.1.call-done.source_ref, f32[16,128,128]{2,1,0:T(8,128)S(1)} %copy-done.3), custom_call_target="tpu_custom_call" | custom-call | tf_op jit(solution)/shard_map/pallas_call | solution.py:145
  162.3 5.3 %slice_add_fusion.2 = (f32[8,2,128,128]{3,2,1,0:T(8,128)}, f32[8,2,128,128]{3,2,1,0:T(8,128)S(1)}, f32[8,2,128,128]{3,2,1,0:T(8,128)}) fusion(f32[32,2,128,128]{3,2,1,0:T(8,128)} %collective-permute-done, f32[32,2,128,128]{3,2,1,0:T(8,128)S(1)} %shard_map.116), kind=kLoop, calls=%fused_computation.2 | loop fusion | flops 786432 | bytes 9437184 | tf_op jit(solution)/shard_map/add | solution.py:225
  167.6 4.4 %collective-permute-start.1 = (f32[8,2,128,128]{3,2,1,0:T(8,128)}, f32[8,2,128,128]{3,2,1,0:T(8,128)}, u32[]{:S(2)}, u32[]{:S(2)}) collective-permute-start(f32[8,2,128,128]{3,2,1,0:T(8,128)} %get-tuple-element.16), channel_id=1, source_target_pairs={{0,64},{32,96},{64,0},{96,32},{1,65},{33,97},{65,1},{97,33},{2,66}... | collective-permute-start | bytes 3145736 | tf_op jit(solution)/shard_map/ppermute | solution.py:229
  172.0 2.5 collective-permute-start.2
  175.5 2.0 shard_map.113
  179.0 17.1 %shard_map.114 = f32[8,2,128,128]{3,2,1,0:T(8,128)S(1)} custom-call(s32[260]{0:T(512)S(1)} %copy-done.7, s32[1]{0:T(128)} %get-tuple-element.9.count_ref, s32[128]{0:T(128)S(1)} %reshape.139.occ_ref, f32[32]{0:T(128)S(1)} %reshape.140.coef_ref, f32[8]{0:T(128)S(1)} %multiply_reduce_fusion.3.damp_ref, f32[8,2,128,128]{3,2,1,0:T(8,128)S(1)} %copy-done.1, ...), custom_call_target="tpu_custom_call" | custom-call | tf_op jit(solution)/shard_map/pallas_call | solution.py:145
  196.2 22.3 %collective-permute-done.2 = f32[8,2,128,128]{3,2,1,0:T(8,128)} collective-permute-done((f32[8,2,128,128]{3,2,1,0:T(8,128)}, f32[8,2,128,128]{3,2,1,0:T(8,128)}, u32[]{:S(2)}, u32[]{:S(2)}) %collective-permute-start.2) | collective-permute-done | bytes 1048608 | tf_op jit(solution)/shard_map/ppermute | solution.py:229
  218.5 3.6 %multiply_reduce_fusion = (f32[]{:T(128)}, f32[8,2,128,128]{3,2,1,0:T(8,128)S(1)}) fusion(f32[8,2,128,128]{3,2,1,0:T(8,128)} %collective-permute-done.3, f32[8,2,128,128]{3,2,1,0:T(8,128)} %collective-permute-done.2, f32[8,2,128,128]{3,2,1,0:T(8,128)} %collective-permute-done.1, f32[8,2,128,128]{3,2,1,0:T(8,128)S(1)} %shard_map.114, ...), kind=kLoop, calls=%fused_computation.9 | loop fusion | flops 1835007 | bytes 7340036 | tf_op jit(solution)/shard_map/reduce_sum | solution.py:231
  222.1 2.5 collective-permute-start.4
  225.3 2.1 collective-permute-start.6
  229.8 3.0 %collective-permute-start.7 = (f32[]{:T(128)}, f32[]{:T(128)}, u32[]{:S(2)}, u32[]{:S(2)}) collective-permute-start(f32[]{:T(128)} %add.163), channel_id=1, source_target_pairs={{0,16},{16,0},{1,17},{17,1},{2,18},{18,2},{3,19},{19,3},{4,20},{20... | collective-permute-start | bytes 20 | tf_op jit(solution)/shard_map/ppermute | solution.py:235
  234.4 3.7 %collective-permute-start.9 = (f32[]{:T(128)}, f32[]{:T(128)}, u32[]{:S(2)}, u32[]{:S(2)}) collective-permute-start(f32[]{:T(128)} %add.164), channel_id=1, source_target_pairs={{0,8},{4,12},{8,0},{12,4},{1,9},{5,13},{9,1},{13,5},{2,10},{6,14},... | collective-permute-start | bytes 20 | tf_op jit(solution)/shard_map/ppermute | solution.py:235
  238.1 1.6 collective-permute-start.10
  242.4 3.3 %collective-permute-start.12 = (f32[]{:T(128)}, f32[]{:T(128)}, u32[]{:S(2)}, u32[]{:S(2)}) collective-permute-start(f32[]{:T(128)} %add.167), channel_id=1, source_target_pairs={{0,2},{1,3},{2,0},{3,1},{4,6},{5,7},{6,4},{7,5},{8,10},{9,11},{10,... | collective-permute-start | bytes 20 | tf_op jit(solution)/shard_map/ppermute | solution.py:235
  245.7 1.6 collective-permute-start.13
  (80 shorter events, 16.8 us)
Async XLA Ops:
  7.2 117.7 %all-gather.2.cloned.1.call-start = ((), (), s32[]{:S(2)}) async-start(), calls=%async_computation.2 | async-start | bytes 17825792 | tf_op jit(solution)/shard_map/all_gather | solution.py:175
  10.5 14.9 %all-to-all-start.1 = ((s32[16,1,8]{2,1,0:T(1,128)}), s32[16,1,8]{2,1,0:T(1,128)S(1)}, u32[]{:S(2)}, u32[]{:S(2)}) async-start(s32[16,1,8]{2,1,0:T(1,128)} %copy.21), calls=%async_computation.1 | async-start | bytes 16384 | tf_op jit(solution)/shard_map/all_to_all | solution.py:182
  25.4 11.1 %all-to-all-start = ((s32[8,1,384]{2,1,0:T(1,128)}), s32[8,1,384]{2,1,0:T(1,128)S(1)}, u32[]{:S(2)}, u32[]{:S(2)}) async-start(s32[8,1,384]{2,1,0:T(1,128)} %reshape.151), calls=%async_computation | async-start | bytes 24576 | tf_op jit(solution)/shard_map/all_to_all | solution.py:178
  126.8 21.9 %copy-start.3 = (f32[16,128,128]{2,1,0:T(8,128)S(1)}, f32[16,128,128]{2,1,0:T(8,128)}, u32[]{:S(2)}) copy-start(f32[16,128,128]{2,1,0:T(8,128)} %q_ref.5) | copy-start | bytes 3145732
  141.7 20.6 %collective-permute-start = (f32[32,2,128,128]{3,2,1,0:T(8,128)}, f32[32,2,128,128]{3,2,1,0:T(8,128)}, u32[]{:S(2)}, u32[]{:S(2)}) collective-permute-start(f32[32,2,128,128]{3,2,1,0:T(8,128)} %shard_map.118), channel_id=1, source_target_pairs={{0,16},{16,0},{1,17},{17,1},{2,18},{18,2},{3,19},{19,3},{4,20},{20... | collective-permute-start | bytes 12582920 | tf_op jit(solution)/shard_map/ppermute | solution.py:220
  162.2 12.6 %copy-start.10 = (s32[8,16]{1,0:T(8,128)S(1)}, s32[8,16]{1,0:T(8,128)}, u32[]{:S(2)}) copy-start(s32[8,16]{1,0:T(8,128)} %param.18) | copy-start | bytes 1540
  162.2 12.6 %copy-start.11 = (s32[8,16]{1,0:T(8,128)S(1)}, s32[8,16]{1,0:T(8,128)}, u32[]{:S(2)}) copy-start(s32[8,16]{1,0:T(8,128)} %param.17) | copy-start | bytes 1540
  162.2 16.0 %copy-start.12 = (f32[16]{0:T(128)S(1)}, f32[16]{0:T(128)}, u32[]{:S(2)}) copy-start(f32[16]{0:T(128)} %param.14) | copy-start | bytes 196
  162.2 16.1 %copy-start.1 = (f32[8,2,128,128]{3,2,1,0:T(8,128)S(1)}, f32[8,2,128,128]{3,2,1,0:T(8,128)}, u32[]{:S(2)}) copy-start(f32[8,2,128,128]{3,2,1,0:T(8,128)} %source_ref.1) | copy-start | bytes 3145732
  162.3 16.1 %copy-start.4 = (f32[2,128,128]{2,1,0:T(8,128)S(1)}, f32[2,128,128]{2,1,0:T(8,128)}, u32[]{:S(2)}) copy-start(f32[2,128,128]{2,1,0:T(8,128)} %h_ref.1) | copy-start | bytes 393220
  167.6 28.6 %collective-permute-start.1 = (f32[8,2,128,128]{3,2,1,0:T(8,128)}, f32[8,2,128,128]{3,2,1,0:T(8,128)}, u32[]{:S(2)}, u32[]{:S(2)}) collective-permute-start(f32[8,2,128,128]{3,2,1,0:T(8,128)} %get-tuple-element.16), channel_id=1, source_target_pairs={{0,64},{32,96},{64,0},{96,32},{1,65},{33,97},{65,1},{97,33},{2,66}... | collective-permute-start | bytes 3145736 | tf_op jit(solution)/shard_map/ppermute | solution.py:229
  172.0 46.5 %collective-permute-start.2 = (f32[8,2,128,128]{3,2,1,0:T(8,128)}, f32[8,2,128,128]{3,2,1,0:T(8,128)}, u32[]{:S(2)}, u32[]{:S(2)}) collective-permute-start(f32[8,2,128,128]{3,2,1,0:T(8,128)} %get-tuple-element.18), channel_id=1, source_target_pairs={{0,32},{32,64},{64,96},{96,0},{1,33},{33,65},{65,97},{97,1},{2,34}... | collective-permute-start | bytes 3145736 | tf_op jit(solution)/shard_map/ppermute | solution.py:229
  174.5 44.0 %collective-permute-start.3 = (f32[8,2,128,128]{3,2,1,0:T(8,128)S(1)}, f32[8,2,128,128]{3,2,1,0:T(8,128)}, u32[]{:S(2)}, u32[]{:S(2)}) collective-permute-start(f32[8,2,128,128]{3,2,1,0:T(8,128)S(1)} %get-tuple-element.17), channel_id=1, source_target_pairs={{0,96},{32,0},{64,32},{96,64},{1,97},{33,1},{65,33},{97,65},{2,98}... | collective-permute-start | bytes 3145736 | tf_op jit(solution)/shard_map/ppermute | solution.py:229
  222.1 28.2 %copy-start.8 = (f32[8,2,128,128]{3,2,1,0:T(8,128)}, f32[8,2,128,128]{3,2,1,0:T(8,128)S(1)}, u32[]{:S(2)}) copy-start(f32[8,2,128,128]{3,2,1,0:T(8,128)S(1)} %get-tuple-element.15) | copy-start | bytes 3145732
  222.1 5.2 %collective-permute-start.4 = (f32[]{:T(128)}, f32[]{:T(128)}, u32[]{:S(2)}, u32[]{:S(2)}) collective-permute-start(f32[]{:T(128)} %get-tuple-element.14), channel_id=1, source_target_pairs={{0,32},{32,64},{64,96},{96,0},{1,33},{33,65},{65,97},{97,1},{2,34}... | collective-permute-start | bytes 20 | tf_op jit(solution)/shard_map/ppermute | solution.py:235
  224.6 4.0 %collective-permute-start.5 = (f32[]{:T(128)}, f32[]{:T(128)}, u32[]{:S(2)}, u32[]{:S(2)}) collective-permute-start(f32[]{:T(128)} %get-tuple-element.14), channel_id=1, source_target_pairs={{0,64},{32,96},{64,0},{96,32},{1,65},{33,97},{65,1},{97,33},{2,66}... | collective-permute-start | bytes 20 | tf_op jit(solution)/shard_map/ppermute | solution.py:235
  225.3 4.0 %collective-permute-start.6 = (f32[]{:T(128)}, f32[]{:T(128)}, u32[]{:S(2)}, u32[]{:S(2)}) collective-permute-start(f32[]{:T(128)} %get-tuple-element.14), channel_id=1, source_target_pairs={{0,96},{32,0},{64,32},{96,64},{1,97},{33,1},{65,33},{97,65},{2,98}... | collective-permute-start | bytes 20 | tf_op jit(solution)/shard_map/ppermute | solution.py:235
  229.8 3.0 %collective-permute-start.7 = (f32[]{:T(128)}, f32[]{:T(128)}, u32[]{:S(2)}, u32[]{:S(2)}) collective-permute-start(f32[]{:T(128)} %add.163), channel_id=1, source_target_pairs={{0,16},{16,0},{1,17},{17,1},{2,18},{18,2},{3,19},{19,3},{4,20},{20... | collective-permute-start | bytes 20 | tf_op jit(solution)/shard_map/ppermute | solution.py:235
  233.4 6.3 %collective-permute-start.8 = (f32[]{:T(128)}, f32[]{:T(128)}, u32[]{:S(2)}, u32[]{:S(2)}) collective-permute-start(f32[]{:T(128)} %add.164), channel_id=1, source_target_pairs={{0,4},{4,8},{8,12},{12,0},{1,5},{5,9},{9,13},{13,1},{2,6},{6,10},{... | collective-permute-start | bytes 20 | tf_op jit(solution)/shard_map/ppermute | solution.py:235
  234.4 5.9 %collective-permute-start.9 = (f32[]{:T(128)}, f32[]{:T(128)}, u32[]{:S(2)}, u32[]{:S(2)}) collective-permute-start(f32[]{:T(128)} %add.164), channel_id=1, source_target_pairs={{0,8},{4,12},{8,0},{12,4},{1,9},{5,13},{9,1},{13,5},{2,10},{6,14},... | collective-permute-start | bytes 20 | tf_op jit(solution)/shard_map/ppermute | solution.py:235
  238.1 2.8 %collective-permute-start.10 = (f32[]{:T(128)}, f32[]{:T(128)}, u32[]{:S(2)}, u32[]{:S(2)}) collective-permute-start(f32[]{:T(128)} %add.164), channel_id=1, source_target_pairs={{0,12},{4,0},{8,4},{12,8},{1,13},{5,1},{9,5},{13,9},{2,14},{6,2},{... | collective-permute-start | bytes 20 | tf_op jit(solution)/shard_map/ppermute | solution.py:235
  241.6 5.7 %collective-permute-start.11 = (f32[]{:T(128)}, f32[]{:T(128)}, u32[]{:S(2)}, u32[]{:S(2)}) collective-permute-start(f32[]{:T(128)} %add.167), channel_id=1, source_target_pairs={{0,1},{1,2},{2,3},{3,0},{4,5},{5,6},{6,7},{7,4},{8,9},{9,10},{10,1... | collective-permute-start | bytes 20 | tf_op jit(solution)/shard_map/ppermute | solution.py:235
  242.4 5.5 %collective-permute-start.12 = (f32[]{:T(128)}, f32[]{:T(128)}, u32[]{:S(2)}, u32[]{:S(2)}) collective-permute-start(f32[]{:T(128)} %add.167), channel_id=1, source_target_pairs={{0,2},{1,3},{2,0},{3,1},{4,6},{5,7},{6,4},{7,5},{8,10},{9,11},{10,... | collective-permute-start | bytes 20 | tf_op jit(solution)/shard_map/ppermute | solution.py:235
  245.7 2.8 %collective-permute-start.13 = (f32[]{:T(128)}, f32[]{:T(128)}, u32[]{:S(2)}, u32[]{:S(2)}) collective-permute-start(f32[]{:T(128)} %add.167), channel_id=1, source_target_pairs={{0,3},{1,0},{2,1},{3,2},{4,7},{5,4},{6,5},{7,6},{8,11},{9,8},{10,9... | collective-permute-start | bytes 20 | tf_op jit(solution)/shard_map/ppermute | solution.py:235
  (6 other events, 21.2 us)
Sparse Core Ops, SparseCore 0:
  10.1 114.6 all-gather.1

commit v2 on v0

v2 whole, which is shorter than its diff:
```python
import functools

import jax
import jax.numpy as jnp
import numpy as np
from jax import lax
from jax.experimental import pallas as pl
from jax.experimental.pallas import tpu as pltpu
from jax.sharding import Mesh
from jax.sharding import PartitionSpec as P

ALL = ("xh", "xl", "c", "yh", "yl", "zh", "zl")
UNROLL = 4
F32 = jnp.float32
BF16 = jnp.bfloat16
PARTS = ((0, 3, "xyz"), (3, 6, "yzx"), (6, 8, "zxy"))


def dot(a, b):
    return jnp.dot(a, b, preferred_element_type=F32)


def cell_pairs(axis):
    pairs = []
    for x, c, y, z in np.ndindex(4, 2, 4, 4):
        at = {"x": x, "y": y, "z": z}
        to = dict(at)
        to[axis] = (((at[axis] + c) % 4 ^ 1) - c) % 4
        pairs.append((((x * 2 + c) * 4 + y) * 4 + z, ((to["x"] * 2 + c) * 4 + to["y"]) * 4 + to["z"]))
    return pairs


def flip(value, axis):
    return lax.ppermute(value, axis, [(0, 1), (1, 0)])


def split(value):
    high = value.astype(BF16)
    return high, (value - high.astype(F32)).astype(BF16)


def load_modes(q_ref, left_ref, right_ref):
    n = q_ref.shape[-1]

    def one(k, carry):
        high, low = split(q_ref[k])
        left_ref[k, :n, :n] = high
        left_ref[k, :n, n:] = high
        left_ref[k, n:, :n] = low
        left_ref[k, n:, n:] = low
        right_ref[k, :n, :n] = high
        right_ref[k, :n, n:] = low
        right_ref[k, n:, :n] = high
        right_ref[k, n:, n:] = low
        return carry

    lax.fori_loop(0, q_ref.shape[0], one, 0)


def products(left, right, u):
    n = u.shape[-1]
    high, low = split(u)
    tall = jnp.concatenate(
        [jnp.concatenate([high[0], high[1]], axis=1), jnp.concatenate([low[0], low[1]], axis=1)], axis=0
    )
    z = dot(left, tall)
    z = z[:n] + z[n:]
    wide = jnp.concatenate([high.reshape(2 * n, n), low.reshape(2 * n, n)], axis=1)
    w = dot(wide, right)
    w = w[:, :n] + w[:, n:]
    return z[:, :n], z[:, n:], w[:n], w[n:]


def plan_kernel(at_ref, low_ref, high_ref, lists_ref, plan_ref):
    x, y, z, c = (at_ref[i] for i in range(4))
    table = jnp.concatenate([low_ref[...], high_ref[...]], axis=0)
    row = lax.broadcasted_iota(jnp.int32, table.shape, 0) >> 3
    lane = lax.broadcasted_iota(jnp.int32, table.shape, 1)
    dx, dy, dz = x ^ (row & 2), y ^ ((row & 4) >> 1), z ^ ((row & 8) >> 2)
    device = (((dx << 1) + (c ^ (row & 1)) << 2) + dy << 2) + dz
    chosen = jnp.where(lane == device, 1.0, 0.0)
    listed = lax.dot_general(
        chosen, lists_ref[...], (((1,), (1,)), ((), ())), preferred_element_type=F32
    )
    far = table - 8
    owner = {"x": far >> 5, "y": (far >> 2) & 3, "z": far & 3}
    inside = (far >= 0) & (((far >> 4) & 1) == c) & (lane < 32)
    differs = {}
    for a, ours in zip("xyz", (x, y, z)):
        theirs, ours = (owner[a] + c) & 3, (ours + c) & 3
        inside = inside & ((theirs >> 1) == (ours >> 1))
        differs[a] = (theirs ^ ours) & 1
    member = sum(differs[a] << s for s, a in enumerate(PARTS[2][2]))
    slot = jnp.full(table.shape, -1.0, F32)
    for b in range(8):
        slot = jnp.where(member == b, listed[:, b : b + 1], slot)
    slot = slot.astype(jnp.int32)
    position = jnp.zeros(table.shape, jnp.int32)
    for lo, hi, order in PARTS:
        block = sum(differs[a] << s for s, a in enumerate(order))
        position = jnp.where((slot >= lo) & (slot < hi), 8 * lo + block * (hi - lo) + slot - lo, position)
    valid = inside & (slot >= 0)
    power = (1 << (lane & 15)).astype(F32)

    def half(bits):
        return jnp.sum(jnp.where(bits, power, 0.0), axis=1, keepdims=True).astype(jnp.int32)

    mask = half(valid & (lane < 16)) + (half(valid & (lane >= 16)) << 16)
    plan_ref[...] = jnp.where(lane == 48, mask, jnp.where(valid, position, table))


def encode(target, row, slot, source):
    return (((target << 7) + row << 5) + slot << 6) + source


def list_near(table_ref, list_ref):
    def visit(i, count):
        row, slot = i >> 5, i & 31
        entry = table_ref[row, slot]
        list_ref[count] = encode(row, row, slot, entry & 63)
        return count + ((entry >= 0) & (entry < 8)).astype(jnp.int32)

    return pad_list(list_ref, lax.fori_loop(0, 8 * 32, visit, jnp.int32(0), unroll=8))


def list_far(targets, rows_ref, first, plan_ref, list_ref):
    def append(state, target, row):
        bits, count = state
        slot = 31 - lax.clz(bits & -bits)
        list_ref[count] = encode(target, row, slot, plan_ref[row, slot])
        return bits & (bits - 1), count + 1

    def visit(target, count):
        row = rows_ref[first + target]
        add = functools.partial(append, target=target, row=row)
        return lax.while_loop(lambda s: s[0] != 0, add, (plan_ref[row, 48], count))[1]

    return pad_list(list_ref, lax.fori_loop(0, targets, visit, jnp.int32(0)))


def pad_list(list_ref, count):
    for j in range(UNROLL):
        list_ref[count + j] = 0
    return count


def add_terms(count, list_ref, plan_ref, coef_ref, source_ref, left_ref, right_ref, out_ref):
    modes = coef_ref.shape[0] // 2

    def step(i, carry):
        for j in range(UNROLL):
            t = i * UNROLL + j
            code = list_ref[t]
            slot = (code >> 6) & 31
            row = (code >> 11) & 127
            target = code >> 18
            k = slot & (modes - 1)
            weight = plan_ref[row, 2 * modes + k].astype(F32)
            down = slot >= modes
            live = t < count
            alpha = jnp.where(live, jnp.where(down, weight * coef_ref[k], 1.0), 0.0)
            beta = jnp.where(live & down, weight * coef_ref[modes + k], 0.0)
            a_re, a_im, b_re, b_im = products(left_ref[k], right_ref[k], source_ref[code & 63])
            out_ref[target, 0] += alpha * (a_im - b_im) + beta * (a_re + b_re)
            out_ref[target, 1] += beta * (a_im + b_im) - alpha * (a_re - b_re)
        return carry

    lax.fori_loop(0, (count + UNROLL - 1) // UNROLL, step, 0)


def own_kernel(
    table_ref, coef_ref, rate_ref, source_ref, q_ref, h_ref, out_ref, left_ref, right_ref, hl_ref, hr_ref, list_ref
):
    load_modes(q_ref, left_ref, right_ref)
    load_modes(h_ref, hl_ref, hr_ref)
    modes = q_ref.shape[0]

    def one(m, carry):
        u = source_ref[m]
        damp = jnp.float32(0)
        for k in range(modes):
            damp += table_ref[m, 2 * modes + k].astype(F32) * rate_ref[k]
        ra, ia, rb, ib = products(hl_ref[0], hr_ref[0], u)
        rc, ic, rd, im = products(hl_ref[1], hr_ref[1], u)
        comm_re = (ra - ic) - (rb - im)
        comm_im = (ia + rc) - (ib + rd)
        out_ref[m, 0] = comm_im - damp * u[0]
        out_ref[m, 1] = -comm_re - damp * u[1]
        return carry

    lax.fori_loop(0, source_ref.shape[0], one, 0)
    count = list_near(table_ref, list_ref)
    add_terms(count, list_ref, table_ref, coef_ref, source_ref, left_ref, right_ref, out_ref)


def far_kernel(pieces, plan_ref, coef_ref, rows_ref, q_ref, *refs):
    blocks, refs = refs[:pieces], refs[pieces:]
    outs, (source_ref, left_ref, right_ref, *lists, sems) = refs[:2], refs[2:]
    copies = []
    for part, (lo, hi, _) in enumerate(PARTS):
        size = hi - lo
        copies.append((blocks[0].at[pl.ds(lo, size)], source_ref.at[pl.ds(8 * lo, size)]))
        for stage in range(3):
            block = blocks[1 + 3 * part + stage]
            for b in range(1 << stage):
                src = block.at[pl.ds(b * (block.shape[0] >> stage), size)]
                copies.append((src, source_ref.at[pl.ds(8 * lo + (size << stage) + b * size, size)]))
    copies = [pltpu.make_async_copy(a, b, sems.at[i]) for i, (a, b) in enumerate(copies)]
    for copy in copies:
        copy.start()
    load_modes(q_ref, left_ref, right_ref)
    targets = outs[0].shape[0]

    def clear(m, carry):
        for out in outs:
            out[m] = jnp.zeros(out.shape[1:], F32)
        return carry

    lax.fori_loop(0, targets, clear, 0)
    counts = [list_far(targets, rows_ref, i * targets, plan_ref, lists[i]) for i in range(2)]
    for copy in copies:
        copy.wait()
    for out, terms, count in zip(outs, lists, counts):
        add_terms(count, terms, plan_ref, coef_ref, source_ref, left_ref, right_ref, out)


def spec(space):
    return pl.BlockSpec(memory_space=space)


def params(mib):
    return pltpu.CompilerParams(vmem_limit_bytes=mib << 20)


def mode_scratch(modes, n):
    return [pltpu.VMEM((modes, 2 * n, 2 * n), BF16)] * 2


def cost(terms, n):
    return pl.CostEstimate(flops=terms * 4 * (2 * n) ** 3, bytes_accessed=1 << 23, transcendentals=0)


def served_rows(rc):
    rows = []
    for high in (1, 0):
        for lo, hi, order in PARTS:
            weight = ["xyz".index(a) for a in order]
            for second, third in np.ndindex(2, 2):
                b = 2 * ((high << weight[0]) + (second << weight[1]) + (third << weight[2])) + rc
                rows += [b * 8 + m for m in range(lo, hi)]
    return np.array(rows, np.int32)


def body(
    state,
    hamiltonian,
    couplings,
    bath_coef,
    bath_rate,
    occupation,
    send_list,
    up_index,
    down_index,
    step,
):
    local, _, n, _ = state.shape
    modes = couplings.shape[0]
    devices = send_list.shape[1]
    bit = {a: lax.axis_index(a) for a in ALL}
    at = jnp.stack([2 * bit[a + "h"] + bit[a + "l"] for a in "xyz"] + [bit["c"]]).astype(jnp.int32)
    pairs = {a: cell_pairs(a) for a in "xyz"}

    held = [[state[lo:hi]] for lo, hi, _ in PARTS]
    note = jnp.zeros((1, 2, n, n), F32).at[0, 0, 0, :devices].set(send_list.reshape(devices).astype(F32))
    held[2][0] = jnp.concatenate([held[2][0], note], axis=0)
    table = jnp.concatenate(
        [up_index, down_index, occupation, jnp.zeros((local, devices - 3 * modes), jnp.int32)], axis=1
    )
    tables = jnp.concatenate([table, flip(table, "c")], axis=0)
    for stage in range(3):
        sends = [part[0] if stage == 0 else jnp.concatenate(part, axis=0) for part in held]
        sends, tables = lax.optimization_barrier((sends, tables))
        for part, block, (_, _, order) in zip(held, sends, PARTS):
            part.append(lax.ppermute(block, ALL, pairs[order[stage]]))
        other = flip(tables, "xyz"[stage] + "h")
        if stage < 2:
            tables = jnp.concatenate([tables, other], axis=0)
    lists = jnp.concatenate([block[2::3, 0, 0, :devices] for block in held[2]], axis=0)

    smem, vmem = spec(pltpu.SMEM), spec(pltpu.VMEM)
    plan = pl.pallas_call(
        plan_kernel,
        out_shape=jax.ShapeDtypeStruct((2 * tables.shape[0], devices), jnp.int32),
        in_specs=[smem] + [vmem] * 3,
        out_specs=vmem,
    )(at, tables, other, lists)

    coef = bath_coef.reshape(-1)
    here, _ = lax.optimization_barrier((state, sends))
    listing = pltpu.SMEM((1024 + UNROLL,), jnp.int32)
    own = pl.pallas_call(
        own_kernel,
        out_shape=jax.ShapeDtypeStruct(state.shape, F32),
        in_specs=[smem] * 3 + [vmem] * 3,
        out_specs=vmem,
        scratch_shapes=mode_scratch(modes, n) + mode_scratch(2, n) + [listing],
        compiler_params=params(16),
        cost_estimate=cost(160, n),
    )(table, coef, bath_rate, here, couplings, hamiltonian)

    blocks = [state] + [block for part in held for block in part[1:]]
    own, plan = lax.optimization_barrier((own, plan))
    target = jax.ShapeDtypeStruct((4 * local, 2, n, n), F32)
    partial = []
    for rc in (1, 0):
        partial += pl.pallas_call(
            functools.partial(far_kernel, len(blocks)),
            out_shape=(target, target),
            in_specs=[smem] * 3 + [vmem] + [spec(pl.ANY)] * len(blocks),
            out_specs=(vmem, vmem),
            scratch_shapes=[pltpu.VMEM((8 * local, 2, n, n), F32)]
            + mode_scratch(modes, n)
            + [listing, listing, pltpu.SemaphoreType.DMA((24,))],
            compiler_params=params(28),
            cost_estimate=cost(48, n),
        )(plan, coef, served_rows(rc), couplings, *blocks)
    swapped = [flip(partial[0], "c"), flip(partial[1], "c")]
    sums = []
    for lo, hi, axes in PARTS:
        rows = slice(4 * lo, 4 * hi)
        give = partial[2][rows] + swapped[0][rows]
        keep = partial[3][rows] + swapped[1][rows]
        for stage in range(3):
            keep = keep + flip(give, axes[stage] + "h")
            half = keep.shape[0] // 2
            if stage < 2:
                keep, give = keep[:half], keep[half:]
        sums.append(keep)
    derivative = own + jnp.concatenate(sums, axis=0)

    total = jnp.sum(derivative * derivative)
    total = jnp.sum(
        lax.all_to_all(jnp.broadcast_to(total, (devices,)), ALL, split_axis=0, concat_axis=0, tiled=True)
    )
    rms = jnp.sqrt(total / (devices * derivative.size) + 1e-06)
    return derivative, state + step[0] / rms * derivative


def solution(mesh):
    torus = Mesh(mesh.devices.reshape((2,) * 7), ALL)
    whole = P(ALL, None, None, None)
    index = P(ALL, None)
    in_specs = (whole, P(), P(), P(), P(), index, P(ALL, None, None), index, index, P())
    return jax.shard_map(body, mesh=torus, in_specs=in_specs, out_specs=(whole, whole), check_vma=False)
```

time: 508 us -> 196 us (0.39)
  blocking collectives: 147 us -> 0 us
  matrix products: 101 us -> 0 us
  local copies, waits for them, and re-layouts: 102 us -> 10.6 us
  starting transfers between devices: 7.22 us -> 55.8 us
  Pallas kernels: 0 us -> 41.8 us
  other arithmetic: 47.2 us -> 16.4 us
  waiting for transfers between devices: 97.6 us -> 69 us
    all_to_all x1 -> x0, blocking collectives: 110 us -> none  [several_exchanges(): lax.all_to_all(slab, axis, split_axis=0, concat_axis=0, tiled=True)]
    dot_general x10 -> x0, matrix products: 101 us -> none  [the longest x1 57.4 us: derive(): jnp.einsum('kij,kmcjl->kmcil', stacked, picked, precision=lax.Precision.H...]
    all_to_all x1, waiting for transfers between devices: 97.6 us -> 8.86 us  [body(): lax.all_to_all(jnp.broadcast_to(total, (devices,)), ALL, split_axis=0, co...]
    ppermute x0 -> x24, waiting for transfers between devices: none -> 60.1 us  [the longest x15 54 us: flip(): return lax.ppermute(value, axis, [(0, 1), (1, 0)])]
    ppermute x0 -> x24, starting transfers between devices: none -> 42.8 us  [the longest x15 26.8 us: flip(): return lax.ppermute(value, axis, [(0, 1), (1, 0)])]
    pallas_call x0 -> x4, Pallas kernels: none -> 41.8 us  [the longest x2 21.8 us: body(): pl.pallas_call(functools.partial(far_kernel, len(blocks)), out_shape=(tar...]
    psum x4 -> x0, blocking collectives: 37 us -> none  [over_axes(): value = lax.psum(value, axis)]
    unnamed x32 -> x42, local copies, waits for them, and re-layouts: 40.4 us -> 7.35 us
  transfers between devices with their start and end apart: 1 -> 25, of which waited for: 1 -> 14; matrix products, arithmetic and copies ran while one was open for 1% -> 7% of each run, Pallas kernels for 0% -> 16%
where the time goes in v2:
time: 196 us
  waiting for transfers between devices  69 us (35%)
  starting transfers between devices  55.8 us (28%)
  Pallas kernels  41.8 us (21%)
  other arithmetic  16.4 us (8%)
  local copies, waits for them, and re-layouts  10.6 us (5%)
  between operations  2.34 us (1%)
    ppermute x15, waiting for transfers between devices, flip(): return lax.ppermute(value, axis, [(0, 1), (1, 0)])  54 us
    ppermute x15, starting transfers between devices, flip(): return lax.ppermute(value, axis, [(0, 1), (1, 0)])  26.8 us
    pallas_call x2, Pallas kernels, body(): pl.pallas_call(functools.partial(far_kernel, len(blocks)), out_shape=(tar...  21.8 us
    pallas_call x1, Pallas kernels, body(): pl.pallas_call(own_kernel, out_shape=jax.ShapeDtypeStruct(state.shape, F3...  18.1 us
    ppermute x9, starting transfers between devices, body(): part.append(lax.ppermute(block, ALL, pairs[order[stage]]))  15.9 us
    all_to_all x1, starting transfers between devices, body(): lax.all_to_all(jnp.broadcast_to(total, (devices,)), ALL, split_axis=0, co...  13 us
    all_to_all x1, waiting for transfers between devices, body(): lax.all_to_all(jnp.broadcast_to(total, (devices,)), ALL, split_axis=0, co...  8.86 us
    unnamed x42, local copies, waits for them, and re-layouts  7.35 us
  transfers between devices with their start and end apart: 25, of which 14 were waited for; matrix products, arithmetic and copies ran while one was open for 7% of the time, Pallas kernels for 16%

profile of v2, /device:TPU:1, one launch (start us, length us, event | category | flops | bytes accessed | tf_op | source)
XLA Modules:
  0.0 195.8 jit_solution(16434796361295060925)
XLA Ops:
  5.9 2.6 %collective-permute-start.1 = (f32[3,2,128,128]{3,2,1,0:T(8,128)S(1)}, f32[3,2,128,128]{3,2,1,0:T(8,128)S(1)}, u32[]{:S(2)}, u32[]{:S(2)}) collective-permute-start(f32[3,2,128,128]{3,2,1,0:T(8,128)S(1)} %get-tuple-element.33), channel_id=1, source_target_pairs={{0,32},{1,33},{2,34},{3,35},{4,36},{5,37},{6,38},{7,39},{8,40},{9,... | collective-permute-start | bytes 1179656 | tf_op jit(solution)/shard_map/ppermute | solution.py:284
  8.5 2.7 %collective-permute-start.2 = (f32[3,2,128,128]{3,2,1,0:T(8,128)S(1)}, f32[3,2,128,128]{3,2,1,0:T(8,128)S(1)}, u32[]{:S(2)}, u32[]{:S(2)}) collective-permute-start(f32[3,2,128,128]{3,2,1,0:T(8,128)S(1)} %get-tuple-element.34), channel_id=1, source_target_pairs={{0,4},{1,5},{2,6},{3,7},{4,0},{5,1},{6,2},{7,3},{8,12},{9,13},{10,... | collective-permute-start | bytes 1179656 | tf_op jit(solution)/shard_map/ppermute | solution.py:284
  11.2 3.8 %collective-permute-start.3 = (f32[3,2,128,128]{3,2,1,0:T(8,128)S(1)}, f32[3,2,128,128]{3,2,1,0:T(8,128)S(1)}, u32[]{:S(2)}, u32[]{:S(2)}) collective-permute-start(f32[3,2,128,128]{3,2,1,0:T(8,128)S(1)} %get-tuple-element.35), channel_id=1, source_target_pairs={{0,1},{1,0},{2,3},{3,2},{4,5},{5,4},{6,7},{7,6},{8,9},{9,8},{10,11... | collective-permute-start | bytes 1179656 | tf_op jit(solution)/shard_map/ppermute | solution.py:284
  15.5 3.5 %collective-permute-done.4 = s32[16,128]{1,0:T(8,128)S(1)} collective-permute-done((s32[16,128]{1,0:T(8,128)S(1)}, s32[16,128]{1,0:T(8,128)S(1)}, u32[]{:S(2)}, u32[]{:S(2)}) %collective-permute-start.4) | collective-permute-done | bytes 8224 | tf_op jit(solution)/shard_map/ppermute | solution.py:34
  20.3 2.8 %collective-permute-start.6 = (f32[6,2,128,128]{3,2,1,0:T(8,128)S(1)}, f32[6,2,128,128]{3,2,1,0:T(8,128)S(1)}, u32[]{:S(2)}, u32[]{:S(2)}) collective-permute-start(f32[6,2,128,128]{3,2,1,0:T(8,128)S(1)} %pad_maximum_fusion.4), channel_id=1, source_target_pairs={{0,1},{1,0},{2,3},{3,2},{4,5},{5,4},{6,7},{7,6},{8,9},{9,8},{10,11... | collective-permute-start | bytes 2359304 | tf_op jit(solution)/shard_map/ppermute | solution.py:284
  24.8 2.8 %collective-permute-done.8 = s32[32,128]{1,0:T(8,128)S(1)} collective-permute-done((s32[32,128]{1,0:T(8,128)S(1)}, s32[32,128]{1,0:T(8,128)S(1)}, u32[]{:S(2)}, u32[]{:S(2)}) %collective-permute-start.8) | collective-permute-done | bytes 16416 | tf_op jit(solution)/shard_map/ppermute | solution.py:34
  27.6 5.1 %collective-permute-done.5.refs_2_ = f32[6,2,128,128]{3,2,1,0:T(8,128)S(1)} collective-permute-done((f32[6,2,128,128]{3,2,1,0:T(8,128)S(1)}, f32[6,2,128,128]{3,2,1,0:T(8,128)S(1)}, u32[]{:S(2)}, u32[]{:S(2)}) %collective-permute-start.5) | collective-permute-done | bytes 786464 | tf_op jit(solution)/shard_map/ppermute | solution.py:284
  42.6 18.1 %shard_map.131 = f32[8,2,128,128]{3,2,1,0:T(8,128)S(1)} custom-call(s32[8,128]{1,0:T(8,128)S(1)} %pad_add_fusion.3.table_ref, f32[32]{0:T(128)S(1)} %reshape.62.coef_ref, f32[16]{0:T(128)S(1)} %copy-done.11, f32[8,2,128,128]{3,2,1,0:T(8,128)S(1)} %copy-done, f32[16,128,128]{2,1,0:T(8,128)S(1)} %copy-done.8, f32[2,128,128]{2,1,0:T(8,128)S(1)} %copy-done.10), custom_call_target="tpu_custom_call" | custom-call | flops 10737418240 | bytes 8388608 | tf_op jit(solution)/shard_map/pallas_call | solution.py:301
  70.0 10.7 %shard_map.134 = (f32[32,2,128,128]{3,2,1,0:T(8,128)S(1)}, f32[32,2,128,128]{3,2,1,0:T(8,128)S(1)}) custom-call(s32[128,128]{1,0:T(8,128)S(1)} %copy-done.7, f32[32]{0:T(128)S(1)} %reshape.62.coef_ref, s32[64]{0:T(128)S(1)} %copy-done.13, f32[16,128,128]{2,1,0:T(8,128)S(1)} %copy-done.9, f32[8,2,128,128]{3,2,1,0:T(8,128)S(1)} %copy-done, ...), custom_call_target="tpu_custom_call" | custom-call | flops 3221225472 | bytes 8388608 | tf_op jit(solution)/shard_map/pallas_call | solution.py:316
  82.1 11.1 %shard_map.133 = (f32[32,2,128,128]{3,2,1,0:T(8,128)S(1)}, f32[32,2,128,128]{3,2,1,0:T(8,128)S(1)}) custom-call(s32[128,128]{1,0:T(8,128)S(1)} %copy-done.7, f32[32]{0:T(128)S(1)} %reshape.62.coef_ref, s32[64]{0:T(128)S(1)} %copy-done.12, f32[16,128,128]{2,1,0:T(8,128)S(1)} %copy-done.9, f32[8,2,128,128]{3,2,1,0:T(8,128)S(1)} %copy-done, ...), custom_call_target="tpu_custom_call" | custom-call | flops 3221225472 | bytes 8388608 | tf_op jit(solution)/shard_map/pallas_call | solution.py:316
  94.6 2.4 %collective-permute-start.15 = (f32[12,2,128,128]{3,2,1,0:T(8,128)S(1)}, f32[12,2,128,128]{3,2,1,0:T(8,128)S(1)}, u32[]{:S(2)}, u32[]{:S(2)}) collective-permute-start(f32[12,2,128,128]{3,2,1,0:T(8,128)S(1)} %get-tuple-element.56), channel_id=1, source_target_pairs={{0,64},{64,0},{1,65},{65,1},{2,66},{66,2},{3,67},{67,3},{4,68},{68... | collective-permute-start | bytes 4718600 | tf_op jit(solution)/shard_map/ppermute | solution.py:34
  99.3 25.0 %collective-permute-done.21 = f32[8,2,128,128]{3,2,1,0:T(8,128)S(1)} collective-permute-done((f32[8,2,128,128]{3,2,1,0:T(8,128)S(1)}, f32[8,2,128,128]{3,2,1,0:T(8,128)S(1)}, u32[]{:S(2)}, u32[]{:S(2)}) %collective-permute-start.21) | collective-permute-done | bytes 1048608 | tf_op jit(solution)/shard_map/ppermute | solution.py:34
  125.8 3.4 %collective-permute-start.22 = (f32[4,2,128,128]{3,2,1,0:T(8,128)S(1)}, f32[4,2,128,128]{3,2,1,0:T(8,128)S(1)}, u32[]{:S(2)}, u32[]{:S(2)}) collective-permute-start(f32[4,2,128,128]{3,2,1,0:T(8,128)S(1)} %slice.163), channel_id=1, source_target_pairs={{0,64},{64,0},{1,65},{65,1},{2,66},{66,2},{3,67},{67,3},{4,68},{68... | collective-permute-start | bytes 1572872 | tf_op jit(solution)/shard_map/ppermute | solution.py:34
  129.2 2.5 %collective-permute-done.15 = f32[12,2,128,128]{3,2,1,0:T(8,128)S(1)} collective-permute-done((f32[12,2,128,128]{3,2,1,0:T(8,128)S(1)}, f32[12,2,128,128]{3,2,1,0:T(8,128)S(1)}, u32[]{:S(2)}, u32[]{:S(2)}) %collective-permute-start.15) | collective-permute-done | bytes 1572896 | tf_op jit(solution)/shard_map/ppermute | solution.py:34
  132.8 2.8 %fusion.1 = (f32[12,2,128,128]{3,2,1,0:T(8,128)S(1)}, f32[12,2,128,128]{3,2,1,0:T(8,128)S(1)}) fusion(f32[12,2,128,128]{3,2,1,0:T(8,128)S(1)} %collective-permute-done.15, f32[32,2,128,128]{3,2,1,0:T(8,128)} %collective-permute-done.13, f32[32,2,128,128]{3,2,1,0:T(8,128)S(1)} %get-tuple-element.48, f32[12,2,128,128]{3,2,1,0:T(8,128)S(1)} %collective-permute-done.18), kind=kLoop, calls=%fused_computation.5 | loop fusion | flops 1572864 | bytes 12582912 | tf_op jit(solution)/shard_map/add | solution.py:334
  135.6 3.4 %collective-permute-start.19 = (f32[6,2,128,128]{3,2,1,0:T(8,128)S(1)}, f32[6,2,128,128]{3,2,1,0:T(8,128)S(1)}, u32[]{:S(2)}, u32[]{:S(2)}) collective-permute-start(f32[6,2,128,128]{3,2,1,0:T(8,128)S(1)} %slice.157), channel_id=1, source_target_pairs={{0,2},{2,0},{1,3},{3,1},{4,6},{6,4},{5,7},{7,5},{8,10},{10,8},{9,1... | collective-permute-start | bytes 2359304 | tf_op jit(solution)/shard_map/ppermute | solution.py:34
  139.7 3.4 %collective-permute-done.22 = f32[4,2,128,128]{3,2,1,0:T(8,128)S(1)} collective-permute-done((f32[4,2,128,128]{3,2,1,0:T(8,128)S(1)}, f32[4,2,128,128]{3,2,1,0:T(8,128)S(1)}, u32[]{:S(2)}, u32[]{:S(2)}) %collective-permute-start.22) | collective-permute-done | bytes 524320 | tf_op jit(solution)/shard_map/ppermute | solution.py:34
  143.1 4.7 %collective-permute-start.23 = (f32[2,2,128,128]{3,2,1,0:T(8,128)S(1)}, f32[2,2,128,128]{3,2,1,0:T(8,128)S(1)}, u32[]{:S(2)}, u32[]{:S(2)}) collective-permute-start(f32[2,2,128,128]{3,2,1,0:T(8,128)S(1)} %slice.165), channel_id=1, source_target_pairs={{0,8},{8,0},{1,9},{9,1},{2,10},{10,2},{3,11},{11,3},{4,12},{12,4},... | collective-permute-start | bytes 786440 | tf_op jit(solution)/shard_map/ppermute | solution.py:34
  147.8 6.5 %collective-permute-done.19 = f32[6,2,128,128]{3,2,1,0:T(8,128)S(1)} collective-permute-done((f32[6,2,128,128]{3,2,1,0:T(8,128)S(1)}, f32[6,2,128,128]{3,2,1,0:T(8,128)S(1)}, u32[]{:S(2)}, u32[]{:S(2)}) %collective-permute-start.19) | collective-permute-done | bytes 786464 | tf_op jit(solution)/shard_map/ppermute | solution.py:34
  154.4 5.2 %collective-permute-start.20 = (f32[3,2,128,128]{3,2,1,0:T(8,128)S(1)}, f32[3,2,128,128]{3,2,1,0:T(8,128)S(1)}, u32[]{:S(2)}, u32[]{:S(2)}) collective-permute-start(f32[3,2,128,128]{3,2,1,0:T(8,128)S(1)} %slice.159), channel_id=1, source_target_pairs={{0,64},{64,0},{1,65},{65,1},{2,66},{66,2},{3,67},{67,3},{4,68},{68... | collective-permute-start | bytes 1179656 | tf_op jit(solution)/shard_map/ppermute | solution.py:34
  159.8 3.6 %collective-permute-done.23 = f32[2,2,128,128]{3,2,1,0:T(8,128)S(1)} collective-permute-done((f32[2,2,128,128]{3,2,1,0:T(8,128)S(1)}, f32[2,2,128,128]{3,2,1,0:T(8,128)S(1)}, u32[]{:S(2)}, u32[]{:S(2)}) %collective-permute-start.23) | collective-permute-done | bytes 262176 | tf_op jit(solution)/shard_map/ppermute | solution.py:34
  163.5 3.9 %collective-permute-done.20 = f32[3,2,128,128]{3,2,1,0:T(8,128)S(1)} collective-permute-done((f32[3,2,128,128]{3,2,1,0:T(8,128)S(1)}, f32[3,2,128,128]{3,2,1,0:T(8,128)S(1)}, u32[]{:S(2)}, u32[]{:S(2)}) %collective-permute-start.20) | collective-permute-done | bytes 393248 | tf_op jit(solution)/shard_map/ppermute | solution.py:34
  170.8 13.0 %all-to-all-start = ((f32[128,1,1]{2,1,0:T(1,128)}), f32[128,1,1]{2,1,0:T(1,128)S(1)}, u32[]{:S(2)}, u32[]{:S(2)}) async-start(f32[128,1,1]{2,1,0:T(1,128)} %broadcast_in_dim.8), calls=%async_computation | async-start | bytes 131072 | tf_op jit(solution)/shard_map/all_to_all | solution.py:343
  184.4 8.9 %all-to-all-done = f32[128,1,1]{2,1,0:T(1,128)S(1)} async-done(((f32[128,1,1]{2,1,0:T(1,128)}), f32[128,1,1]{2,1,0:T(1,128)S(1)}, u32[]{:S(2)}, u32[]{:S(2)}) %all-to-all-start) | async-done | bytes 544 | tf_op jit(solution)/shard_map/all_to_all | solution.py:343
  (113 shorter events, 41.8 us)
Async XLA Ops:
  1.5 4.3 %collective-permute-start = (s32[8,128]{1,0:T(8,128)S(1)}, s32[8,128]{1,0:T(8,128)S(1)}, u32[]{:S(2)}, u32[]{:S(2)}) collective-permute-start(s32[8,128]{1,0:T(8,128)S(1)} %pad_add_fusion.3.table_ref), channel_id=1, source_target_pairs={{0,16},{16,0},{1,17},{17,1},{2,18},{18,2},{3,19},{19,3},{4,20},{20... | collective-permute-start | bytes 12296 | tf_op jit(solution)/shard_map/ppermute | solution.py:34
  5.9 13.1 %collective-permute-start.1 = (f32[3,2,128,128]{3,2,1,0:T(8,128)S(1)}, f32[3,2,128,128]{3,2,1,0:T(8,128)S(1)}, u32[]{:S(2)}, u32[]{:S(2)}) collective-permute-start(f32[3,2,128,128]{3,2,1,0:T(8,128)S(1)} %get-tuple-element.33), channel_id=1, source_target_pairs={{0,32},{1,33},{2,34},{3,35},{4,36},{5,37},{6,38},{7,39},{8,40},{9,... | collective-permute-start | bytes 1179656 | tf_op jit(solution)/shard_map/ppermute | solution.py:284
  8.5 10.6 %collective-permute-start.2 = (f32[3,2,128,128]{3,2,1,0:T(8,128)S(1)}, f32[3,2,128,128]{3,2,1,0:T(8,128)S(1)}, u32[]{:S(2)}, u32[]{:S(2)}) collective-permute-start(f32[3,2,128,128]{3,2,1,0:T(8,128)S(1)} %get-tuple-element.34), channel_id=1, source_target_pairs={{0,4},{1,5},{2,6},{3,7},{4,0},{5,1},{6,2},{7,3},{8,12},{9,13},{10,... | collective-permute-start | bytes 1179656 | tf_op jit(solution)/shard_map/ppermute | solution.py:284
  11.2 8.9 %collective-permute-start.3 = (f32[3,2,128,128]{3,2,1,0:T(8,128)S(1)}, f32[3,2,128,128]{3,2,1,0:T(8,128)S(1)}, u32[]{:S(2)}, u32[]{:S(2)}) collective-permute-start(f32[3,2,128,128]{3,2,1,0:T(8,128)S(1)} %get-tuple-element.35), channel_id=1, source_target_pairs={{0,1},{1,0},{2,3},{3,2},{4,5},{5,4},{6,7},{7,6},{8,9},{9,8},{10,11... | collective-permute-start | bytes 1179656 | tf_op jit(solution)/shard_map/ppermute | solution.py:284
  20.2 12.5 %collective-permute-start.5 = (f32[6,2,128,128]{3,2,1,0:T(8,128)S(1)}, f32[6,2,128,128]{3,2,1,0:T(8,128)S(1)}, u32[]{:S(2)}, u32[]{:S(2)}) collective-permute-start(f32[6,2,128,128]{3,2,1,0:T(8,128)S(1)} %pad_maximum_fusion.3), channel_id=1, source_target_pairs={{0,4},{1,5},{2,6},{3,7},{4,0},{5,1},{6,2},{7,3},{8,12},{9,13},{10,... | collective-permute-start | bytes 2359304 | tf_op jit(solution)/shard_map/ppermute | solution.py:284
  20.3 13.8 %collective-permute-start.6 = (f32[6,2,128,128]{3,2,1,0:T(8,128)S(1)}, f32[6,2,128,128]{3,2,1,0:T(8,128)S(1)}, u32[]{:S(2)}, u32[]{:S(2)}) collective-permute-start(f32[6,2,128,128]{3,2,1,0:T(8,128)S(1)} %pad_maximum_fusion.4), channel_id=1, source_target_pairs={{0,1},{1,0},{2,3},{3,2},{4,5},{5,4},{6,7},{7,6},{8,9},{9,8},{10,11... | collective-permute-start | bytes 2359304 | tf_op jit(solution)/shard_map/ppermute | solution.py:284
  23.0 12.5 %collective-permute-start.7 = (f32[6,2,128,128]{3,2,1,0:T(8,128)S(1)}, f32[6,2,128,128]{3,2,1,0:T(8,128)S(1)}, u32[]{:S(2)}, u32[]{:S(2)}) collective-permute-start(f32[6,2,128,128]{3,2,1,0:T(8,128)S(1)} %pad_maximum_fusion.5), channel_id=1, source_target_pairs={{0,32},{1,33},{2,34},{3,35},{4,36},{5,37},{6,38},{7,39},{8,40},{9,... | collective-permute-start | bytes 2359304 | tf_op jit(solution)/shard_map/ppermute | solution.py:284
  23.3 4.3 %collective-permute-start.8 = (s32[32,128]{1,0:T(8,128)S(1)}, s32[32,128]{1,0:T(8,128)S(1)}, u32[]{:S(2)}, u32[]{:S(2)}) collective-permute-start(s32[32,128]{1,0:T(8,128)S(1)} %pad_add_fusion.1), channel_id=1, source_target_pairs={{0,8},{8,0},{1,9},{9,1},{2,10},{10,2},{3,11},{11,3},{4,12},{12,4},... | collective-permute-start | bytes 49160 | tf_op jit(solution)/shard_map/ppermute | solution.py:34
  36.8 23.8 %collective-permute-start.10 = (f32[12,2,128,128]{3,2,1,0:T(8,128)}, f32[12,2,128,128]{3,2,1,0:T(8,128)}, u32[]{:S(2)}, u32[]{:S(2)}) collective-permute-start(f32[12,2,128,128]{3,2,1,0:T(8,128)} %pad_maximum_fusion.2), channel_id=1, source_target_pairs={{0,4},{1,5},{2,6},{3,7},{4,0},{5,1},{6,2},{7,3},{8,12},{9,13},{10,... | collective-permute-start | bytes 4718600 | tf_op jit(solution)/shard_map/ppermute | solution.py:284
  39.1 25.4 %collective-permute-start.11 = (f32[12,2,128,128]{3,2,1,0:T(8,128)}, f32[12,2,128,128]{3,2,1,0:T(8,128)}, u32[]{:S(2)}, u32[]{:S(2)}) collective-permute-start(f32[12,2,128,128]{3,2,1,0:T(8,128)} %pad_maximum_fusion), channel_id=1, source_target_pairs={{0,1},{1,0},{2,3},{3,2},{4,5},{5,4},{6,7},{7,6},{8,9},{9,8},{10,11... | collective-permute-start | bytes 4718600 | tf_op jit(solution)/shard_map/ppermute | solution.py:284
  40.4 24.1 %collective-permute-start.12 = (f32[12,2,128,128]{3,2,1,0:T(8,128)}, f32[12,2,128,128]{3,2,1,0:T(8,128)}, u32[]{:S(2)}, u32[]{:S(2)}) collective-permute-start(f32[12,2,128,128]{3,2,1,0:T(8,128)} %pad_maximum_fusion.1), channel_id=1, source_target_pairs={{0,32},{1,33},{2,34},{3,35},{4,36},{5,37},{6,38},{7,39},{8,40},{9,... | collective-permute-start | bytes 4718600 | tf_op jit(solution)/shard_map/ppermute | solution.py:284
  41.3 20.7 %collective-permute-start.9 = (s32[64,128]{1,0:T(8,128)S(1)}, s32[64,128]{1,0:T(8,128)S(1)}, u32[]{:S(2)}, u32[]{:S(2)}) collective-permute-start(s32[64,128]{1,0:T(8,128)S(1)} %pad_add_fusion.low_ref), channel_id=1, source_target_pairs={{0,2},{2,0},{1,3},{3,1},{4,6},{6,4},{5,7},{7,5},{8,10},{10,8},{9,1... | collective-permute-start | bytes 98312 | tf_op jit(solution)/shard_map/ppermute | solution.py:34
  80.7 13.2 %collective-permute-start.14 = (f32[32,2,128,128]{3,2,1,0:T(8,128)S(1)}, f32[32,2,128,128]{3,2,1,0:T(8,128)S(1)}, u32[]{:S(2)}, u32[]{:S(2)}) collective-permute-start(f32[32,2,128,128]{3,2,1,0:T(8,128)S(1)} %get-tuple-element.51), channel_id=1, source_target_pairs={{0,16},{16,0},{1,17},{17,1},{2,18},{18,2},{3,19},{19,3},{4,20},{20... | collective-permute-start | bytes 12582920 | tf_op jit(solution)/shard_map/ppermute | solution.py:34
  82.0 17.2 %collective-permute-start.13 = (f32[32,2,128,128]{3,2,1,0:T(8,128)S(1)}, f32[32,2,128,128]{3,2,1,0:T(8,128)}, u32[]{:S(2)}, u32[]{:S(2)}) collective-permute-start(f32[32,2,128,128]{3,2,1,0:T(8,128)S(1)} %get-tuple-element.49), channel_id=1, source_target_pairs={{0,16},{16,0},{1,17},{17,1},{2,18},{18,2},{3,19},{19,3},{4,20},{20... | collective-permute-start | bytes 12582920 | tf_op jit(solution)/shard_map/ppermute | solution.py:34
  94.6 37.2 %collective-permute-start.15 = (f32[12,2,128,128]{3,2,1,0:T(8,128)S(1)}, f32[12,2,128,128]{3,2,1,0:T(8,128)S(1)}, u32[]{:S(2)}, u32[]{:S(2)}) collective-permute-start(f32[12,2,128,128]{3,2,1,0:T(8,128)S(1)} %get-tuple-element.56), channel_id=1, source_target_pairs={{0,64},{64,0},{1,65},{65,1},{2,66},{66,2},{3,67},{67,3},{4,68},{68... | collective-permute-start | bytes 4718600 | tf_op jit(solution)/shard_map/ppermute | solution.py:34
  96.9 35.8 %collective-permute-start.18 = (f32[12,2,128,128]{3,2,1,0:T(8,128)S(1)}, f32[12,2,128,128]{3,2,1,0:T(8,128)S(1)}, u32[]{:S(2)}, u32[]{:S(2)}) collective-permute-start(f32[12,2,128,128]{3,2,1,0:T(8,128)S(1)} %get-tuple-element.57), channel_id=1, source_target_pairs={{0,8},{8,0},{1,9},{9,1},{2,10},{10,2},{3,11},{11,3},{4,12},{12,4},... | collective-permute-start | bytes 4718600 | tf_op jit(solution)/shard_map/ppermute | solution.py:34
  99.0 25.3 %collective-permute-start.21 = (f32[8,2,128,128]{3,2,1,0:T(8,128)S(1)}, f32[8,2,128,128]{3,2,1,0:T(8,128)S(1)}, u32[]{:S(2)}, u32[]{:S(2)}) collective-permute-start(f32[8,2,128,128]{3,2,1,0:T(8,128)S(1)} %slice_add_fusion.4), channel_id=1, source_target_pairs={{0,2},{2,0},{1,3},{3,1},{4,6},{6,4},{5,7},{7,5},{8,10},{10,8},{9,1... | collective-permute-start | bytes 3145736 | tf_op jit(solution)/shard_map/ppermute | solution.py:34
  125.8 17.2 %collective-permute-start.22 = (f32[4,2,128,128]{3,2,1,0:T(8,128)S(1)}, f32[4,2,128,128]{3,2,1,0:T(8,128)S(1)}, u32[]{:S(2)}, u32[]{:S(2)}) collective-permute-start(f32[4,2,128,128]{3,2,1,0:T(8,128)S(1)} %slice.163), channel_id=1, source_target_pairs={{0,64},{64,0},{1,65},{65,1},{2,66},{66,2},{3,67},{67,3},{4,68},{68... | collective-permute-start | bytes 1572872 | tf_op jit(solution)/shard_map/ppermute | solution.py:34
  135.6 18.7 %collective-permute-start.19 = (f32[6,2,128,128]{3,2,1,0:T(8,128)S(1)}, f32[6,2,128,128]{3,2,1,0:T(8,128)S(1)}, u32[]{:S(2)}, u32[]{:S(2)}) collective-permute-start(f32[6,2,128,128]{3,2,1,0:T(8,128)S(1)} %slice.157), channel_id=1, source_target_pairs={{0,2},{2,0},{1,3},{3,1},{4,6},{6,4},{5,7},{7,5},{8,10},{10,8},{9,1... | collective-permute-start | bytes 2359304 | tf_op jit(solution)/shard_map/ppermute | solution.py:34
  139.0 20.6 %collective-permute-start.16 = (f32[6,2,128,128]{3,2,1,0:T(8,128)S(1)}, f32[6,2,128,128]{3,2,1,0:T(8,128)S(1)}, u32[]{:S(2)}, u32[]{:S(2)}) collective-permute-start(f32[6,2,128,128]{3,2,1,0:T(8,128)S(1)} %slice.151), channel_id=1, source_target_pairs={{0,8},{8,0},{1,9},{9,1},{2,10},{10,2},{3,11},{11,3},{4,12},{12,4},... | collective-permute-start | bytes 2359304 | tf_op jit(solution)/shard_map/ppermute | solution.py:34
  143.1 20.4 %collective-permute-start.23 = (f32[2,2,128,128]{3,2,1,0:T(8,128)S(1)}, f32[2,2,128,128]{3,2,1,0:T(8,128)S(1)}, u32[]{:S(2)}, u32[]{:S(2)}) collective-permute-start(f32[2,2,128,128]{3,2,1,0:T(8,128)S(1)} %slice.165), channel_id=1, source_target_pairs={{0,8},{8,0},{1,9},{9,1},{2,10},{10,2},{3,11},{11,3},{4,12},{12,4},... | collective-permute-start | bytes 786440 | tf_op jit(solution)/shard_map/ppermute | solution.py:34
  154.4 13.0 %collective-permute-start.20 = (f32[3,2,128,128]{3,2,1,0:T(8,128)S(1)}, f32[3,2,128,128]{3,2,1,0:T(8,128)S(1)}, u32[]{:S(2)}, u32[]{:S(2)}) collective-permute-start(f32[3,2,128,128]{3,2,1,0:T(8,128)S(1)} %slice.159), channel_id=1, source_target_pairs={{0,64},{64,0},{1,65},{65,1},{2,66},{66,2},{3,67},{67,3},{4,68},{68... | collective-permute-start | bytes 1179656 | tf_op jit(solution)/shard_map/ppermute | solution.py:34
  159.7 8.9 %collective-permute-start.17 = (f32[3,2,128,128]{3,2,1,0:T(8,128)S(1)}, f32[3,2,128,128]{3,2,1,0:T(8,128)S(1)}, u32[]{:S(2)}, u32[]{:S(2)}) collective-permute-start(f32[3,2,128,128]{3,2,1,0:T(8,128)S(1)} %slice.153), channel_id=1, source_target_pairs={{0,2},{2,0},{1,3},{3,1},{4,6},{6,4},{5,7},{7,5},{8,10},{10,8},{9,1... | collective-permute-start | bytes 1179656 | tf_op jit(solution)/shard_map/ppermute | solution.py:34
  170.8 22.5 %all-to-all-start = ((f32[128,1,1]{2,1,0:T(1,128)}), f32[128,1,1]{2,1,0:T(1,128)S(1)}, u32[]{:S(2)}, u32[]{:S(2)}) async-start(f32[128,1,1]{2,1,0:T(1,128)} %broadcast_in_dim.8), calls=%async_computation | async-start | bytes 131072 | tf_op jit(solution)/shard_map/all_to_all | solution.py:343
  (22 other events, 139.5 us)

commit v3 on v2

--- a/solution.py
+++ b/solution.py
@@ -169,11 +169,10 @@
 
 
 def own_kernel(
-    table_ref, coef_ref, rate_ref, source_ref, q_ref, h_ref, out_ref, left_ref, right_ref, hl_ref, hr_ref, list_ref
+    table_ref, coef_ref, rate_ref, source_ref, left_ref, right_ref, h_ref, out_ref, hl_ref, hr_ref, list_ref
 ):
-    load_modes(q_ref, left_ref, right_ref)
     load_modes(h_ref, hl_ref, hr_ref)
-    modes = q_ref.shape[0]
+    modes = left_ref.shape[0]
 
     def one(m, carry):
         u = source_ref[m]
@@ -193,35 +192,60 @@
     add_terms(count, list_ref, table_ref, coef_ref, source_ref, left_ref, right_ref, out_ref)
 
 
-def far_kernel(pieces, plan_ref, coef_ref, rows_ref, q_ref, *refs):
-    blocks, refs = refs[:pieces], refs[pieces:]
-    outs, (source_ref, left_ref, right_ref, *lists, sems) = refs[:2], refs[2:]
+HELD = ((0, 1), (1, 1), (2, 2), (4, 4))
+
+
+def clear(out_ref):
+    def one(m, carry):
+        out_ref[m] = jnp.zeros(out_ref.shape[1:], F32)
+        return carry
+
+    lax.fori_loop(0, out_ref.shape[0], one, 0)
+
+
+def block_copies(blocks, stages, source_ref, sems):
     copies = []
-    for part, (lo, hi, _) in enumerate(PARTS):
+    for (lo, hi, _), part in zip(PARTS, blocks):
         size = hi - lo
-        copies.append((blocks[0].at[pl.ds(lo, size)], source_ref.at[pl.ds(8 * lo, size)]))
-        for stage in range(3):
-            block = blocks[1 + 3 * part + stage]
-            for b in range(1 << stage):
-                src = block.at[pl.ds(b * (block.shape[0] >> stage), size)]
-                copies.append((src, source_ref.at[pl.ds(8 * lo + (size << stage) + b * size, size)]))
-    copies = [pltpu.make_async_copy(a, b, sems.at[i]) for i, (a, b) in enumerate(copies)]
+        for block, (first, members) in zip(part, (HELD[i] for i in stages)):
+            for b in range(members):
+                src = block.at[pl.ds(b * (block.shape[0] // members), size)]
+                copies.append((src, source_ref.at[pl.ds(8 * lo + (first + b) * size, size)]))
+    return [pltpu.make_async_copy(a, b, sems.at[i]) for i, (a, b) in enumerate(copies)]
+
+
+def early_kernel(q_ref, *refs):
+    blocks, (source_ref, left_ref, right_ref, sems) = refs[:-4], refs[-4:]
+    own = [blocks[0].at[pl.ds(lo, hi - lo)] for lo, hi, _ in PARTS]
+    parts = [[own[i], *blocks[1 + 2 * i : 3 + 2 * i]] for i in range(len(PARTS))]
+    copies = block_copies(parts, (0, 1, 2), source_ref, sems)
     for copy in copies:
         copy.start()
     load_modes(q_ref, left_ref, right_ref)
-    targets = outs[0].shape[0]
-
-    def clear(m, carry):
-        for out in outs:
-            out[m] = jnp.zeros(out.shape[1:], F32)
-        return carry
-
-    lax.fori_loop(0, targets, clear, 0)
-    counts = [list_far(targets, rows_ref, i * targets, plan_ref, lists[i]) for i in range(2)]
     for copy in copies:
         copy.wait()
-    for out, terms, count in zip(outs, lists, counts):
-        add_terms(count, terms, plan_ref, coef_ref, source_ref, left_ref, right_ref, out)
+
+
+def first_kernel(
+    plan_ref, coef_ref, rows_ref, left_ref, right_ref, _, a_ref, b_ref, c_ref, source_ref, out_ref, list_ref, sems
+):
+    copies = block_copies([[a_ref], [b_ref], [c_ref]], (3,), source_ref, sems)
+    for copy in copies:
+        copy.start()
+    count = list_far(out_ref.shape[0], rows_ref, 0, plan_ref, list_ref)
+    clear(out_ref)
+    for copy in copies:
+        copy.wait()
+    add_terms(count, list_ref, plan_ref, coef_ref, source_ref, left_ref, right_ref, out_ref)
+
+
+def next_kernel(outs, plan_ref, coef_ref, rows_ref, source_ref, left_ref, right_ref, *refs):
+    list_ref = refs[outs]
+    for i, out_ref in enumerate(refs[:outs]):
+        targets = out_ref.shape[0]
+        count = list_far(targets, rows_ref, i * targets, plan_ref, list_ref)
+        clear(out_ref)
+        add_terms(count, list_ref, plan_ref, coef_ref, source_ref, left_ref, right_ref, out_ref)
 
 
 def spec(space):
@@ -240,14 +264,13 @@
     return pl.CostEstimate(flops=terms * 4 * (2 * n) ** 3, bytes_accessed=1 << 23, transcendentals=0)
 
 
-def served_rows(rc):
+def served_rows(rc, high):
     rows = []
-    for high in (1, 0):
-        for lo, hi, order in PARTS:
-            weight = ["xyz".index(a) for a in order]
-            for second, third in np.ndindex(2, 2):
-                b = 2 * ((high << weight[0]) + (second << weight[1]) + (third << weight[2])) + rc
-                rows += [b * 8 + m for m in range(lo, hi)]
+    for lo, hi, order in PARTS:
+        weight = ["xyz".index(a) for a in order]
+        for second, third in np.ndindex(2, 2):
+            b = 2 * ((high << weight[0]) + (second << weight[1]) + (third << weight[2])) + rc
+            rows += [b * 8 + m for m in range(lo, hi)]
     return np.array(rows, np.int32)
 
 
@@ -293,43 +316,75 @@
         out_shape=jax.ShapeDtypeStruct((2 * tables.shape[0], devices), jnp.int32),
         in_specs=[smem] + [vmem] * 3,
         out_specs=vmem,
+        compiler_params=params(4),
     )(at, tables, other, lists)
 
     coef = bath_coef.reshape(-1)
-    here, _ = lax.optimization_barrier((state, sends))
     listing = pltpu.SMEM((1024 + UNROLL,), jnp.int32)
+    target = jax.ShapeDtypeStruct((4 * local, 2, n, n), F32)
+    half_modes = jax.ShapeDtypeStruct((modes, 2 * n, 2 * n), BF16)
+
+    everything = jax.ShapeDtypeStruct((8 * local, 2, n, n), F32)
+    early, late = [state], []
+    for part in held:
+        early += part[1:3]
+        late.append(part[3])
+    early, _ = lax.optimization_barrier((early, sends))
+    early, late = ([pltpu.with_memory_space_constraint(b, pltpu.HBM) for b in group] for group in (early, late))
+    source, left, right = pl.pallas_call(
+        early_kernel,
+        out_shape=(everything, half_modes, half_modes),
+        in_specs=[vmem] + [spec(pltpu.HBM)] * len(early),
+        out_specs=(vmem,) * 3,
+        scratch_shapes=[pltpu.SemaphoreType.DMA((12,))],
+        compiler_params=params(20),
+        cost_estimate=cost(160, n),
+    )(couplings, *early)
+
+    source, other = pl.pallas_call(
+        first_kernel,
+        out_shape=(everything, target),
+        in_specs=[smem] * 3 + [vmem] * 3 + [spec(pltpu.HBM)] * 3,
+        out_specs=(vmem,) * 2,
+        scratch_shapes=[listing, pltpu.SemaphoreType.DMA((12,))],
+        input_output_aliases={5: 0},
+        compiler_params=params(24),
+        cost_estimate=cost(32, n),
+    )(plan, coef, served_rows(1, 1), left, right, source, *late)
+    parts = [slice(4 * lo, 4 * hi) for lo, hi, _ in PARTS]
+    swapped = flip(other, "c")
+
+    def later(plan, rows, outs):
+        return pl.pallas_call(
+            functools.partial(next_kernel, outs),
+            out_shape=(target,) * outs,
+            in_specs=[smem] * 3 + [vmem] * 3,
+            out_specs=(vmem,) * outs,
+            scratch_shapes=[listing],
+            compiler_params=params(24),
+            cost_estimate=cost(24 * outs, n),
+        )(plan, coef, rows, source, left, right)
+
+    same, other = later(plan, np.concatenate([served_rows(0, 1), served_rows(1, 0)]), 2)
+    gives = [same[rows] + swapped[rows] for rows in parts]
+
+    here, plan, gives, other = lax.optimization_barrier((state, plan, gives, other))
+    swapped = flip(other, "c")
     own = pl.pallas_call(
         own_kernel,
         out_shape=jax.ShapeDtypeStruct(state.shape, F32),
-        in_specs=[smem] * 3 + [vmem] * 3,
+        in_specs=[smem] * 3 + [vmem] * 4,
         out_specs=vmem,
-        scratch_shapes=mode_scratch(modes, n) + mode_scratch(2, n) + [listing],
+        scratch_shapes=mode_scratch(2, n) + [listing],
         compiler_params=params(16),
         cost_estimate=cost(160, n),
-    )(table, coef, bath_rate, here, couplings, hamiltonian)
-
-    blocks = [state] + [block for part in held for block in part[1:]]
-    own, plan = lax.optimization_barrier((own, plan))
-    target = jax.ShapeDtypeStruct((4 * local, 2, n, n), F32)
-    partial = []
-    for rc in (1, 0):
-        partial += pl.pallas_call(
-            functools.partial(far_kernel, len(blocks)),
-            out_shape=(target, target),
-            in_specs=[smem] * 3 + [vmem] + [spec(pl.ANY)] * len(blocks),
-            out_specs=(vmem, vmem),
-            scratch_shapes=[pltpu.VMEM((8 * local, 2, n, n), F32)]
-            + mode_scratch(modes, n)
-            + [listing, listing, pltpu.SemaphoreType.DMA((24,))],
-            compiler_params=params(28),
-            cost_estimate=cost(48, n),
-        )(plan, coef, served_rows(rc), couplings, *blocks)
-    swapped = [flip(partial[0], "c"), flip(partial[1], "c")]
+    )(table, coef, bath_rate, here, left, right, hamiltonian)
+    (kept,) = later(plan, served_rows(0, 0), 1)
+    keeps = [kept[rows] + swapped[rows] for rows in parts]
+    keeps, own = lax.optimization_barrier((keeps, own))
+
     sums = []
-    for lo, hi, axes in PARTS:
-        rows = slice(4 * lo, 4 * hi)
-        give = partial[2][rows] + swapped[0][rows]
-        keep = partial[3][rows] + swapped[1][rows]
+    for give, keep, (_, _, axes) in zip(gives, keeps, PARTS):
         for stage in range(3):
             keep = keep + flip(give, axes[stage] + "h")
             half = keep.shape[0] // 2

time: 196 us -> 174 us (0.89)
  local copies, waits for them, and re-layouts: 10.6 us -> 3.3 us
  starting transfers between devices: 55.8 us -> 49.1 us
  other arithmetic: 16.4 us -> 12.3 us
  waiting for transfers between devices: 69 us -> 65.6 us
    ppermute x15, waiting for transfers between devices: 54 us -> 35.7 us  [flip(): return lax.ppermute(value, axis, [(0, 1), (1, 0)])]
    ppermute x9, waiting for transfers between devices: 6.09 us -> 21 us  [body(): part.append(lax.ppermute(block, ALL, pairs[order[stage]]))]
    unnamed x42 -> x36, local copies, waits for them, and re-layouts: 7.35 us -> 0.09 us
    ppermute x15, starting transfers between devices: 26.8 us -> 22.2 us  [flip(): return lax.ppermute(value, axis, [(0, 1), (1, 0)])]
    add x8 -> x9, other arithmetic: 4.64 us -> 0.93 us  [body(): keep = keep + flip(give, axes[stage] + 'h')]
    all_to_all x1, starting transfers between devices: 13 us -> 10.7 us  [body(): lax.all_to_all(jnp.broadcast_to(total, (devices,)), ALL, split_axis=0, co...]
    pallas_call x2 -> x4, Pallas kernels: 21.8 us -> 22.8 us  [the longest x2 13.6 us: later(): pl.pallas_call(functools.partial(next_kernel, outs), out_shape=(target,)...]
  transfers between devices with their start and end apart: 25 -> 25, of which waited for: 14 -> 16; matrix products, arithmetic and copies ran while one was open for 7% -> 5% of each run, Pallas kernels for 16% -> 20%
where the time goes in v3:
time: 174 us
  waiting for transfers between devices  65.6 us (38%)
  starting transfers between devices  49.1 us (28%)
  Pallas kernels  41 us (24%)
  other arithmetic  12.3 us (7%)
  local copies, waits for them, and re-layouts  3.3 us (2%)
  between operations  2.41 us (1%)
    ppermute x15, waiting for transfers between devices, flip(): return lax.ppermute(value, axis, [(0, 1), (1, 0)])  35.7 us
    ppermute x15, starting transfers between devices, flip(): return lax.ppermute(value, axis, [(0, 1), (1, 0)])  22.2 us
    ppermute x9, waiting for transfers between devices, body(): part.append(lax.ppermute(block, ALL, pairs[order[stage]]))  21 us
    pallas_call x1, Pallas kernels, body(): pl.pallas_call(own_kernel, out_shape=jax.ShapeDtypeStruct(state.shape, F3...  17.1 us
    ppermute x9, starting transfers between devices, body(): part.append(lax.ppermute(block, ALL, pairs[order[stage]]))  16.2 us
    pallas_call x2, Pallas kernels, later(): pl.pallas_call(functools.partial(next_kernel, outs), out_shape=(target,)...  13.6 us
    all_to_all x1, starting transfers between devices, body(): lax.all_to_all(jnp.broadcast_to(total, (devices,)), ALL, split_axis=0, co...  10.7 us
    all_to_all x1, waiting for transfers between devices, body(): lax.all_to_all(jnp.broadcast_to(total, (devices,)), ALL, split_axis=0, co...  8.86 us
  transfers between devices with their start and end apart: 25, of which 16 were waited for; matrix products, arithmetic and copies ran while one was open for 5% of the time, Pallas kernels for 20%

profile of v3, /device:TPU:1, one launch (start us, length us, event | category | flops | bytes accessed | tf_op | source)
XLA Modules:
  0.0 173.6 jit_solution(17826176220859827327)
XLA Ops:
  5.9 2.8 %collective-permute-start.2 = (f32[3,2,128,128]{3,2,1,0:T(8,128)S(1)}, f32[3,2,128,128]{3,2,1,0:T(8,128)S(1)}, u32[]{:S(2)}, u32[]{:S(2)}) collective-permute-start(f32[3,2,128,128]{3,2,1,0:T(8,128)S(1)} %get-tuple-element.51), channel_id=1, source_target_pairs={{0,4},{1,5},{2,6},{3,7},{4,0},{5,1},{6,2},{7,3},{8,12},{9,13},{10,... | collective-permute-start | bytes 1179656 | tf_op jit(solution)/shard_map/ppermute | solution.py:307
  8.7 2.5 %collective-permute-start.1 = (f32[3,2,128,128]{3,2,1,0:T(8,128)S(1)}, f32[3,2,128,128]{3,2,1,0:T(8,128)S(1)}, u32[]{:S(2)}, u32[]{:S(2)}) collective-permute-start(f32[3,2,128,128]{3,2,1,0:T(8,128)S(1)} %get-tuple-element.50), channel_id=1, source_target_pairs={{0,32},{1,33},{2,34},{3,35},{4,36},{5,37},{6,38},{7,39},{8,40},{9,... | collective-permute-start | bytes 1179656 | tf_op jit(solution)/shard_map/ppermute | solution.py:307
  11.2 3.8 %collective-permute-start.3 = (f32[3,2,128,128]{3,2,1,0:T(8,128)S(1)}, f32[3,2,128,128]{3,2,1,0:T(8,128)S(1)}, u32[]{:S(2)}, u32[]{:S(2)}) collective-permute-start(f32[3,2,128,128]{3,2,1,0:T(8,128)S(1)} %get-tuple-element.52), channel_id=1, source_target_pairs={{0,1},{1,0},{2,3},{3,2},{4,5},{5,4},{6,7},{7,6},{8,9},{9,8},{10,11... | collective-permute-start | bytes 1179656 | tf_op jit(solution)/shard_map/ppermute | solution.py:307
  15.5 3.5 %collective-permute-done.4 = s32[16,128]{1,0:T(8,128)S(1)} collective-permute-done((s32[16,128]{1,0:T(8,128)S(1)}, s32[16,128]{1,0:T(8,128)S(1)}, u32[]{:S(2)}, u32[]{:S(2)}) %collective-permute-start.4) | collective-permute-done | bytes 8224 | tf_op jit(solution)/shard_map/ppermute | solution.py:34
  20.5 2.7 %collective-permute-start.6 = (f32[6,2,128,128]{3,2,1,0:T(8,128)S(1)}, f32[6,2,128,128]{3,2,1,0:T(8,128)S(1)}, u32[]{:S(2)}, u32[]{:S(2)}) collective-permute-start(f32[6,2,128,128]{3,2,1,0:T(8,128)S(1)} %pad_maximum_fusion.4), channel_id=1, source_target_pairs={{0,1},{1,0},{2,3},{3,2},{4,5},{5,4},{6,7},{7,6},{8,9},{9,8},{10,11... | collective-permute-start | bytes 2359304 | tf_op jit(solution)/shard_map/ppermute | solution.py:307
  24.9 2.9 %collective-permute-done.8 = s32[32,128]{1,0:T(8,128)S(1)} collective-permute-done((s32[32,128]{1,0:T(8,128)S(1)}, s32[32,128]{1,0:T(8,128)S(1)}, u32[]{:S(2)}, u32[]{:S(2)}) %collective-permute-start.8) | collective-permute-done | bytes 16416 | tf_op jit(solution)/shard_map/ppermute | solution.py:34
  27.8 4.6 %collective-permute-done.7.refs_6_ = f32[6,2,128,128]{3,2,1,0:T(8,128)S(1)} collective-permute-done((f32[6,2,128,128]{3,2,1,0:T(8,128)S(1)}, f32[6,2,128,128]{3,2,1,0:T(8,128)S(1)}, u32[]{:S(2)}, u32[]{:S(2)}) %collective-permute-start.7) | collective-permute-done | bytes 786464 | tf_op jit(solution)/shard_map/ppermute | solution.py:307
  43.5 14.3 %collective-permute-done.10.c_ref = f32[12,2,128,128]{3,2,1,0:T(8,128)} collective-permute-done((f32[12,2,128,128]{3,2,1,0:T(8,128)}, f32[12,2,128,128]{3,2,1,0:T(8,128)}, u32[]{:S(2)}, u32[]{:S(2)}) %collective-permute-start.10) | collective-permute-done | bytes 1572896 | tf_op jit(solution)/shard_map/ppermute | solution.py:307
  60.2 7.0 %shard_map.142 = (f32[64,2,128,128]{3,2,1,0:T(8,128)S(1)}, f32[32,2,128,128]{3,2,1,0:T(8,128)S(1)}) custom-call(s32[128,128]{1,0:T(8,128)S(1)} %shard_map.140.plan_ref, f32[32]{0:T(128)S(1)} %reshape.62.coef_ref, s32[32]{0:T(128)S(1)} %copy-done.3, bf16[16,256,256]{2,1,0:T(8,128)(2,1)S(1)} %get-tuple-element.69.left_ref, ...), custom_call_target="tpu_custom_call", output_to_operand_aliasing={{0}: (5, {})} | custom-call | flops 2147483648 | bytes 8388608 | tf_op jit(solution)/shard_map/pallas_call | solution.py:344
  67.1 3.3 %collective-permute-start.13 = (f32[32,2,128,128]{3,2,1,0:T(8,128)S(1)}, f32[32,2,128,128]{3,2,1,0:T(8,128)S(1)}, u32[]{:S(2)}, u32[]{:S(2)}) collective-permute-start(f32[32,2,128,128]{3,2,1,0:T(8,128)S(1)} %get-tuple-element.74), channel_id=1, source_target_pairs={{0,16},{16,0},{1,17},{17,1},{2,18},{18,2},{3,19},{19,3},{4,20},{20... | collective-permute-start | bytes 12582920 | tf_op jit(solution)/shard_map/ppermute | solution.py:34
  70.5 8.7 %shard_map.143 = (f32[32,2,128,128]{3,2,1,0:T(8,128)S(1)}, f32[32,2,128,128]{3,2,1,0:T(8,128)S(1)}) custom-call(s32[128,128]{1,0:T(8,128)S(1)} %shard_map.140.plan_ref, f32[32]{0:T(128)S(1)} %reshape.62.coef_ref, s32[64]{0:T(128)S(1)} %copy-done.2, f32[64,2,128,128]{3,2,1,0:T(8,128)S(1)} %get-tuple-element.72.source_ref, ...), custom_call_target="tpu_custom_call" | custom-call | flops 3221225472 | bytes 8388608 | tf_op jit(solution)/shard_map/pallas_call | solution.py:358
  80.5 2.5 %collective-permute-start.15 = (f32[12,2,128,128]{3,2,1,0:T(8,128)S(1)}, f32[12,2,128,128]{3,2,1,0:T(8,128)S(1)}, u32[]{:S(2)}, u32[]{:S(2)}) collective-permute-start(f32[12,2,128,128]{3,2,1,0:T(8,128)S(1)} %get-tuple-element.81), channel_id=1, source_target_pairs={{0,64},{64,0},{1,65},{65,1},{2,66},{66,2},{3,67},{67,3},{4,68},{68... | collective-permute-start | bytes 4718600 | tf_op jit(solution)/shard_map/ppermute | solution.py:34
  84.8 17.1 %shard_map.145 = f32[8,2,128,128]{3,2,1,0:T(8,128)S(1)} custom-call(s32[8,128]{1,0:T(8,128)S(1)} %pad_add_fusion.3.table_ref, f32[32]{0:T(128)S(1)} %reshape.62.coef_ref, f32[16]{0:T(128)S(1)} %copy-done.6, f32[8,2,128,128]{3,2,1,0:T(8,128)S(1)} %copy-done, bf16[16,256,256]{2,1,0:T(8,128)(2,1)S(1)} %get-tuple-element.69.left_ref, ...), custom_call_target="tpu_custom_call" | custom-call | flops 10737418240 | bytes 8388608 | tf_op jit(solution)/shard_map/pallas_call | solution.py:373
  101.9 4.9 %shard_map.144 = f32[32,2,128,128]{3,2,1,0:T(8,128)S(1)} custom-call(s32[128,128]{1,0:T(8,128)S(1)} %shard_map.140.plan_ref, f32[32]{0:T(128)S(1)} %reshape.62.coef_ref, s32[32]{0:T(128)S(1)} %copy-done.1, f32[64,2,128,128]{3,2,1,0:T(8,128)S(1)} %get-tuple-element.72.source_ref, bf16[16,256,256]{2,1,0:T(8,128)(2,1)S(1)} %get-tuple-element.69.left_ref, ...), custom_call_target="tpu_custom_call" | custom-call | flops 1610612736 | bytes 8388608 | tf_op jit(solution)/shard_map/pallas_call | solution.py:358
  107.7 2.6 %collective-permute-done.21 = f32[8,2,128,128]{3,2,1,0:T(8,128)S(1)} collective-permute-done((f32[8,2,128,128]{3,2,1,0:T(8,128)S(1)}, f32[8,2,128,128]{3,2,1,0:T(8,128)S(1)}, u32[]{:S(2)}, u32[]{:S(2)}) %collective-permute-start.21) | collective-permute-done | bytes 1048608 | tf_op jit(solution)/shard_map/ppermute | solution.py:34
  111.9 6.1 %collective-permute-done.15 = f32[12,2,128,128]{3,2,1,0:T(8,128)S(1)} collective-permute-done((f32[12,2,128,128]{3,2,1,0:T(8,128)S(1)}, f32[12,2,128,128]{3,2,1,0:T(8,128)S(1)}, u32[]{:S(2)}, u32[]{:S(2)}) %collective-permute-start.15) | collective-permute-done | bytes 1572896 | tf_op jit(solution)/shard_map/ppermute | solution.py:34
  118.3 2.6 %collective-permute-start.16 = (f32[6,2,128,128]{3,2,1,0:T(8,128)S(1)}, f32[6,2,128,128]{3,2,1,0:T(8,128)S(1)}, u32[]{:S(2)}, u32[]{:S(2)}) collective-permute-start(f32[6,2,128,128]{3,2,1,0:T(8,128)S(1)} %slice.158), channel_id=1, source_target_pairs={{0,8},{8,0},{1,9},{9,1},{2,10},{10,2},{3,11},{11,3},{4,12},{12,4},... | collective-permute-start | bytes 2359304 | tf_op jit(solution)/shard_map/ppermute | solution.py:34
  121.7 7.5 %collective-permute-done.22 = f32[4,2,128,128]{3,2,1,0:T(8,128)S(1)} collective-permute-done((f32[4,2,128,128]{3,2,1,0:T(8,128)S(1)}, f32[4,2,128,128]{3,2,1,0:T(8,128)S(1)}, u32[]{:S(2)}, u32[]{:S(2)}) %collective-permute-start.22) | collective-permute-done | bytes 524320 | tf_op jit(solution)/shard_map/ppermute | solution.py:34
  129.3 2.6 %collective-permute-start.23 = (f32[2,2,128,128]{3,2,1,0:T(8,128)S(1)}, f32[2,2,128,128]{3,2,1,0:T(8,128)S(1)}, u32[]{:S(2)}, u32[]{:S(2)}) collective-permute-start(f32[2,2,128,128]{3,2,1,0:T(8,128)S(1)} %slice.168), channel_id=1, source_target_pairs={{0,8},{8,0},{1,9},{9,1},{2,10},{10,2},{3,11},{11,3},{4,12},{12,4},... | collective-permute-start | bytes 786440 | tf_op jit(solution)/shard_map/ppermute | solution.py:34
  131.9 5.6 %collective-permute-done.16 = f32[6,2,128,128]{3,2,1,0:T(8,128)S(1)} collective-permute-done((f32[6,2,128,128]{3,2,1,0:T(8,128)S(1)}, f32[6,2,128,128]{3,2,1,0:T(8,128)S(1)}, u32[]{:S(2)}, u32[]{:S(2)}) %collective-permute-start.16) | collective-permute-done | bytes 786464 | tf_op jit(solution)/shard_map/ppermute | solution.py:34
  143.2 3.0 %collective-permute-done.17 = f32[3,2,128,128]{3,2,1,0:T(8,128)S(1)} collective-permute-done((f32[3,2,128,128]{3,2,1,0:T(8,128)S(1)}, f32[3,2,128,128]{3,2,1,0:T(8,128)S(1)}, u32[]{:S(2)}, u32[]{:S(2)}) %collective-permute-start.17) | collective-permute-done | bytes 393248 | tf_op jit(solution)/shard_map/ppermute | solution.py:34
  146.2 2.5 %collective-permute-done.20 = f32[3,2,128,128]{3,2,1,0:T(8,128)S(1)} collective-permute-done((f32[3,2,128,128]{3,2,1,0:T(8,128)S(1)}, f32[3,2,128,128]{3,2,1,0:T(8,128)S(1)}, u32[]{:S(2)}, u32[]{:S(2)}) %collective-permute-start.20) | collective-permute-done | bytes 393248 | tf_op jit(solution)/shard_map/ppermute | solution.py:34
  150.9 10.7 %all-to-all-start = ((f32[128,1,1]{2,1,0:T(1,128)}), f32[128,1,1]{2,1,0:T(1,128)S(1)}, u32[]{:S(2)}, u32[]{:S(2)}) async-start(f32[128,1,1]{2,1,0:T(1,128)} %broadcast_in_dim.8), calls=%async_computation | async-start | bytes 131072 | tf_op jit(solution)/shard_map/all_to_all | solution.py:398
  162.2 8.9 %all-to-all-done = f32[128,1,1]{2,1,0:T(1,128)S(1)} async-done(((f32[128,1,1]{2,1,0:T(1,128)}), f32[128,1,1]{2,1,0:T(1,128)S(1)}, u32[]{:S(2)}, u32[]{:S(2)}) %all-to-all-start) | async-done | bytes 544 | tf_op jit(solution)/shard_map/all_to_all | solution.py:398
  (112 shorter events, 38.4 us)
Async XLA Ops:
  1.5 4.3 %collective-permute-start = (s32[8,128]{1,0:T(8,128)S(1)}, s32[8,128]{1,0:T(8,128)S(1)}, u32[]{:S(2)}, u32[]{:S(2)}) collective-permute-start(s32[8,128]{1,0:T(8,128)S(1)} %pad_add_fusion.3.table_ref), channel_id=1, source_target_pairs={{0,16},{16,0},{1,17},{17,1},{2,18},{18,2},{3,19},{19,3},{4,20},{20... | collective-permute-start | bytes 12296 | tf_op jit(solution)/shard_map/ppermute | solution.py:34
  5.9 13.1 %collective-permute-start.2 = (f32[3,2,128,128]{3,2,1,0:T(8,128)S(1)}, f32[3,2,128,128]{3,2,1,0:T(8,128)S(1)}, u32[]{:S(2)}, u32[]{:S(2)}) collective-permute-start(f32[3,2,128,128]{3,2,1,0:T(8,128)S(1)} %get-tuple-element.51), channel_id=1, source_target_pairs={{0,4},{1,5},{2,6},{3,7},{4,0},{5,1},{6,2},{7,3},{8,12},{9,13},{10,... | collective-permute-start | bytes 1179656 | tf_op jit(solution)/shard_map/ppermute | solution.py:307
  8.7 10.3 %collective-permute-start.1 = (f32[3,2,128,128]{3,2,1,0:T(8,128)S(1)}, f32[3,2,128,128]{3,2,1,0:T(8,128)S(1)}, u32[]{:S(2)}, u32[]{:S(2)}) collective-permute-start(f32[3,2,128,128]{3,2,1,0:T(8,128)S(1)} %get-tuple-element.50), channel_id=1, source_target_pairs={{0,32},{1,33},{2,34},{3,35},{4,36},{5,37},{6,38},{7,39},{8,40},{9,... | collective-permute-start | bytes 1179656 | tf_op jit(solution)/shard_map/ppermute | solution.py:307
  11.2 8.9 %collective-permute-start.3 = (f32[3,2,128,128]{3,2,1,0:T(8,128)S(1)}, f32[3,2,128,128]{3,2,1,0:T(8,128)S(1)}, u32[]{:S(2)}, u32[]{:S(2)}) collective-permute-start(f32[3,2,128,128]{3,2,1,0:T(8,128)S(1)} %get-tuple-element.52), channel_id=1, source_target_pairs={{0,1},{1,0},{2,3},{3,2},{4,5},{5,4},{6,7},{7,6},{8,9},{9,8},{10,11... | collective-permute-start | bytes 1179656 | tf_op jit(solution)/shard_map/ppermute | solution.py:307
  20.2 12.1 %collective-permute-start.7 = (f32[6,2,128,128]{3,2,1,0:T(8,128)S(1)}, f32[6,2,128,128]{3,2,1,0:T(8,128)S(1)}, u32[]{:S(2)}, u32[]{:S(2)}) collective-permute-start(f32[6,2,128,128]{3,2,1,0:T(8,128)S(1)} %pad_maximum_fusion.5), channel_id=1, source_target_pairs={{0,32},{1,33},{2,34},{3,35},{4,36},{5,37},{6,38},{7,39},{8,40},{9,... | collective-permute-start | bytes 2359304 | tf_op jit(solution)/shard_map/ppermute | solution.py:307
  20.5 13.2 %collective-permute-start.6 = (f32[6,2,128,128]{3,2,1,0:T(8,128)S(1)}, f32[6,2,128,128]{3,2,1,0:T(8,128)S(1)}, u32[]{:S(2)}, u32[]{:S(2)}) collective-permute-start(f32[6,2,128,128]{3,2,1,0:T(8,128)S(1)} %pad_maximum_fusion.4), channel_id=1, source_target_pairs={{0,1},{1,0},{2,3},{3,2},{4,5},{5,4},{6,7},{7,6},{8,9},{9,8},{10,11... | collective-permute-start | bytes 2359304 | tf_op jit(solution)/shard_map/ppermute | solution.py:307
  23.2 12.4 %collective-permute-start.5 = (f32[6,2,128,128]{3,2,1,0:T(8,128)S(1)}, f32[6,2,128,128]{3,2,1,0:T(8,128)S(1)}, u32[]{:S(2)}, u32[]{:S(2)}) collective-permute-start(f32[6,2,128,128]{3,2,1,0:T(8,128)S(1)} %pad_maximum_fusion.3), channel_id=1, source_target_pairs={{0,4},{1,5},{2,6},{3,7},{4,0},{5,1},{6,2},{7,3},{8,12},{9,13},{10,... | collective-permute-start | bytes 2359304 | tf_op jit(solution)/shard_map/ppermute | solution.py:307
  23.4 4.3 %collective-permute-start.8 = (s32[32,128]{1,0:T(8,128)S(1)}, s32[32,128]{1,0:T(8,128)S(1)}, u32[]{:S(2)}, u32[]{:S(2)}) collective-permute-start(s32[32,128]{1,0:T(8,128)S(1)} %pad_add_fusion.1), channel_id=1, source_target_pairs={{0,8},{8,0},{1,9},{9,1},{2,10},{10,2},{3,11},{11,3},{4,12},{12,4},... | collective-permute-start | bytes 49160 | tf_op jit(solution)/shard_map/ppermute | solution.py:34
  37.0 20.8 %collective-permute-start.10 = (f32[12,2,128,128]{3,2,1,0:T(8,128)}, f32[12,2,128,128]{3,2,1,0:T(8,128)}, u32[]{:S(2)}, u32[]{:S(2)}) collective-permute-start(f32[12,2,128,128]{3,2,1,0:T(8,128)} %pad_maximum_fusion.2), channel_id=1, source_target_pairs={{0,4},{1,5},{2,6},{3,7},{4,0},{5,1},{6,2},{7,3},{8,12},{9,13},{10,... | collective-permute-start | bytes 4718600 | tf_op jit(solution)/shard_map/ppermute | solution.py:307
  37.2 22.4 %collective-permute-start.11 = (f32[12,2,128,128]{3,2,1,0:T(8,128)}, f32[12,2,128,128]{3,2,1,0:T(8,128)}, u32[]{:S(2)}, u32[]{:S(2)}) collective-permute-start(f32[12,2,128,128]{3,2,1,0:T(8,128)} %pad_maximum_fusion), channel_id=1, source_target_pairs={{0,1},{1,0},{2,3},{3,2},{4,5},{5,4},{6,7},{7,6},{8,9},{9,8},{10,11... | collective-permute-start | bytes 4718600 | tf_op jit(solution)/shard_map/ppermute | solution.py:307
  39.4 20.8 %collective-permute-start.12 = (f32[12,2,128,128]{3,2,1,0:T(8,128)}, f32[12,2,128,128]{3,2,1,0:T(8,128)}, u32[]{:S(2)}, u32[]{:S(2)}) collective-permute-start(f32[12,2,128,128]{3,2,1,0:T(8,128)} %pad_maximum_fusion.1), channel_id=1, source_target_pairs={{0,32},{1,33},{2,34},{3,35},{4,36},{5,37},{6,38},{7,39},{8,40},{9,... | collective-permute-start | bytes 4718600 | tf_op jit(solution)/shard_map/ppermute | solution.py:307
  41.1 17.4 %collective-permute-start.9 = (s32[64,128]{1,0:T(8,128)S(1)}, s32[64,128]{1,0:T(8,128)S(1)}, u32[]{:S(2)}, u32[]{:S(2)}) collective-permute-start(s32[64,128]{1,0:T(8,128)S(1)} %pad_add_fusion.low_ref), channel_id=1, source_target_pairs={{0,2},{2,0},{1,3},{3,1},{4,6},{6,4},{5,7},{7,5},{8,10},{10,8},{9,1... | collective-permute-start | bytes 98312 | tf_op jit(solution)/shard_map/ppermute | solution.py:34
  67.1 12.0 %collective-permute-start.13 = (f32[32,2,128,128]{3,2,1,0:T(8,128)S(1)}, f32[32,2,128,128]{3,2,1,0:T(8,128)S(1)}, u32[]{:S(2)}, u32[]{:S(2)}) collective-permute-start(f32[32,2,128,128]{3,2,1,0:T(8,128)S(1)} %get-tuple-element.74), channel_id=1, source_target_pairs={{0,16},{16,0},{1,17},{17,1},{2,18},{18,2},{3,19},{19,3},{4,20},{20... | collective-permute-start | bytes 12582920 | tf_op jit(solution)/shard_map/ppermute | solution.py:34
  79.9 26.9 %collective-permute-start.14 = (f32[32,2,128,128]{3,2,1,0:T(8,128)S(1)}, f32[32,2,128,128]{3,2,1,0:T(8,128)S(1)}, u32[]{:S(2)}, u32[]{:S(2)}) collective-permute-start(f32[32,2,128,128]{3,2,1,0:T(8,128)S(1)} %get-tuple-element.77), channel_id=1, source_target_pairs={{0,16},{16,0},{1,17},{17,1},{2,18},{18,2},{3,19},{19,3},{4,20},{20... | collective-permute-start | bytes 12582920 | tf_op jit(solution)/shard_map/ppermute | solution.py:34
  80.5 37.5 %collective-permute-start.15 = (f32[12,2,128,128]{3,2,1,0:T(8,128)S(1)}, f32[12,2,128,128]{3,2,1,0:T(8,128)S(1)}, u32[]{:S(2)}, u32[]{:S(2)}) collective-permute-start(f32[12,2,128,128]{3,2,1,0:T(8,128)S(1)} %get-tuple-element.81), channel_id=1, source_target_pairs={{0,64},{64,0},{1,65},{65,1},{2,66},{66,2},{3,67},{67,3},{4,68},{68... | collective-permute-start | bytes 4718600 | tf_op jit(solution)/shard_map/ppermute | solution.py:34
  83.1 37.8 %collective-permute-start.18 = (f32[12,2,128,128]{3,2,1,0:T(8,128)S(1)}, f32[12,2,128,128]{3,2,1,0:T(8,128)S(1)}, u32[]{:S(2)}, u32[]{:S(2)}) collective-permute-start(f32[12,2,128,128]{3,2,1,0:T(8,128)S(1)} %get-tuple-element.83), channel_id=1, source_target_pairs={{0,8},{8,0},{1,9},{9,1},{2,10},{10,2},{3,11},{11,3},{4,12},{12,4},... | collective-permute-start | bytes 4718600 | tf_op jit(solution)/shard_map/ppermute | solution.py:34
  84.8 25.6 %collective-permute-start.21 = (f32[8,2,128,128]{3,2,1,0:T(8,128)S(1)}, f32[8,2,128,128]{3,2,1,0:T(8,128)S(1)}, u32[]{:S(2)}, u32[]{:S(2)}) collective-permute-start(f32[8,2,128,128]{3,2,1,0:T(8,128)S(1)} %slice_add_fusion.5), channel_id=1, source_target_pairs={{0,2},{2,0},{1,3},{3,1},{4,6},{6,4},{5,7},{7,5},{8,10},{10,8},{9,1... | collective-permute-start | bytes 3145736 | tf_op jit(solution)/shard_map/ppermute | solution.py:34
  110.5 18.7 %collective-permute-start.22 = (f32[4,2,128,128]{3,2,1,0:T(8,128)S(1)}, f32[4,2,128,128]{3,2,1,0:T(8,128)S(1)}, u32[]{:S(2)}, u32[]{:S(2)}) collective-permute-start(f32[4,2,128,128]{3,2,1,0:T(8,128)S(1)} %slice.166), channel_id=1, source_target_pairs={{0,64},{64,0},{1,65},{65,1},{2,66},{66,2},{3,67},{67,3},{4,68},{68... | collective-permute-start | bytes 1572872 | tf_op jit(solution)/shard_map/ppermute | solution.py:34
  118.3 19.3 %collective-permute-start.16 = (f32[6,2,128,128]{3,2,1,0:T(8,128)S(1)}, f32[6,2,128,128]{3,2,1,0:T(8,128)S(1)}, u32[]{:S(2)}, u32[]{:S(2)}) collective-permute-start(f32[6,2,128,128]{3,2,1,0:T(8,128)S(1)} %slice.158), channel_id=1, source_target_pairs={{0,8},{8,0},{1,9},{9,1},{2,10},{10,2},{3,11},{11,3},{4,12},{12,4},... | collective-permute-start | bytes 2359304 | tf_op jit(solution)/shard_map/ppermute | solution.py:34
  121.1 19.0 %collective-permute-start.19 = (f32[6,2,128,128]{3,2,1,0:T(8,128)S(1)}, f32[6,2,128,128]{3,2,1,0:T(8,128)S(1)}, u32[]{:S(2)}, u32[]{:S(2)}) collective-permute-start(f32[6,2,128,128]{3,2,1,0:T(8,128)S(1)} %slice.162), channel_id=1, source_target_pairs={{0,2},{2,0},{1,3},{3,1},{4,6},{6,4},{5,7},{7,5},{8,10},{10,8},{9,1... | collective-permute-start | bytes 2359304 | tf_op jit(solution)/shard_map/ppermute | solution.py:34
  129.3 13.8 %collective-permute-start.23 = (f32[2,2,128,128]{3,2,1,0:T(8,128)S(1)}, f32[2,2,128,128]{3,2,1,0:T(8,128)S(1)}, u32[]{:S(2)}, u32[]{:S(2)}) collective-permute-start(f32[2,2,128,128]{3,2,1,0:T(8,128)S(1)} %slice.168), channel_id=1, source_target_pairs={{0,8},{8,0},{1,9},{9,1},{2,10},{10,2},{3,11},{11,3},{4,12},{12,4},... | collective-permute-start | bytes 786440 | tf_op jit(solution)/shard_map/ppermute | solution.py:34
  137.7 8.5 %collective-permute-start.17 = (f32[3,2,128,128]{3,2,1,0:T(8,128)S(1)}, f32[3,2,128,128]{3,2,1,0:T(8,128)S(1)}, u32[]{:S(2)}, u32[]{:S(2)}) collective-permute-start(f32[3,2,128,128]{3,2,1,0:T(8,128)S(1)} %slice.160), channel_id=1, source_target_pairs={{0,2},{2,0},{1,3},{3,1},{4,6},{6,4},{5,7},{7,5},{8,10},{10,8},{9,1... | collective-permute-start | bytes 1179656 | tf_op jit(solution)/shard_map/ppermute | solution.py:34
  140.3 8.5 %collective-permute-start.20 = (f32[3,2,128,128]{3,2,1,0:T(8,128)S(1)}, f32[3,2,128,128]{3,2,1,0:T(8,128)S(1)}, u32[]{:S(2)}, u32[]{:S(2)}) collective-permute-start(f32[3,2,128,128]{3,2,1,0:T(8,128)S(1)} %slice.164), channel_id=1, source_target_pairs={{0,64},{64,0},{1,65},{65,1},{2,66},{66,2},{3,67},{67,3},{4,68},{68... | collective-permute-start | bytes 1179656 | tf_op jit(solution)/shard_map/ppermute | solution.py:34
  150.9 20.2 %all-to-all-start = ((f32[128,1,1]{2,1,0:T(1,128)}), f32[128,1,1]{2,1,0:T(1,128)S(1)}, u32[]{:S(2)}, u32[]{:S(2)}) async-start(f32[128,1,1]{2,1,0:T(1,128)} %broadcast_in_dim.8), calls=%async_computation | async-start | bytes 131072 | tf_op jit(solution)/shard_map/all_to_all | solution.py:398
  (19 other events, 188.9 us)

commit v4 on v3

--- a/solution.py
+++ b/solution.py
@@ -98,7 +98,8 @@
     position = jnp.zeros(table.shape, jnp.int32)
     for lo, hi, order in PARTS:
         block = sum(differs[a] << s for s, a in enumerate(order))
-        position = jnp.where((slot >= lo) & (slot < hi), 8 * lo + block * (hi - lo) + slot - lo, position)
+        place = 8 * lo + block * (hi - lo) + slot - lo + ((block >> 2) << 6)
+        position = jnp.where((slot >= lo) & (slot < hi), place, position)
     valid = inside & (slot >= 0)
     power = (1 << (lane & 15)).astype(F32)
 
@@ -127,7 +128,7 @@
     def append(state, target, row):
         bits, count = state
         slot = 31 - lax.clz(bits & -bits)
-        list_ref[count] = encode(target, row, slot, plan_ref[row, slot])
+        list_ref[count] = encode(target, row, slot, plan_ref[row, slot] & 63)
         return bits & (bits - 1), count + 1
 
     def visit(target, count):
@@ -136,6 +137,25 @@
         return lax.while_loop(lambda s: s[0] != 0, add, (plan_ref[row, 48], count))[1]
 
     return pad_list(list_ref, lax.fori_loop(0, targets, visit, jnp.int32(0)))
+
+
+def list_split(targets, rows_ref, plan_ref, early_ref, late_ref):
+    def append(state, target, row):
+        bits, early, late = state
+        slot = 31 - lax.clz(bits & -bits)
+        value = plan_ref[row, slot]
+        code = encode(target, row, slot, value & 63)
+        early_ref[early] = code
+        late_ref[late] = code
+        return bits & (bits - 1), early + 1 - (value >> 6), late + (value >> 6)
+
+    def visit(target, counts):
+        row = rows_ref[target]
+        add = functools.partial(append, target=target, row=row)
+        return lax.while_loop(lambda s: s[0] != 0, add, (plan_ref[row, 48], *counts))[1:]
+
+    early, late = lax.fori_loop(0, targets, visit, (jnp.int32(0), jnp.int32(0)))
+    return pad_list(early_ref, early), pad_list(late_ref, late)
 
 
 def pad_list(list_ref, count):
@@ -227,16 +247,18 @@
 
 
 def first_kernel(
-    plan_ref, coef_ref, rows_ref, left_ref, right_ref, _, a_ref, b_ref, c_ref, source_ref, out_ref, list_ref, sems
+    plan_ref, coef_ref, rows_ref, left_ref, right_ref, _, a_ref, b_ref, c_ref, source_ref, out_ref, *refs
 ):
+    early_ref, late_ref, sems = refs
     copies = block_copies([[a_ref], [b_ref], [c_ref]], (3,), source_ref, sems)
     for copy in copies:
         copy.start()
-    count = list_far(out_ref.shape[0], rows_ref, 0, plan_ref, list_ref)
+    early, late = list_split(out_ref.shape[0], rows_ref, plan_ref, early_ref, late_ref)
     clear(out_ref)
+    add_terms(early, early_ref, plan_ref, coef_ref, source_ref, left_ref, right_ref, out_ref)
     for copy in copies:
         copy.wait()
-    add_terms(count, list_ref, plan_ref, coef_ref, source_ref, left_ref, right_ref, out_ref)
+    add_terms(late, late_ref, plan_ref, coef_ref, source_ref, left_ref, right_ref, out_ref)
 
 
 def next_kernel(outs, plan_ref, coef_ref, rows_ref, source_ref, left_ref, right_ref, *refs):
@@ -246,6 +268,30 @@
         count = list_far(targets, rows_ref, i * targets, plan_ref, list_ref)
         clear(out_ref)
         add_terms(count, list_ref, plan_ref, coef_ref, source_ref, left_ref, right_ref, out_ref)
+
+
+def derivative_kernel(own_ref, *refs):
+    ins, (out_ref, again_ref, total_ref) = refs[:-3], refs[-3:]
+    squares = jnp.zeros(own_ref.shape[2:], F32)
+    for i, (lo, hi, _) in enumerate(PARTS):
+        keep_ref, mate_ref = ins[2 * i : 2 * i + 2]
+        for m in range(lo, hi):
+            for part in range(2):
+                value = own_ref[m, part] + (keep_ref[m - lo, part] + mate_ref[m - lo, part])
+                out_ref[m, part] = value
+                again_ref[m, part] = value
+                squares += value * value
+    total = jnp.sum(jnp.sum(squares, axis=0, keepdims=True), axis=1, keepdims=True)
+    total_ref[...] = jnp.broadcast_to(total.reshape(1, 1, 1), total_ref.shape)
+
+
+def advance_kernel(step_ref, totals_ref, derivative_ref, state_ref, out_ref):
+    total = jnp.sum(totals_ref[...], axis=0)
+    rms = jnp.sqrt(total / (totals_ref.shape[0] * derivative_ref.size) + 1e-06)
+    scale = step_ref[0] / rms
+    for m in range(out_ref.shape[0]):
+        for part in range(2):
+            out_ref[m, part] = state_ref[m, part] + scale * derivative_ref[m, part]
 
 
 def spec(space):
@@ -346,7 +392,7 @@
         out_shape=(everything, target),
         in_specs=[smem] * 3 + [vmem] * 3 + [spec(pltpu.HBM)] * 3,
         out_specs=(vmem,) * 2,
-        scratch_shapes=[listing, pltpu.SemaphoreType.DMA((12,))],
+        scratch_shapes=[listing, listing, pltpu.SemaphoreType.DMA((12,))],
         input_output_aliases={5: 0},
         compiler_params=params(24),
         cost_estimate=cost(32, n),
@@ -383,22 +429,31 @@
     keeps = [kept[rows] + swapped[rows] for rows in parts]
     keeps, own = lax.optimization_barrier((keeps, own))
 
-    sums = []
+    ends = []
     for give, keep, (_, _, axes) in zip(gives, keeps, PARTS):
-        for stage in range(3):
+        for stage in range(2):
             keep = keep + flip(give, axes[stage] + "h")
             half = keep.shape[0] // 2
-            if stage < 2:
+            if stage == 0:
                 keep, give = keep[:half], keep[half:]
-        sums.append(keep)
-    derivative = own + jnp.concatenate(sums, axis=0)
-
-    total = jnp.sum(derivative * derivative)
-    total = jnp.sum(
-        lax.all_to_all(jnp.broadcast_to(total, (devices,)), ALL, split_axis=0, concat_axis=0, tiled=True)
-    )
-    rms = jnp.sqrt(total / (devices * derivative.size) + 1e-06)
-    return derivative, state + step[0] / rms * derivative
+        ends += [keep, flip(keep[half:], axes[2] + "h")]
+    whole = jax.ShapeDtypeStruct(state.shape, F32)
+    derivative, again, total = pl.pallas_call(
+        derivative_kernel,
+        out_shape=(whole, whole, jax.ShapeDtypeStruct((devices, 1, n), F32)),
+        in_specs=[vmem] * 7,
+        out_specs=(vmem,) * 3,
+        compiler_params=params(8),
+    )(own, *ends)
+    totals = lax.all_to_all(total, ALL, split_axis=0, concat_axis=0, tiled=True)
+    advanced = pl.pallas_call(
+        advance_kernel,
+        out_shape=whole,
+        in_specs=[smem] + [vmem] * 3,
+        out_specs=vmem,
+        compiler_params=params(8),
+    )(step, totals, again, state)
+    return derivative, advanced
 
 
 def solution(mesh):

time: 174 us -> 172 us (0.989)
  other arithmetic: 12.3 us -> 9.59 us
  Pallas kernels: 41 us -> 43.4 us
    ppermute x15, starting transfers between devices: 22.2 us -> 24.8 us  [flip(): return lax.ppermute(value, axis, [(0, 1), (1, 0)])]
    pallas_call x0 -> x2, Pallas kernels: none -> 2.38 us  [the longest x1 1.22 us: body(): pl.pallas_call(advance_kernel, out_shape=whole, in_specs=[smem] + [vmem]...]
  transfers between devices with their start and end apart: 25 -> 25, of which waited for: 16 -> 12; matrix products, arithmetic and copies ran while one was open for 5% -> 5% of each run, Pallas kernels for 20% -> 21%
where the time goes in v4:
time: 172 us; the launch traced here: 171 us
  waiting for transfers between devices  64.4 us (37%)
  starting transfers between devices  50.1 us (29%)
  Pallas kernels  43.4 us (25%)
  other arithmetic  9.59 us (6%)
  local copies, waits for them, and re-layouts  2.1 us (1%)
  between operations  1.73 us (1%)
    ppermute x15, waiting for transfers between devices, flip(): return lax.ppermute(value, axis, [(0, 1), (1, 0)])  34.5 us
    ppermute x15, starting transfers between devices, flip(): return lax.ppermute(value, axis, [(0, 1), (1, 0)])  24.8 us
    ppermute x9, waiting for transfers between devices, body(): part.append(lax.ppermute(block, ALL, pairs[order[stage]]))  21 us
    pallas_call x1, Pallas kernels, body(): pl.pallas_call(own_kernel, out_shape=jax.ShapeDtypeStruct(state.shape, F3...  17.6 us
    ppermute x9, starting transfers between devices, body(): part.append(lax.ppermute(block, ALL, pairs[order[stage]]))  16.2 us
    pallas_call x2, Pallas kernels, later(): pl.pallas_call(functools.partial(next_kernel, outs), out_shape=(target,)...  14.6 us
    all_to_all x1, starting transfers between devices, body(): totals = lax.all_to_all(total, ALL, split_axis=0, concat_axis=0, tiled=True)  8.98 us
    all_to_all x1, waiting for transfers between devices, body(): totals = lax.all_to_all(total, ALL, split_axis=0, concat_axis=0, tiled=True)  8.86 us
  transfers between devices with their start and end apart: 25, of which 12 were waited for; matrix products, arithmetic and copies ran while one was open for 5% of the time, Pallas kernels for 21%

profile of v4, /device:TPU:1, one launch (start us, length us, event | category | flops | bytes accessed | tf_op | source)
XLA Modules:
  0.0 171.2 jit_solution(4153480514501144801)
XLA Ops:
  5.9 2.8 %collective-permute-start.2 = (f32[3,2,128,128]{3,2,1,0:T(8,128)S(1)}, f32[3,2,128,128]{3,2,1,0:T(8,128)S(1)}, u32[]{:S(2)}, u32[]{:S(2)}) collective-permute-start(f32[3,2,128,128]{3,2,1,0:T(8,128)S(1)} %get-tuple-element.54), channel_id=1, source_target_pairs={{0,4},{1,5},{2,6},{3,7},{4,0},{5,1},{6,2},{7,3},{8,12},{9,13},{10,... | collective-permute-start | bytes 1179656 | tf_op jit(solution)/shard_map/ppermute | solution.py:353
  8.8 2.5 %collective-permute-start.1 = (f32[3,2,128,128]{3,2,1,0:T(8,128)S(1)}, f32[3,2,128,128]{3,2,1,0:T(8,128)S(1)}, u32[]{:S(2)}, u32[]{:S(2)}) collective-permute-start(f32[3,2,128,128]{3,2,1,0:T(8,128)S(1)} %get-tuple-element.53), channel_id=1, source_target_pairs={{0,32},{1,33},{2,34},{3,35},{4,36},{5,37},{6,38},{7,39},{8,40},{9,... | collective-permute-start | bytes 1179656 | tf_op jit(solution)/shard_map/ppermute | solution.py:353
  11.2 3.8 %collective-permute-start.3 = (f32[3,2,128,128]{3,2,1,0:T(8,128)S(1)}, f32[3,2,128,128]{3,2,1,0:T(8,128)S(1)}, u32[]{:S(2)}, u32[]{:S(2)}) collective-permute-start(f32[3,2,128,128]{3,2,1,0:T(8,128)S(1)} %get-tuple-element.55), channel_id=1, source_target_pairs={{0,1},{1,0},{2,3},{3,2},{4,5},{5,4},{6,7},{7,6},{8,9},{9,8},{10,11... | collective-permute-start | bytes 1179656 | tf_op jit(solution)/shard_map/ppermute | solution.py:353
  15.5 3.5 %collective-permute-done.4 = s32[16,128]{1,0:T(8,128)S(1)} collective-permute-done((s32[16,128]{1,0:T(8,128)S(1)}, s32[16,128]{1,0:T(8,128)S(1)}, u32[]{:S(2)}, u32[]{:S(2)}) %collective-permute-start.4) | collective-permute-done | bytes 8224 | tf_op jit(solution)/shard_map/ppermute | solution.py:34
  20.5 2.7 %collective-permute-start.6 = (f32[6,2,128,128]{3,2,1,0:T(8,128)S(1)}, f32[6,2,128,128]{3,2,1,0:T(8,128)S(1)}, u32[]{:S(2)}, u32[]{:S(2)}) collective-permute-start(f32[6,2,128,128]{3,2,1,0:T(8,128)S(1)} %pad_maximum_fusion.4), channel_id=1, source_target_pairs={{0,1},{1,0},{2,3},{3,2},{4,5},{5,4},{6,7},{7,6},{8,9},{9,8},{10,11... | collective-permute-start | bytes 2359304 | tf_op jit(solution)/shard_map/ppermute | solution.py:353
  24.9 2.9 %collective-permute-done.8 = s32[32,128]{1,0:T(8,128)S(1)} collective-permute-done((s32[32,128]{1,0:T(8,128)S(1)}, s32[32,128]{1,0:T(8,128)S(1)}, u32[]{:S(2)}, u32[]{:S(2)}) %collective-permute-start.8) | collective-permute-done | bytes 16416 | tf_op jit(solution)/shard_map/ppermute | solution.py:34
  27.8 4.6 %collective-permute-done.7.refs_6_ = f32[6,2,128,128]{3,2,1,0:T(8,128)S(1)} collective-permute-done((f32[6,2,128,128]{3,2,1,0:T(8,128)S(1)}, f32[6,2,128,128]{3,2,1,0:T(8,128)S(1)}, u32[]{:S(2)}, u32[]{:S(2)}) %collective-permute-start.7) | collective-permute-done | bytes 786464 | tf_op jit(solution)/shard_map/ppermute | solution.py:353
  41.3 2.2 %shard_map.141 = (f32[64,2,128,128]{3,2,1,0:T(8,128)S(1)}, bf16[16,256,256]{2,1,0:T(8,128)(2,1)S(1)}, bf16[16,256,256]{2,1,0:T(8,128)(2,1)S(1)}) custom-call(f32[16,128,128]{2,1,0:T(8,128)S(1)} %copy-done.4, f32[8,2,128,128]{3,2,1,0:T(8,128)} %state_ref.1, f32[3,2,128,128]{3,2,1,0:T(8,128)} %copy-done.8, f32[6,2,128,128]{3,2,1,0:T(8,128)} %copy-done.12, ...), custom_call_target="tpu_custom_call" | custom-call | flops 10737418240 | bytes 8388608 | tf_op jit(solution)/shard_map/pallas_call | solution.py:380
  43.5 14.3 %collective-permute-done.10.c_ref = f32[12,2,128,128]{3,2,1,0:T(8,128)} collective-permute-done((f32[12,2,128,128]{3,2,1,0:T(8,128)}, f32[12,2,128,128]{3,2,1,0:T(8,128)}, u32[]{:S(2)}, u32[]{:S(2)}) %collective-permute-start.10) | collective-permute-done | bytes 1572896 | tf_op jit(solution)/shard_map/ppermute | solution.py:353
  60.2 5.5 %shard_map.142 = (f32[64,2,128,128]{3,2,1,0:T(8,128)S(1)}, f32[32,2,128,128]{3,2,1,0:T(8,128)S(1)}) custom-call(s32[128,128]{1,0:T(8,128)S(1)} %shard_map.140.plan_ref, f32[32]{0:T(128)S(1)} %reshape.60.coef_ref, s32[32]{0:T(128)S(1)} %copy-done.3, bf16[16,256,256]{2,1,0:T(8,128)(2,1)S(1)} %get-tuple-element.72.left_ref, ...), custom_call_target="tpu_custom_call", output_to_operand_aliasing={{0}: (5, {})} | custom-call | flops 2147483648 | bytes 8388608 | tf_op jit(solution)/shard_map/pallas_call | solution.py:390
  65.7 3.3 %collective-permute-start.13 = (f32[32,2,128,128]{3,2,1,0:T(8,128)S(1)}, f32[32,2,128,128]{3,2,1,0:T(8,128)S(1)}, u32[]{:S(2)}, u32[]{:S(2)}) collective-permute-start(f32[32,2,128,128]{3,2,1,0:T(8,128)S(1)} %get-tuple-element.77), channel_id=1, source_target_pairs={{0,16},{16,0},{1,17},{17,1},{2,18},{18,2},{3,19},{19,3},{4,20},{20... | collective-permute-start | bytes 12582920 | tf_op jit(solution)/shard_map/ppermute | solution.py:34
  69.1 9.7 %shard_map.143 = (f32[32,2,128,128]{3,2,1,0:T(8,128)S(1)}, f32[32,2,128,128]{3,2,1,0:T(8,128)S(1)}) custom-call(s32[128,128]{1,0:T(8,128)S(1)} %shard_map.140.plan_ref, f32[32]{0:T(128)S(1)} %reshape.60.coef_ref, s32[64]{0:T(128)S(1)} %copy-done.2, f32[64,2,128,128]{3,2,1,0:T(8,128)S(1)} %get-tuple-element.75.source_ref, ...), custom_call_target="tpu_custom_call" | custom-call | flops 3221225472 | bytes 8388608 | tf_op jit(solution)/shard_map/pallas_call | solution.py:404
  80.9 2.5 %collective-permute-start.18 = (f32[12,2,128,128]{3,2,1,0:T(8,128)S(1)}, f32[12,2,128,128]{3,2,1,0:T(8,128)S(1)}, u32[]{:S(2)}, u32[]{:S(2)}) collective-permute-start(f32[12,2,128,128]{3,2,1,0:T(8,128)S(1)} %get-tuple-element.86), channel_id=1, source_target_pairs={{0,8},{8,0},{1,9},{9,1},{2,10},{10,2},{3,11},{11,3},{4,12},{12,4},... | collective-permute-start | bytes 4718600 | tf_op jit(solution)/shard_map/ppermute | solution.py:34
  83.9 4.9 %shard_map.144 = f32[32,2,128,128]{3,2,1,0:T(8,128)S(1)} custom-call(s32[128,128]{1,0:T(8,128)S(1)} %shard_map.140.plan_ref, f32[32]{0:T(128)S(1)} %reshape.60.coef_ref, s32[32]{0:T(128)S(1)} %copy-done.1, f32[64,2,128,128]{3,2,1,0:T(8,128)S(1)} %get-tuple-element.75.source_ref, bf16[16,256,256]{2,1,0:T(8,128)(2,1)S(1)} %get-tuple-element.72.left_ref, ...), custom_call_target="tpu_custom_call" | custom-call | flops 1610612736 | bytes 8388608 | tf_op jit(solution)/shard_map/pallas_call | solution.py:404
  88.9 17.6 %shard_map.145.own_ref = f32[8,2,128,128]{3,2,1,0:T(8,128)S(1)} custom-call(s32[8,128]{1,0:T(8,128)S(1)} %pad_add_fusion.3.table_ref, f32[32]{0:T(128)S(1)} %reshape.60.coef_ref, f32[16]{0:T(128)S(1)} %copy-done.6, f32[8,2,128,128]{3,2,1,0:T(8,128)S(1)} %copy-done, bf16[16,256,256]{2,1,0:T(8,128)(2,1)S(1)} %get-tuple-element.72.left_ref, ...), custom_call_target="tpu_custom_call" | custom-call | flops 10737418240 | bytes 8388608 | tf_op jit(solution)/shard_map/pallas_call | solution.py:419
  107.3 10.3 %collective-permute-done.18 = f32[12,2,128,128]{3,2,1,0:T(8,128)S(1)} collective-permute-done((f32[12,2,128,128]{3,2,1,0:T(8,128)S(1)}, f32[12,2,128,128]{3,2,1,0:T(8,128)S(1)}, u32[]{:S(2)}, u32[]{:S(2)}) %collective-permute-start.18) | collective-permute-done | bytes 1572896 | tf_op jit(solution)/shard_map/ppermute | solution.py:34
  117.9 2.8 %collective-permute-start.19 = (f32[6,2,128,128]{3,2,1,0:T(8,128)S(1)}, f32[6,2,128,128]{3,2,1,0:T(8,128)S(1)}, u32[]{:S(2)}, u32[]{:S(2)}) collective-permute-start(f32[6,2,128,128]{3,2,1,0:T(8,128)S(1)} %slice.149), channel_id=1, source_target_pairs={{0,2},{2,0},{1,3},{3,1},{4,6},{6,4},{5,7},{7,5},{8,10},{10,8},{9,1... | collective-permute-start | bytes 2359304 | tf_op jit(solution)/shard_map/ppermute | solution.py:34
  121.0 2.7 %collective-permute-start.16 = (f32[6,2,128,128]{3,2,1,0:T(8,128)S(1)}, f32[6,2,128,128]{3,2,1,0:T(8,128)S(1)}, u32[]{:S(2)}, u32[]{:S(2)}) collective-permute-start(f32[6,2,128,128]{3,2,1,0:T(8,128)S(1)} %slice.146), channel_id=1, source_target_pairs={{0,8},{8,0},{1,9},{9,1},{2,10},{10,2},{3,11},{11,3},{4,12},{12,4},... | collective-permute-start | bytes 2359304 | tf_op jit(solution)/shard_map/ppermute | solution.py:34
  125.2 11.8 %collective-permute-done.19 = f32[6,2,128,128]{3,2,1,0:T(8,128)S(1)} collective-permute-done((f32[6,2,128,128]{3,2,1,0:T(8,128)S(1)}, f32[6,2,128,128]{3,2,1,0:T(8,128)S(1)}, u32[]{:S(2)}, u32[]{:S(2)}) %collective-permute-start.19) | collective-permute-done | bytes 786464 | tf_op jit(solution)/shard_map/ppermute | solution.py:34
  137.1 3.3 %collective-permute-start.20 = (f32[3,2,128,128]{3,2,1,0:T(8,128)S(1)}, f32[3,2,128,128]{3,2,1,0:T(8,128)S(1)}, u32[]{:S(2)}, u32[]{:S(2)}) collective-permute-start(f32[3,2,128,128]{3,2,1,0:T(8,128)S(1)} %slice.150), channel_id=1, source_target_pairs={{0,64},{64,0},{1,65},{65,1},{2,66},{66,2},{3,67},{67,3},{4,68},{68... | collective-permute-start | bytes 1179656 | tf_op jit(solution)/shard_map/ppermute | solution.py:34
  142.0 2.3 %collective-permute-start.23 = (f32[2,2,128,128]{3,2,1,0:T(8,128)S(1)}, f32[2,2,128,128]{3,2,1,0:T(8,128)S(1)}, u32[]{:S(2)}, u32[]{:S(2)}) collective-permute-start(f32[2,2,128,128]{3,2,1,0:T(8,128)S(1)} %slice.153), channel_id=1, source_target_pairs={{0,8},{8,0},{1,9},{9,1},{2,10},{10,2},{3,11},{11,3},{4,12},{12,4},... | collective-permute-start | bytes 786440 | tf_op jit(solution)/shard_map/ppermute | solution.py:34
  144.3 4.8 %collective-permute-done.23.refs_5_ = f32[2,2,128,128]{3,2,1,0:T(8,128)S(1)} collective-permute-done((f32[2,2,128,128]{3,2,1,0:T(8,128)S(1)}, f32[2,2,128,128]{3,2,1,0:T(8,128)S(1)}, u32[]{:S(2)}, u32[]{:S(2)}) %collective-permute-start.23) | collective-permute-done | bytes 262176 | tf_op jit(solution)/shard_map/ppermute | solution.py:34
  151.5 9.0 %all-to-all-start = ((f32[128,1,128]{2,1,0:T(1,128)}), f32[128,1,128]{2,1,0:T(1,128)S(1)}, u32[]{:S(2)}, u32[]{:S(2)}) async-start(f32[128,1,128]{2,1,0:T(1,128)} %get-tuple-element.90), calls=%async_computation | async-start | bytes 131072 | tf_op jit(solution)/shard_map/all_to_all | solution.py:448
  161.1 8.9 %all-to-all-done.totals_ref = f32[128,1,128]{2,1,0:T(1,128)S(1)} async-done(((f32[128,1,128]{2,1,0:T(1,128)}), f32[128,1,128]{2,1,0:T(1,128)S(1)}, u32[]{:S(2)}, u32[]{:S(2)}) %all-to-all-start) | async-done | bytes 65568 | tf_op jit(solution)/shard_map/all_to_all | solution.py:448
  (105 shorter events, 30.8 us)
Async XLA Ops:
  1.5 4.3 %collective-permute-start = (s32[8,128]{1,0:T(8,128)S(1)}, s32[8,128]{1,0:T(8,128)S(1)}, u32[]{:S(2)}, u32[]{:S(2)}) collective-permute-start(s32[8,128]{1,0:T(8,128)S(1)} %pad_add_fusion.3.table_ref), channel_id=1, source_target_pairs={{0,16},{16,0},{1,17},{17,1},{2,18},{18,2},{3,19},{19,3},{4,20},{20... | collective-permute-start | bytes 12296 | tf_op jit(solution)/shard_map/ppermute | solution.py:34
  5.9 13.1 %collective-permute-start.2 = (f32[3,2,128,128]{3,2,1,0:T(8,128)S(1)}, f32[3,2,128,128]{3,2,1,0:T(8,128)S(1)}, u32[]{:S(2)}, u32[]{:S(2)}) collective-permute-start(f32[3,2,128,128]{3,2,1,0:T(8,128)S(1)} %get-tuple-element.54), channel_id=1, source_target_pairs={{0,4},{1,5},{2,6},{3,7},{4,0},{5,1},{6,2},{7,3},{8,12},{9,13},{10,... | collective-permute-start | bytes 1179656 | tf_op jit(solution)/shard_map/ppermute | solution.py:353
  8.8 10.3 %collective-permute-start.1 = (f32[3,2,128,128]{3,2,1,0:T(8,128)S(1)}, f32[3,2,128,128]{3,2,1,0:T(8,128)S(1)}, u32[]{:S(2)}, u32[]{:S(2)}) collective-permute-start(f32[3,2,128,128]{3,2,1,0:T(8,128)S(1)} %get-tuple-element.53), channel_id=1, source_target_pairs={{0,32},{1,33},{2,34},{3,35},{4,36},{5,37},{6,38},{7,39},{8,40},{9,... | collective-permute-start | bytes 1179656 | tf_op jit(solution)/shard_map/ppermute | solution.py:353
  11.2 8.9 %collective-permute-start.3 = (f32[3,2,128,128]{3,2,1,0:T(8,128)S(1)}, f32[3,2,128,128]{3,2,1,0:T(8,128)S(1)}, u32[]{:S(2)}, u32[]{:S(2)}) collective-permute-start(f32[3,2,128,128]{3,2,1,0:T(8,128)S(1)} %get-tuple-element.55), channel_id=1, source_target_pairs={{0,1},{1,0},{2,3},{3,2},{4,5},{5,4},{6,7},{7,6},{8,9},{9,8},{10,11... | collective-permute-start | bytes 1179656 | tf_op jit(solution)/shard_map/ppermute | solution.py:353
  20.2 12.1 %collective-permute-start.7 = (f32[6,2,128,128]{3,2,1,0:T(8,128)S(1)}, f32[6,2,128,128]{3,2,1,0:T(8,128)S(1)}, u32[]{:S(2)}, u32[]{:S(2)}) collective-permute-start(f32[6,2,128,128]{3,2,1,0:T(8,128)S(1)} %pad_maximum_fusion.5), channel_id=1, source_target_pairs={{0,32},{1,33},{2,34},{3,35},{4,36},{5,37},{6,38},{7,39},{8,40},{9,... | collective-permute-start | bytes 2359304 | tf_op jit(solution)/shard_map/ppermute | solution.py:353
  20.5 13.2 %collective-permute-start.6 = (f32[6,2,128,128]{3,2,1,0:T(8,128)S(1)}, f32[6,2,128,128]{3,2,1,0:T(8,128)S(1)}, u32[]{:S(2)}, u32[]{:S(2)}) collective-permute-start(f32[6,2,128,128]{3,2,1,0:T(8,128)S(1)} %pad_maximum_fusion.4), channel_id=1, source_target_pairs={{0,1},{1,0},{2,3},{3,2},{4,5},{5,4},{6,7},{7,6},{8,9},{9,8},{10,11... | collective-permute-start | bytes 2359304 | tf_op jit(solution)/shard_map/ppermute | solution.py:353
  23.2 12.4 %collective-permute-start.5 = (f32[6,2,128,128]{3,2,1,0:T(8,128)S(1)}, f32[6,2,128,128]{3,2,1,0:T(8,128)S(1)}, u32[]{:S(2)}, u32[]{:S(2)}) collective-permute-start(f32[6,2,128,128]{3,2,1,0:T(8,128)S(1)} %pad_maximum_fusion.3), channel_id=1, source_target_pairs={{0,4},{1,5},{2,6},{3,7},{4,0},{5,1},{6,2},{7,3},{8,12},{9,13},{10,... | collective-permute-start | bytes 2359304 | tf_op jit(solution)/shard_map/ppermute | solution.py:353
  23.5 4.3 %collective-permute-start.8 = (s32[32,128]{1,0:T(8,128)S(1)}, s32[32,128]{1,0:T(8,128)S(1)}, u32[]{:S(2)}, u32[]{:S(2)}) collective-permute-start(s32[32,128]{1,0:T(8,128)S(1)} %pad_add_fusion.1), channel_id=1, source_target_pairs={{0,8},{8,0},{1,9},{9,1},{2,10},{10,2},{3,11},{11,3},{4,12},{12,4},... | collective-permute-start | bytes 49160 | tf_op jit(solution)/shard_map/ppermute | solution.py:34
  37.1 20.8 %collective-permute-start.10 = (f32[12,2,128,128]{3,2,1,0:T(8,128)}, f32[12,2,128,128]{3,2,1,0:T(8,128)}, u32[]{:S(2)}, u32[]{:S(2)}) collective-permute-start(f32[12,2,128,128]{3,2,1,0:T(8,128)} %pad_maximum_fusion.2), channel_id=1, source_target_pairs={{0,4},{1,5},{2,6},{3,7},{4,0},{5,1},{6,2},{7,3},{8,12},{9,13},{10,... | collective-permute-start | bytes 4718600 | tf_op jit(solution)/shard_map/ppermute | solution.py:353
  37.3 22.4 %collective-permute-start.11 = (f32[12,2,128,128]{3,2,1,0:T(8,128)}, f32[12,2,128,128]{3,2,1,0:T(8,128)}, u32[]{:S(2)}, u32[]{:S(2)}) collective-permute-start(f32[12,2,128,128]{3,2,1,0:T(8,128)} %pad_maximum_fusion), channel_id=1, source_target_pairs={{0,1},{1,0},{2,3},{3,2},{4,5},{5,4},{6,7},{7,6},{8,9},{9,8},{10,11... | collective-permute-start | bytes 4718600 | tf_op jit(solution)/shard_map/ppermute | solution.py:353
  39.4 20.8 %collective-permute-start.12 = (f32[12,2,128,128]{3,2,1,0:T(8,128)}, f32[12,2,128,128]{3,2,1,0:T(8,128)}, u32[]{:S(2)}, u32[]{:S(2)}) collective-permute-start(f32[12,2,128,128]{3,2,1,0:T(8,128)} %pad_maximum_fusion.1), channel_id=1, source_target_pairs={{0,32},{1,33},{2,34},{3,35},{4,36},{5,37},{6,38},{7,39},{8,40},{9,... | collective-permute-start | bytes 4718600 | tf_op jit(solution)/shard_map/ppermute | solution.py:353
  41.2 17.4 %collective-permute-start.9 = (s32[64,128]{1,0:T(8,128)S(1)}, s32[64,128]{1,0:T(8,128)S(1)}, u32[]{:S(2)}, u32[]{:S(2)}) collective-permute-start(s32[64,128]{1,0:T(8,128)S(1)} %pad_add_fusion.low_ref), channel_id=1, source_target_pairs={{0,2},{2,0},{1,3},{3,1},{4,6},{6,4},{5,7},{7,5},{8,10},{10,8},{9,1... | collective-permute-start | bytes 98312 | tf_op jit(solution)/shard_map/ppermute | solution.py:34
  65.7 13.0 %collective-permute-start.13 = (f32[32,2,128,128]{3,2,1,0:T(8,128)S(1)}, f32[32,2,128,128]{3,2,1,0:T(8,128)S(1)}, u32[]{:S(2)}, u32[]{:S(2)}) collective-permute-start(f32[32,2,128,128]{3,2,1,0:T(8,128)S(1)} %get-tuple-element.77), channel_id=1, source_target_pairs={{0,16},{16,0},{1,17},{17,1},{2,18},{18,2},{3,19},{19,3},{4,20},{20... | collective-permute-start | bytes 12582920 | tf_op jit(solution)/shard_map/ppermute | solution.py:34
  79.6 26.9 %collective-permute-start.14 = (f32[32,2,128,128]{3,2,1,0:T(8,128)S(1)}, f32[32,2,128,128]{3,2,1,0:T(8,128)S(1)}, u32[]{:S(2)}, u32[]{:S(2)}) collective-permute-start(f32[32,2,128,128]{3,2,1,0:T(8,128)S(1)} %get-tuple-element.80), channel_id=1, source_target_pairs={{0,16},{16,0},{1,17},{17,1},{2,18},{18,2},{3,19},{19,3},{4,20},{20... | collective-permute-start | bytes 12582920 | tf_op jit(solution)/shard_map/ppermute | solution.py:34
  79.7 44.0 %collective-permute-start.21 = (f32[8,2,128,128]{3,2,1,0:T(8,128)S(1)}, f32[8,2,128,128]{3,2,1,0:T(8,128)S(1)}, u32[]{:S(2)}, u32[]{:S(2)}) collective-permute-start(f32[8,2,128,128]{3,2,1,0:T(8,128)S(1)} %slice_add_fusion.5), channel_id=1, source_target_pairs={{0,2},{2,0},{1,3},{3,1},{4,6},{6,4},{5,7},{7,5},{8,10},{10,8},{9,1... | collective-permute-start | bytes 3145736 | tf_op jit(solution)/shard_map/ppermute | solution.py:34
  80.9 36.7 %collective-permute-start.18 = (f32[12,2,128,128]{3,2,1,0:T(8,128)S(1)}, f32[12,2,128,128]{3,2,1,0:T(8,128)S(1)}, u32[]{:S(2)}, u32[]{:S(2)}) collective-permute-start(f32[12,2,128,128]{3,2,1,0:T(8,128)S(1)} %get-tuple-element.86), channel_id=1, source_target_pairs={{0,8},{8,0},{1,9},{9,1},{2,10},{10,2},{3,11},{11,3},{4,12},{12,4},... | collective-permute-start | bytes 4718600 | tf_op jit(solution)/shard_map/ppermute | solution.py:34
  83.4 37.3 %collective-permute-start.15 = (f32[12,2,128,128]{3,2,1,0:T(8,128)S(1)}, f32[12,2,128,128]{3,2,1,0:T(8,128)S(1)}, u32[]{:S(2)}, u32[]{:S(2)}) collective-permute-start(f32[12,2,128,128]{3,2,1,0:T(8,128)S(1)} %get-tuple-element.84), channel_id=1, source_target_pairs={{0,64},{64,0},{1,65},{65,1},{2,66},{66,2},{3,67},{67,3},{4,68},{68... | collective-permute-start | bytes 4718600 | tf_op jit(solution)/shard_map/ppermute | solution.py:34
  117.9 19.0 %collective-permute-start.19 = (f32[6,2,128,128]{3,2,1,0:T(8,128)S(1)}, f32[6,2,128,128]{3,2,1,0:T(8,128)S(1)}, u32[]{:S(2)}, u32[]{:S(2)}) collective-permute-start(f32[6,2,128,128]{3,2,1,0:T(8,128)S(1)} %slice.149), channel_id=1, source_target_pairs={{0,2},{2,0},{1,3},{3,1},{4,6},{6,4},{5,7},{7,5},{8,10},{10,8},{9,1... | collective-permute-start | bytes 2359304 | tf_op jit(solution)/shard_map/ppermute | solution.py:34
  121.0 19.4 %collective-permute-start.16 = (f32[6,2,128,128]{3,2,1,0:T(8,128)S(1)}, f32[6,2,128,128]{3,2,1,0:T(8,128)S(1)}, u32[]{:S(2)}, u32[]{:S(2)}) collective-permute-start(f32[6,2,128,128]{3,2,1,0:T(8,128)S(1)} %slice.146), channel_id=1, source_target_pairs={{0,8},{8,0},{1,9},{9,1},{2,10},{10,2},{3,11},{11,3},{4,12},{12,4},... | collective-permute-start | bytes 2359304 | tf_op jit(solution)/shard_map/ppermute | solution.py:34
  123.9 18.0 %collective-permute-start.22 = (f32[4,2,128,128]{3,2,1,0:T(8,128)S(1)}, f32[4,2,128,128]{3,2,1,0:T(8,128)S(1)}, u32[]{:S(2)}, u32[]{:S(2)}) collective-permute-start(f32[4,2,128,128]{3,2,1,0:T(8,128)S(1)} %slice.152), channel_id=1, source_target_pairs={{0,64},{64,0},{1,65},{65,1},{2,66},{66,2},{3,67},{67,3},{4,68},{68... | collective-permute-start | bytes 1572872 | tf_op jit(solution)/shard_map/ppermute | solution.py:34
  137.1 12.0 %collective-permute-start.20 = (f32[3,2,128,128]{3,2,1,0:T(8,128)S(1)}, f32[3,2,128,128]{3,2,1,0:T(8,128)S(1)}, u32[]{:S(2)}, u32[]{:S(2)}) collective-permute-start(f32[3,2,128,128]{3,2,1,0:T(8,128)S(1)} %slice.150), channel_id=1, source_target_pairs={{0,64},{64,0},{1,65},{65,1},{2,66},{66,2},{3,67},{67,3},{4,68},{68... | collective-permute-start | bytes 1179656 | tf_op jit(solution)/shard_map/ppermute | solution.py:34
  140.5 9.8 %collective-permute-start.17 = (f32[3,2,128,128]{3,2,1,0:T(8,128)S(1)}, f32[3,2,128,128]{3,2,1,0:T(8,128)S(1)}, u32[]{:S(2)}, u32[]{:S(2)}) collective-permute-start(f32[3,2,128,128]{3,2,1,0:T(8,128)S(1)} %slice.147), channel_id=1, source_target_pairs={{0,2},{2,0},{1,3},{3,1},{4,6},{6,4},{5,7},{7,5},{8,10},{10,8},{9,1... | collective-permute-start | bytes 1179656 | tf_op jit(solution)/shard_map/ppermute | solution.py:34
  142.0 7.1 %collective-permute-start.23 = (f32[2,2,128,128]{3,2,1,0:T(8,128)S(1)}, f32[2,2,128,128]{3,2,1,0:T(8,128)S(1)}, u32[]{:S(2)}, u32[]{:S(2)}) collective-permute-start(f32[2,2,128,128]{3,2,1,0:T(8,128)S(1)} %slice.153), channel_id=1, source_target_pairs={{0,8},{8,0},{1,9},{9,1},{2,10},{10,2},{3,11},{11,3},{4,12},{12,4},... | collective-permute-start | bytes 786440 | tf_op jit(solution)/shard_map/ppermute | solution.py:34
  151.5 18.5 %all-to-all-start = ((f32[128,1,128]{2,1,0:T(1,128)}), f32[128,1,128]{2,1,0:T(1,128)S(1)}, u32[]{:S(2)}, u32[]{:S(2)}) async-start(f32[128,1,128]{2,1,0:T(1,128)} %get-tuple-element.90), calls=%async_computation | async-start | bytes 131072 | tf_op jit(solution)/shard_map/all_to_all | solution.py:448
  (18 other events, 156.3 us)

commit v5 on v4

--- a/solution.py
+++ b/solution.py
@@ -10,7 +10,7 @@
 from jax.sharding import PartitionSpec as P
 
 ALL = ("xh", "xl", "c", "yh", "yl", "zh", "zl")
-UNROLL = 4
+UNROLL = 6
 F32 = jnp.float32
 BF16 = jnp.bfloat16
 PARTS = ((0, 3, "xyz"), (3, 6, "yzx"), (6, 8, "zxy"))

time: 172 us -> 171 us (level)
  waiting for transfers between devices: 64.4 us -> 68 us
  Pallas kernels: 43.4 us -> 40.4 us
    ppermute x15, waiting for transfers between devices: 34.5 us -> 38.2 us  [flip(): return lax.ppermute(value, axis, [(0, 1), (1, 0)])]
    pallas_call x1, Pallas kernels: 17.6 us -> 14.5 us  [body(): pl.pallas_call(own_kernel, out_shape=jax.ShapeDtypeStruct(state.shape, F3...]
    ppermute x15, starting transfers between devices: 24.8 us -> 22.4 us  [flip(): return lax.ppermute(value, axis, [(0, 1), (1, 0)])]
  transfers between devices with their start and end apart: 25 -> 25, of which waited for: 12 -> 13; matrix products, arithmetic and copies ran while one was open for 5% -> 5% of each run, Pallas kernels for 21% -> 19%
where the time goes in v5:
time: 171 us
  waiting for transfers between devices  68 us (40%)
  starting transfers between devices  49.1 us (29%)
  Pallas kernels  40.4 us (24%)
  other arithmetic  9.59 us (6%)
  local copies, waits for them, and re-layouts  2.1 us (1%)
  between operations  1.73 us (1%)
    ppermute x15, waiting for transfers between devices, flip(): return lax.ppermute(value, axis, [(0, 1), (1, 0)])  38.2 us
    ppermute x15, starting transfers between devices, flip(): return lax.ppermute(value, axis, [(0, 1), (1, 0)])  22.4 us
    ppermute x9, waiting for transfers between devices, body(): part.append(lax.ppermute(block, ALL, pairs[order[stage]]))  21 us
    ppermute x9, starting transfers between devices, body(): part.append(lax.ppermute(block, ALL, pairs[order[stage]]))  16.2 us
    pallas_call x2, Pallas kernels, later(): pl.pallas_call(functools.partial(next_kernel, outs), out_shape=(target,)...  15 us
    pallas_call x1, Pallas kernels, body(): pl.pallas_call(own_kernel, out_shape=jax.ShapeDtypeStruct(state.shape, F3...  14.5 us
    all_to_all x1, starting transfers between devices, body(): totals = lax.all_to_all(total, ALL, split_axis=0, concat_axis=0, tiled=True)  10.4 us
    all_to_all x1, waiting for transfers between devices, body(): totals = lax.all_to_all(total, ALL, split_axis=0, concat_axis=0, tiled=True)  8.86 us
  transfers between devices with their start and end apart: 25, of which 13 were waited for; matrix products, arithmetic and copies ran while one was open for 5% of the time, Pallas kernels for 19%

profile of v5, /device:TPU:1, one launch (start us, length us, event | category | flops | bytes accessed | tf_op | source)
XLA Modules:
  0.0 170.9 jit_solution(5289965453167014956)
XLA Ops:
  5.9 2.8 %collective-permute-start.2 = (f32[3,2,128,128]{3,2,1,0:T(8,128)S(1)}, f32[3,2,128,128]{3,2,1,0:T(8,128)S(1)}, u32[]{:S(2)}, u32[]{:S(2)}) collective-permute-start(f32[3,2,128,128]{3,2,1,0:T(8,128)S(1)} %get-tuple-element.54), channel_id=1, source_target_pairs={{0,4},{1,5},{2,6},{3,7},{4,0},{5,1},{6,2},{7,3},{8,12},{9,13},{10,... | collective-permute-start | bytes 1179656 | tf_op jit(solution)/shard_map/ppermute | solution.py:353
  8.8 2.5 %collective-permute-start.1 = (f32[3,2,128,128]{3,2,1,0:T(8,128)S(1)}, f32[3,2,128,128]{3,2,1,0:T(8,128)S(1)}, u32[]{:S(2)}, u32[]{:S(2)}) collective-permute-start(f32[3,2,128,128]{3,2,1,0:T(8,128)S(1)} %get-tuple-element.53), channel_id=1, source_target_pairs={{0,32},{1,33},{2,34},{3,35},{4,36},{5,37},{6,38},{7,39},{8,40},{9,... | collective-permute-start | bytes 1179656 | tf_op jit(solution)/shard_map/ppermute | solution.py:353
  11.2 3.8 %collective-permute-start.3 = (f32[3,2,128,128]{3,2,1,0:T(8,128)S(1)}, f32[3,2,128,128]{3,2,1,0:T(8,128)S(1)}, u32[]{:S(2)}, u32[]{:S(2)}) collective-permute-start(f32[3,2,128,128]{3,2,1,0:T(8,128)S(1)} %get-tuple-element.55), channel_id=1, source_target_pairs={{0,1},{1,0},{2,3},{3,2},{4,5},{5,4},{6,7},{7,6},{8,9},{9,8},{10,11... | collective-permute-start | bytes 1179656 | tf_op jit(solution)/shard_map/ppermute | solution.py:353
  15.5 3.5 %collective-permute-done.4 = s32[16,128]{1,0:T(8,128)S(1)} collective-permute-done((s32[16,128]{1,0:T(8,128)S(1)}, s32[16,128]{1,0:T(8,128)S(1)}, u32[]{:S(2)}, u32[]{:S(2)}) %collective-permute-start.4) | collective-permute-done | bytes 8224 | tf_op jit(solution)/shard_map/ppermute | solution.py:34
  20.5 2.7 %collective-permute-start.6 = (f32[6,2,128,128]{3,2,1,0:T(8,128)S(1)}, f32[6,2,128,128]{3,2,1,0:T(8,128)S(1)}, u32[]{:S(2)}, u32[]{:S(2)}) collective-permute-start(f32[6,2,128,128]{3,2,1,0:T(8,128)S(1)} %pad_maximum_fusion.4), channel_id=1, source_target_pairs={{0,1},{1,0},{2,3},{3,2},{4,5},{5,4},{6,7},{7,6},{8,9},{9,8},{10,11... | collective-permute-start | bytes 2359304 | tf_op jit(solution)/shard_map/ppermute | solution.py:353
  24.9 2.9 %collective-permute-done.8 = s32[32,128]{1,0:T(8,128)S(1)} collective-permute-done((s32[32,128]{1,0:T(8,128)S(1)}, s32[32,128]{1,0:T(8,128)S(1)}, u32[]{:S(2)}, u32[]{:S(2)}) %collective-permute-start.8) | collective-permute-done | bytes 16416 | tf_op jit(solution)/shard_map/ppermute | solution.py:34
  27.8 4.6 %collective-permute-done.7.refs_6_ = f32[6,2,128,128]{3,2,1,0:T(8,128)S(1)} collective-permute-done((f32[6,2,128,128]{3,2,1,0:T(8,128)S(1)}, f32[6,2,128,128]{3,2,1,0:T(8,128)S(1)}, u32[]{:S(2)}, u32[]{:S(2)}) %collective-permute-start.7) | collective-permute-done | bytes 786464 | tf_op jit(solution)/shard_map/ppermute | solution.py:353
  37.3 2.1 %collective-permute-start.11 = (f32[12,2,128,128]{3,2,1,0:T(8,128)}, f32[12,2,128,128]{3,2,1,0:T(8,128)}, u32[]{:S(2)}, u32[]{:S(2)}) collective-permute-start(f32[12,2,128,128]{3,2,1,0:T(8,128)} %pad_maximum_fusion), channel_id=1, source_target_pairs={{0,1},{1,0},{2,3},{3,2},{4,5},{5,4},{6,7},{7,6},{8,9},{9,8},{10,11... | collective-permute-start | bytes 4718600 | tf_op jit(solution)/shard_map/ppermute | solution.py:353
  41.3 2.2 %shard_map.141 = (f32[64,2,128,128]{3,2,1,0:T(8,128)S(1)}, bf16[16,256,256]{2,1,0:T(8,128)(2,1)S(1)}, bf16[16,256,256]{2,1,0:T(8,128)(2,1)S(1)}) custom-call(f32[16,128,128]{2,1,0:T(8,128)S(1)} %copy-done.4, f32[8,2,128,128]{3,2,1,0:T(8,128)} %state_ref.1, f32[3,2,128,128]{3,2,1,0:T(8,128)} %copy-done.8, f32[6,2,128,128]{3,2,1,0:T(8,128)} %copy-done.12, ...), custom_call_target="tpu_custom_call" | custom-call | flops 10737418240 | bytes 8388608 | tf_op jit(solution)/shard_map/pallas_call | solution.py:380
  43.5 14.3 %collective-permute-done.10.c_ref = f32[12,2,128,128]{3,2,1,0:T(8,128)} collective-permute-done((f32[12,2,128,128]{3,2,1,0:T(8,128)}, f32[12,2,128,128]{3,2,1,0:T(8,128)}, u32[]{:S(2)}, u32[]{:S(2)}) %collective-permute-start.10) | collective-permute-done | bytes 1572896 | tf_op jit(solution)/shard_map/ppermute | solution.py:353
  60.2 5.2 %shard_map.142 = (f32[64,2,128,128]{3,2,1,0:T(8,128)S(1)}, f32[32,2,128,128]{3,2,1,0:T(8,128)S(1)}) custom-call(s32[128,128]{1,0:T(8,128)S(1)} %shard_map.140.plan_ref, f32[32]{0:T(128)S(1)} %reshape.60.coef_ref, s32[32]{0:T(128)S(1)} %copy-done.3, bf16[16,256,256]{2,1,0:T(8,128)(2,1)S(1)} %get-tuple-element.72.left_ref, ...), custom_call_target="tpu_custom_call", output_to_operand_aliasing={{0}: (5, {})} | custom-call | flops 2147483648 | bytes 8388608 | tf_op jit(solution)/shard_map/pallas_call | solution.py:390
  65.4 4.0 %collective-permute-start.13 = (f32[32,2,128,128]{3,2,1,0:T(8,128)S(1)}, f32[32,2,128,128]{3,2,1,0:T(8,128)S(1)}, u32[]{:S(2)}, u32[]{:S(2)}) collective-permute-start(f32[32,2,128,128]{3,2,1,0:T(8,128)S(1)} %get-tuple-element.77), channel_id=1, source_target_pairs={{0,16},{16,0},{1,17},{17,1},{2,18},{18,2},{3,19},{19,3},{4,20},{20... | collective-permute-start | bytes 12582920 | tf_op jit(solution)/shard_map/ppermute | solution.py:34
  69.4 9.3 %shard_map.143 = (f32[32,2,128,128]{3,2,1,0:T(8,128)S(1)}, f32[32,2,128,128]{3,2,1,0:T(8,128)S(1)}) custom-call(s32[128,128]{1,0:T(8,128)S(1)} %shard_map.140.plan_ref, f32[32]{0:T(128)S(1)} %reshape.60.coef_ref, s32[64]{0:T(128)S(1)} %copy-done.2, f32[64,2,128,128]{3,2,1,0:T(8,128)S(1)} %get-tuple-element.75.source_ref, ...), custom_call_target="tpu_custom_call" | custom-call | flops 3221225472 | bytes 8388608 | tf_op jit(solution)/shard_map/pallas_call | solution.py:404
  81.4 3.2 %collective-permute-start.15 = (f32[12,2,128,128]{3,2,1,0:T(8,128)S(1)}, f32[12,2,128,128]{3,2,1,0:T(8,128)S(1)}, u32[]{:S(2)}, u32[]{:S(2)}) collective-permute-start(f32[12,2,128,128]{3,2,1,0:T(8,128)S(1)} %get-tuple-element.84), channel_id=1, source_target_pairs={{0,64},{64,0},{1,65},{65,1},{2,66},{66,2},{3,67},{67,3},{4,68},{68... | collective-permute-start | bytes 4718600 | tf_op jit(solution)/shard_map/ppermute | solution.py:34
  84.6 5.7 %shard_map.144 = f32[32,2,128,128]{3,2,1,0:T(8,128)S(1)} custom-call(s32[128,128]{1,0:T(8,128)S(1)} %shard_map.140.plan_ref, f32[32]{0:T(128)S(1)} %reshape.60.coef_ref, s32[32]{0:T(128)S(1)} %copy-done.1, f32[64,2,128,128]{3,2,1,0:T(8,128)S(1)} %get-tuple-element.75.source_ref, bf16[16,256,256]{2,1,0:T(8,128)(2,1)S(1)} %get-tuple-element.72.left_ref, ...), custom_call_target="tpu_custom_call" | custom-call | flops 1610612736 | bytes 8388608 | tf_op jit(solution)/shard_map/pallas_call | solution.py:404
  90.4 14.5 %shard_map.145.own_ref = f32[8,2,128,128]{3,2,1,0:T(8,128)S(1)} custom-call(s32[8,128]{1,0:T(8,128)S(1)} %pad_add_fusion.3.table_ref, f32[32]{0:T(128)S(1)} %reshape.60.coef_ref, f32[16]{0:T(128)S(1)} %copy-done.6, f32[8,2,128,128]{3,2,1,0:T(8,128)S(1)} %copy-done, bf16[16,256,256]{2,1,0:T(8,128)(2,1)S(1)} %get-tuple-element.72.left_ref, ...), custom_call_target="tpu_custom_call" | custom-call | flops 10737418240 | bytes 8388608 | tf_op jit(solution)/shard_map/pallas_call | solution.py:419
  105.8 11.2 %collective-permute-done.18 = f32[12,2,128,128]{3,2,1,0:T(8,128)S(1)} collective-permute-done((f32[12,2,128,128]{3,2,1,0:T(8,128)S(1)}, f32[12,2,128,128]{3,2,1,0:T(8,128)S(1)}, u32[]{:S(2)}, u32[]{:S(2)}) %collective-permute-start.18) | collective-permute-done | bytes 1572896 | tf_op jit(solution)/shard_map/ppermute | solution.py:34
  117.3 2.7 %collective-permute-start.19 = (f32[6,2,128,128]{3,2,1,0:T(8,128)S(1)}, f32[6,2,128,128]{3,2,1,0:T(8,128)S(1)}, u32[]{:S(2)}, u32[]{:S(2)}) collective-permute-start(f32[6,2,128,128]{3,2,1,0:T(8,128)S(1)} %slice.149), channel_id=1, source_target_pairs={{0,2},{2,0},{1,3},{3,1},{4,6},{6,4},{5,7},{7,5},{8,10},{10,8},{9,1... | collective-permute-start | bytes 2359304 | tf_op jit(solution)/shard_map/ppermute | solution.py:34
  122.9 14.0 %collective-permute-done.19 = f32[6,2,128,128]{3,2,1,0:T(8,128)S(1)} collective-permute-done((f32[6,2,128,128]{3,2,1,0:T(8,128)S(1)}, f32[6,2,128,128]{3,2,1,0:T(8,128)S(1)}, u32[]{:S(2)}, u32[]{:S(2)}) %collective-permute-start.19) | collective-permute-done | bytes 786464 | tf_op jit(solution)/shard_map/ppermute | solution.py:34
  137.0 1.8 %collective-permute-start.20 = (f32[3,2,128,128]{3,2,1,0:T(8,128)S(1)}, f32[3,2,128,128]{3,2,1,0:T(8,128)S(1)}, u32[]{:S(2)}, u32[]{:S(2)}) collective-permute-start(f32[3,2,128,128]{3,2,1,0:T(8,128)S(1)} %slice.150), channel_id=1, source_target_pairs={{0,64},{64,0},{1,65},{65,1},{2,66},{66,2},{3,67},{67,3},{4,68},{68... | collective-permute-start | bytes 1179656 | tf_op jit(solution)/shard_map/ppermute | solution.py:34
  140.4 1.8 %collective-permute-start.23 = (f32[2,2,128,128]{3,2,1,0:T(8,128)S(1)}, f32[2,2,128,128]{3,2,1,0:T(8,128)S(1)}, u32[]{:S(2)}, u32[]{:S(2)}) collective-permute-start(f32[2,2,128,128]{3,2,1,0:T(8,128)S(1)} %slice.153), channel_id=1, source_target_pairs={{0,8},{8,0},{1,9},{9,1},{2,10},{10,2},{3,11},{11,3},{4,12},{12,4},... | collective-permute-start | bytes 786440 | tf_op jit(solution)/shard_map/ppermute | solution.py:34
  142.2 5.3 %collective-permute-done.23.refs_5_ = f32[2,2,128,128]{3,2,1,0:T(8,128)S(1)} collective-permute-done((f32[2,2,128,128]{3,2,1,0:T(8,128)S(1)}, f32[2,2,128,128]{3,2,1,0:T(8,128)S(1)}, u32[]{:S(2)}, u32[]{:S(2)}) %collective-permute-start.23) | collective-permute-done | bytes 262176 | tf_op jit(solution)/shard_map/ppermute | solution.py:34
  149.7 10.4 %all-to-all-start = ((f32[128,1,128]{2,1,0:T(1,128)}), f32[128,1,128]{2,1,0:T(1,128)S(1)}, u32[]{:S(2)}, u32[]{:S(2)}) async-start(f32[128,1,128]{2,1,0:T(1,128)} %get-tuple-element.90), calls=%async_computation | async-start | bytes 131072 | tf_op jit(solution)/shard_map/all_to_all | solution.py:448
  160.8 8.9 %all-to-all-done.totals_ref = f32[128,1,128]{2,1,0:T(1,128)S(1)} async-done(((f32[128,1,128]{2,1,0:T(1,128)}), f32[128,1,128]{2,1,0:T(1,128)S(1)}, u32[]{:S(2)}, u32[]{:S(2)}) %all-to-all-start) | async-done | bytes 65568 | tf_op jit(solution)/shard_map/all_to_all | solution.py:448
  (105 shorter events, 29.7 us)
Async XLA Ops:
  1.5 4.3 %collective-permute-start = (s32[8,128]{1,0:T(8,128)S(1)}, s32[8,128]{1,0:T(8,128)S(1)}, u32[]{:S(2)}, u32[]{:S(2)}) collective-permute-start(s32[8,128]{1,0:T(8,128)S(1)} %pad_add_fusion.3.table_ref), channel_id=1, source_target_pairs={{0,16},{16,0},{1,17},{17,1},{2,18},{18,2},{3,19},{19,3},{4,20},{20... | collective-permute-start | bytes 12296 | tf_op jit(solution)/shard_map/ppermute | solution.py:34
  5.9 13.1 %collective-permute-start.2 = (f32[3,2,128,128]{3,2,1,0:T(8,128)S(1)}, f32[3,2,128,128]{3,2,1,0:T(8,128)S(1)}, u32[]{:S(2)}, u32[]{:S(2)}) collective-permute-start(f32[3,2,128,128]{3,2,1,0:T(8,128)S(1)} %get-tuple-element.54), channel_id=1, source_target_pairs={{0,4},{1,5},{2,6},{3,7},{4,0},{5,1},{6,2},{7,3},{8,12},{9,13},{10,... | collective-permute-start | bytes 1179656 | tf_op jit(solution)/shard_map/ppermute | solution.py:353
  8.8 10.3 %collective-permute-start.1 = (f32[3,2,128,128]{3,2,1,0:T(8,128)S(1)}, f32[3,2,128,128]{3,2,1,0:T(8,128)S(1)}, u32[]{:S(2)}, u32[]{:S(2)}) collective-permute-start(f32[3,2,128,128]{3,2,1,0:T(8,128)S(1)} %get-tuple-element.53), channel_id=1, source_target_pairs={{0,32},{1,33},{2,34},{3,35},{4,36},{5,37},{6,38},{7,39},{8,40},{9,... | collective-permute-start | bytes 1179656 | tf_op jit(solution)/shard_map/ppermute | solution.py:353
  11.2 8.9 %collective-permute-start.3 = (f32[3,2,128,128]{3,2,1,0:T(8,128)S(1)}, f32[3,2,128,128]{3,2,1,0:T(8,128)S(1)}, u32[]{:S(2)}, u32[]{:S(2)}) collective-permute-start(f32[3,2,128,128]{3,2,1,0:T(8,128)S(1)} %get-tuple-element.55), channel_id=1, source_target_pairs={{0,1},{1,0},{2,3},{3,2},{4,5},{5,4},{6,7},{7,6},{8,9},{9,8},{10,11... | collective-permute-start | bytes 1179656 | tf_op jit(solution)/shard_map/ppermute | solution.py:353
  20.2 12.1 %collective-permute-start.7 = (f32[6,2,128,128]{3,2,1,0:T(8,128)S(1)}, f32[6,2,128,128]{3,2,1,0:T(8,128)S(1)}, u32[]{:S(2)}, u32[]{:S(2)}) collective-permute-start(f32[6,2,128,128]{3,2,1,0:T(8,128)S(1)} %pad_maximum_fusion.5), channel_id=1, source_target_pairs={{0,32},{1,33},{2,34},{3,35},{4,36},{5,37},{6,38},{7,39},{8,40},{9,... | collective-permute-start | bytes 2359304 | tf_op jit(solution)/shard_map/ppermute | solution.py:353
  20.5 13.2 %collective-permute-start.6 = (f32[6,2,128,128]{3,2,1,0:T(8,128)S(1)}, f32[6,2,128,128]{3,2,1,0:T(8,128)S(1)}, u32[]{:S(2)}, u32[]{:S(2)}) collective-permute-start(f32[6,2,128,128]{3,2,1,0:T(8,128)S(1)} %pad_maximum_fusion.4), channel_id=1, source_target_pairs={{0,1},{1,0},{2,3},{3,2},{4,5},{5,4},{6,7},{7,6},{8,9},{9,8},{10,11... | collective-permute-start | bytes 2359304 | tf_op jit(solution)/shard_map/ppermute | solution.py:353
  23.2 12.4 %collective-permute-start.5 = (f32[6,2,128,128]{3,2,1,0:T(8,128)S(1)}, f32[6,2,128,128]{3,2,1,0:T(8,128)S(1)}, u32[]{:S(2)}, u32[]{:S(2)}) collective-permute-start(f32[6,2,128,128]{3,2,1,0:T(8,128)S(1)} %pad_maximum_fusion.3), channel_id=1, source_target_pairs={{0,4},{1,5},{2,6},{3,7},{4,0},{5,1},{6,2},{7,3},{8,12},{9,13},{10,... | collective-permute-start | bytes 2359304 | tf_op jit(solution)/shard_map/ppermute | solution.py:353
  23.5 4.3 %collective-permute-start.8 = (s32[32,128]{1,0:T(8,128)S(1)}, s32[32,128]{1,0:T(8,128)S(1)}, u32[]{:S(2)}, u32[]{:S(2)}) collective-permute-start(s32[32,128]{1,0:T(8,128)S(1)} %pad_add_fusion.1), channel_id=1, source_target_pairs={{0,8},{8,0},{1,9},{9,1},{2,10},{10,2},{3,11},{11,3},{4,12},{12,4},... | collective-permute-start | bytes 49160 | tf_op jit(solution)/shard_map/ppermute | solution.py:34
  37.1 20.8 %collective-permute-start.10 = (f32[12,2,128,128]{3,2,1,0:T(8,128)}, f32[12,2,128,128]{3,2,1,0:T(8,128)}, u32[]{:S(2)}, u32[]{:S(2)}) collective-permute-start(f32[12,2,128,128]{3,2,1,0:T(8,128)} %pad_maximum_fusion.2), channel_id=1, source_target_pairs={{0,4},{1,5},{2,6},{3,7},{4,0},{5,1},{6,2},{7,3},{8,12},{9,13},{10,... | collective-permute-start | bytes 4718600 | tf_op jit(solution)/shard_map/ppermute | solution.py:353
  37.3 22.4 %collective-permute-start.11 = (f32[12,2,128,128]{3,2,1,0:T(8,128)}, f32[12,2,128,128]{3,2,1,0:T(8,128)}, u32[]{:S(2)}, u32[]{:S(2)}) collective-permute-start(f32[12,2,128,128]{3,2,1,0:T(8,128)} %pad_maximum_fusion), channel_id=1, source_target_pairs={{0,1},{1,0},{2,3},{3,2},{4,5},{5,4},{6,7},{7,6},{8,9},{9,8},{10,11... | collective-permute-start | bytes 4718600 | tf_op jit(solution)/shard_map/ppermute | solution.py:353
  39.4 20.8 %collective-permute-start.12 = (f32[12,2,128,128]{3,2,1,0:T(8,128)}, f32[12,2,128,128]{3,2,1,0:T(8,128)}, u32[]{:S(2)}, u32[]{:S(2)}) collective-permute-start(f32[12,2,128,128]{3,2,1,0:T(8,128)} %pad_maximum_fusion.1), channel_id=1, source_target_pairs={{0,32},{1,33},{2,34},{3,35},{4,36},{5,37},{6,38},{7,39},{8,40},{9,... | collective-permute-start | bytes 4718600 | tf_op jit(solution)/shard_map/ppermute | solution.py:353
  41.2 17.4 %collective-permute-start.9 = (s32[64,128]{1,0:T(8,128)S(1)}, s32[64,128]{1,0:T(8,128)S(1)}, u32[]{:S(2)}, u32[]{:S(2)}) collective-permute-start(s32[64,128]{1,0:T(8,128)S(1)} %pad_add_fusion.low_ref), channel_id=1, source_target_pairs={{0,2},{2,0},{1,3},{3,1},{4,6},{6,4},{5,7},{7,5},{8,10},{10,8},{9,1... | collective-permute-start | bytes 98312 | tf_op jit(solution)/shard_map/ppermute | solution.py:34
  65.4 13.2 %collective-permute-start.13 = (f32[32,2,128,128]{3,2,1,0:T(8,128)S(1)}, f32[32,2,128,128]{3,2,1,0:T(8,128)S(1)}, u32[]{:S(2)}, u32[]{:S(2)}) collective-permute-start(f32[32,2,128,128]{3,2,1,0:T(8,128)S(1)} %get-tuple-element.77), channel_id=1, source_target_pairs={{0,16},{16,0},{1,17},{17,1},{2,18},{18,2},{3,19},{19,3},{4,20},{20... | collective-permute-start | bytes 12582920 | tf_op jit(solution)/shard_map/ppermute | solution.py:34
  79.5 25.4 %collective-permute-start.14 = (f32[32,2,128,128]{3,2,1,0:T(8,128)S(1)}, f32[32,2,128,128]{3,2,1,0:T(8,128)S(1)}, u32[]{:S(2)}, u32[]{:S(2)}) collective-permute-start(f32[32,2,128,128]{3,2,1,0:T(8,128)S(1)} %get-tuple-element.80), channel_id=1, source_target_pairs={{0,16},{16,0},{1,17},{17,1},{2,18},{18,2},{3,19},{19,3},{4,20},{20... | collective-permute-start | bytes 12582920 | tf_op jit(solution)/shard_map/ppermute | solution.py:34
  79.7 42.3 %collective-permute-start.21 = (f32[8,2,128,128]{3,2,1,0:T(8,128)S(1)}, f32[8,2,128,128]{3,2,1,0:T(8,128)S(1)}, u32[]{:S(2)}, u32[]{:S(2)}) collective-permute-start(f32[8,2,128,128]{3,2,1,0:T(8,128)S(1)} %slice_add_fusion.5), channel_id=1, source_target_pairs={{0,2},{2,0},{1,3},{3,1},{4,6},{6,4},{5,7},{7,5},{8,10},{10,8},{9,1... | collective-permute-start | bytes 3145736 | tf_op jit(solution)/shard_map/ppermute | solution.py:34
  79.7 37.2 %collective-permute-start.18 = (f32[12,2,128,128]{3,2,1,0:T(8,128)S(1)}, f32[12,2,128,128]{3,2,1,0:T(8,128)S(1)}, u32[]{:S(2)}, u32[]{:S(2)}) collective-permute-start(f32[12,2,128,128]{3,2,1,0:T(8,128)S(1)} %get-tuple-element.86), channel_id=1, source_target_pairs={{0,8},{8,0},{1,9},{9,1},{2,10},{10,2},{3,11},{11,3},{4,12},{12,4},... | collective-permute-start | bytes 4718600 | tf_op jit(solution)/shard_map/ppermute | solution.py:34
  81.4 38.6 %collective-permute-start.15 = (f32[12,2,128,128]{3,2,1,0:T(8,128)S(1)}, f32[12,2,128,128]{3,2,1,0:T(8,128)S(1)}, u32[]{:S(2)}, u32[]{:S(2)}) collective-permute-start(f32[12,2,128,128]{3,2,1,0:T(8,128)S(1)} %get-tuple-element.84), channel_id=1, source_target_pairs={{0,64},{64,0},{1,65},{65,1},{2,66},{66,2},{3,67},{67,3},{4,68},{68... | collective-permute-start | bytes 4718600 | tf_op jit(solution)/shard_map/ppermute | solution.py:34
  117.3 19.6 %collective-permute-start.19 = (f32[6,2,128,128]{3,2,1,0:T(8,128)S(1)}, f32[6,2,128,128]{3,2,1,0:T(8,128)S(1)}, u32[]{:S(2)}, u32[]{:S(2)}) collective-permute-start(f32[6,2,128,128]{3,2,1,0:T(8,128)S(1)} %slice.149), channel_id=1, source_target_pairs={{0,2},{2,0},{1,3},{3,1},{4,6},{6,4},{5,7},{7,5},{8,10},{10,8},{9,1... | collective-permute-start | bytes 2359304 | tf_op jit(solution)/shard_map/ppermute | solution.py:34
  120.3 18.8 %collective-permute-start.16 = (f32[6,2,128,128]{3,2,1,0:T(8,128)S(1)}, f32[6,2,128,128]{3,2,1,0:T(8,128)S(1)}, u32[]{:S(2)}, u32[]{:S(2)}) collective-permute-start(f32[6,2,128,128]{3,2,1,0:T(8,128)S(1)} %slice.146), channel_id=1, source_target_pairs={{0,8},{8,0},{1,9},{9,1},{2,10},{10,2},{3,11},{11,3},{4,12},{12,4},... | collective-permute-start | bytes 2359304 | tf_op jit(solution)/shard_map/ppermute | solution.py:34
  122.1 18.2 %collective-permute-start.22 = (f32[4,2,128,128]{3,2,1,0:T(8,128)S(1)}, f32[4,2,128,128]{3,2,1,0:T(8,128)S(1)}, u32[]{:S(2)}, u32[]{:S(2)}) collective-permute-start(f32[4,2,128,128]{3,2,1,0:T(8,128)S(1)} %slice.152), channel_id=1, source_target_pairs={{0,64},{64,0},{1,65},{65,1},{2,66},{66,2},{3,67},{67,3},{4,68},{68... | collective-permute-start | bytes 1572872 | tf_op jit(solution)/shard_map/ppermute | solution.py:34
  137.0 10.4 %collective-permute-start.20 = (f32[3,2,128,128]{3,2,1,0:T(8,128)S(1)}, f32[3,2,128,128]{3,2,1,0:T(8,128)S(1)}, u32[]{:S(2)}, u32[]{:S(2)}) collective-permute-start(f32[3,2,128,128]{3,2,1,0:T(8,128)S(1)} %slice.150), channel_id=1, source_target_pairs={{0,64},{64,0},{1,65},{65,1},{2,66},{66,2},{3,67},{67,3},{4,68},{68... | collective-permute-start | bytes 1179656 | tf_op jit(solution)/shard_map/ppermute | solution.py:34
  139.2 9.4 %collective-permute-start.17 = (f32[3,2,128,128]{3,2,1,0:T(8,128)S(1)}, f32[3,2,128,128]{3,2,1,0:T(8,128)S(1)}, u32[]{:S(2)}, u32[]{:S(2)}) collective-permute-start(f32[3,2,128,128]{3,2,1,0:T(8,128)S(1)} %slice.147), channel_id=1, source_target_pairs={{0,2},{2,0},{1,3},{3,1},{4,6},{6,4},{5,7},{7,5},{8,10},{10,8},{9,1... | collective-permute-start | bytes 1179656 | tf_op jit(solution)/shard_map/ppermute | solution.py:34
  140.4 7.1 %collective-permute-start.23 = (f32[2,2,128,128]{3,2,1,0:T(8,128)S(1)}, f32[2,2,128,128]{3,2,1,0:T(8,128)S(1)}, u32[]{:S(2)}, u32[]{:S(2)}) collective-permute-start(f32[2,2,128,128]{3,2,1,0:T(8,128)S(1)} %slice.153), channel_id=1, source_target_pairs={{0,8},{8,0},{1,9},{9,1},{2,10},{10,2},{3,11},{11,3},{4,12},{12,4},... | collective-permute-start | bytes 786440 | tf_op jit(solution)/shard_map/ppermute | solution.py:34
  149.7 19.9 %all-to-all-start = ((f32[128,1,128]{2,1,0:T(1,128)}), f32[128,1,128]{2,1,0:T(1,128)S(1)}, u32[]{:S(2)}, u32[]{:S(2)}) async-start(f32[128,1,128]{2,1,0:T(1,128)} %get-tuple-element.90), calls=%async_computation | async-start | bytes 131072 | tf_op jit(solution)/shard_map/all_to_all | solution.py:448
  (18 other events, 162.2 us)
